TPU v7x, 32 devices: a whole 2x2x4 slice. The times are simulated.
32 devices in a mesh: ctx: 16 (over z, y, x), tp: 2 (over core).
Axes of the slice: x: 2, y: 2, z: 4, core: 2. Of those that a mesh axis runs over, the one named last changes fastest.
Arguments:
- tokens: bfloat16 [4, 2048, 1280], P(None, 'ctx'), may hold values from -6 to 6
- cotangent: bfloat16 [4, 2048, 1280], P(None, 'ctx'), may hold values from -6 to 6
- doc_lengths: int32 [4, 8], replicated, may hold values from 1 to 1536, 2048 in all within a row
- w_query: bfloat16 [1280, 1280], P('ctx', 'tp'), may hold values from -0.15625 to 0.15625
- w_key: bfloat16 [1280, 1280], P('ctx', 'tp'), may hold values from -0.15625 to 0.15625
- w_value: bfloat16 [1280, 1280], P('ctx', 'tp'), may hold values from -0.15625 to 0.15625
- w_out: bfloat16 [1280, 1280], P('tp', 'ctx'), may hold values from -0.625 to 0.625
- w_up: bfloat16 [1280, 1280], P('ctx', 'tp'), may hold values from -0.15625 to 0.15625
- w_down: bfloat16 [1280, 1280], P('tp', 'ctx'), may hold values from -0.25 to 0.25
- gain_attn: bfloat16 [1280], P('ctx'), may hold values from 0.099609375 to 1.8984375
- gain_mlp: bfloat16 [1280], P('ctx'), may hold values from 0.099609375 to 1.8984375
- query_scale: float32 [80], replicated, may hold values from 0.06 to 0.3
Outputs:
- layer_out: bfloat16 [4, 2048, 1280], P(None, 'ctx')
- grad_tokens: float32 [4, 2048, 1280], P(None, 'ctx')
- grad_query: float32 [1280, 1280], P('ctx', 'tp')
- grad_key: float32 [1280, 1280], P('ctx', 'tp')
- grad_value: float32 [1280, 1280], P('ctx', 'tp')
- grad_out: float32 [1280, 1280], P('tp', 'ctx')
- grad_up: float32 [1280, 1280], P('ctx', 'tp')
- grad_down: float32 [1280, 1280], P('tp', 'ctx')
- grad_gain_attn: float32 [1280], P('ctx')
- grad_gain_mlp: float32 [1280], P('ctx')
- grad_scale: float32 [80], replicated
Inputs may be any that keep to these rules, and one draw needn't show every extreme that they name: `doc_lengths`: each row holds the lengths of the 8 documents of one stream in order; they sum to 2048, and the longest is exactly 1536.
All inputs are finite; a program needn't handle non-finite values.
Results may differ from a plain program's by a relative error of at most 0.024.
Values may be sent and summed in bfloat16 or wider, within the bound.
No kernel may reach another device: no remote copies, remote signals or barrier semaphores. Data moves between devices by JAX's collectives and lax.ppermute only.
A program may use at most 192 MiB of HBM per device.

v0:
```python
import functools
import math

import jax
import jax.numpy as jnp
from jax import lax
from jax.experimental import pallas as pl
from jax.experimental.pallas import tpu as pltpu
from jax.sharding import PartitionSpec as P

EPSILON = 1e-06
MASKED = -1e30
LANES = 128
WIDE = 512
BF = jnp.bfloat16
F32 = jnp.float32
SPARE_VMEM = 12 * 1024 * 1024


def call(kernel, out_shape, kinds, scratch=(), flops=0, moved=0, aliases=None):
    vmem = pl.BlockSpec(memory_space=pltpu.VMEM)
    smem = pl.BlockSpec(memory_space=pltpu.SMEM)
    hbm = pl.BlockSpec(memory_space=pl.ANY)
    room = sum(
        math.prod(ref.shape) * jnp.dtype(ref.dtype).itemsize
        for ref in scratch
        if ref.memory_space == pltpu.VMEM
    )
    return pl.pallas_call(
        kernel,
        out_shape=out_shape,
        in_specs=[{"s": smem, "v": vmem, "h": hbm}[kind] for kind in kinds],
        out_specs=jax.tree.map(lambda _: vmem, out_shape),
        scratch_shapes=list(scratch),
        input_output_aliases=aliases or {},
        compiler_params=pltpu.CompilerParams(vmem_limit_bytes=room + SPARE_VMEM),
        cost_estimate=pl.CostEstimate(
            flops=int(flops), transcendentals=0, bytes_accessed=int(moved)
        ),
    )


def struct(shape, dtype):
    return jax.ShapeDtypeStruct(tuple(shape), dtype)


def nn(a, b):
    return jnp.dot(a, b, preferred_element_type=F32)


def nt(a, b):
    return lax.dot_general(a, b, (((1,), (1,)), ((), ())), preferred_element_type=F32)


def tn(a, b):
    return lax.dot_general(a, b, (((0,), (0,)), ((), ())), preferred_element_type=F32)


def at(start, size, step=None):
    return pl.ds(pl.multiple_of(start, step or size), size)


def inverse_rms(values):
    return lax.rsqrt(jnp.mean(values * values, axis=-1, keepdims=True) + EPSILON)


def split_kernel(ids, whole, *out):
    z, c = ids[0], ids[2]
    half = out[0].shape[0]
    for kz in range(len(out)):
        out[kz][...] = whole[z ^ kz, at(c * half, half), :]


def split(ids, whole):
    groups, rows, width = whole.shape
    return call(
        split_kernel,
        (struct((rows // 2, width), whole.dtype),) * groups,
        "sv",
        moved=whole.size * 4,
    )(ids, whole)


def assemble_kernel(ids, own, other, out):
    groups, half, _ = own.shape
    c = ids[2]
    for kz in range(groups):
        out[ids[0] ^ kz, at(c * half, half), :] = own[kz].astype(out.dtype)
        out[ids[0] ^ kz, at((1 - c) * half, half), :] = other[kz].astype(out.dtype)


def assemble(ids, own, other, dtype):
    groups, half, width = own.shape
    return call(
        assemble_kernel, struct((groups, 2 * half, width), dtype), "svv", moved=own.size * 12
    )(ids, own, other)


def place_kernel(groups, ids, *refs):
    own, other, out = refs[:groups], refs[groups : 2 * groups], refs[2 * groups]
    half = own[0].shape[0]
    z, c = ids[0], ids[2]
    for kz in range(groups):
        out[z ^ kz, at(c * half, half), :] = own[kz][...].astype(out.dtype)
        out[z ^ kz, at((1 - c) * half, half), :] = other[kz][...].astype(out.dtype)


def pack_kernel(mine, ids, query, key, value, gains, *refs):
    out, tmp = refs[:-1], refs[-1]
    rows = query.shape[0]
    rest = jnp.concatenate([gains[...], jnp.zeros((rows, WIDE - 3 * mine - 2), BF)], axis=1)
    for k in range(len(out)):
        cols = slice(k * mine, (k + 1) * mine)
        tmp[k] = jnp.concatenate([query[:, cols], key[:, cols], value[:, cols], rest], axis=1)
    for kj in range(len(out)):
        out[kj][...] = tmp[ids[1] ^ kj]


def stack_kernel(up, out_t, down_t, out):
    cols = up.shape[1]
    for g in range(out.shape[0]):
        for n, part in enumerate((up, out_t, down_t)):
            out[g, :, n * cols : (n + 1) * cols] = part[...]


def spread_kernel(heads, size, ids, pieces, w, w_t, gains, rows_ref):
    groups, members, rows, _ = pieces.shape
    for kz in range(groups):
        for kj in range(members):
            where = at((kz * members + (ids[1] ^ kj)) * rows, rows, 16)
            rows_ref[where, :] = pieces[kz, kj]
    block = rows_ref[...]
    zeros = jnp.zeros((block.shape[0], LANES - size), BF)
    for h in range(3 * heads):
        w[:, h * LANES : (h + 1) * LANES] = jnp.concatenate(
            [block[:, h * size : (h + 1) * size], zeros], axis=1
        )
    w_t[...] = w[...].T
    first = 3 * heads * size - (WIDE - LANES)
    gains[...] = block[:, WIDE - LANES :].astype(F32).T[first : first + 8, :]


def order_kernel(ids, *refs):
    pieces, out = refs[:-3], refs[-3:]
    groups, rows, _ = pieces[0].shape
    members, cols = len(pieces), out[0].shape[1]
    for kj in range(members):
        for kz in range(groups):
            where = at((kz * members + (ids[1] ^ kj)) * rows, rows, 16)
            for n in range(3):
                out[n][where, :] = pieces[kj][kz, :, n * cols : (n + 1) * cols]


def project_kernel(members, step, ids, *refs):
    pieces = refs[: 2 * members]
    w, gain, scale, proj, normed = refs[2 * members :]
    groups, half, _ = pieces[0].shape
    z, j, c = ids[0], ids[1], ids[2]
    for kj in range(members):
        for kc in range(2):
            for kz in range(groups):
                base = (z ^ kz) * (members * 2) + (j ^ kj) * 2 + (c ^ kc)
                normed[at(base * half, half), :] = pieces[kc * members + kj][kz]

    def block(n, _):
        rows = at(n * step, step)
        x = normed[rows, :].astype(F32)
        xn = (x * inverse_rms(x) * gain[0:1, :]).astype(BF)
        normed[rows, :] = xn
        proj[rows, :] = (nn(xn, w[...]) * scale[...]).astype(BF)
        return 0

    lax.fori_loop(0, normed.shape[0] // step, block, 0)


def doc_bounds(lengths, z, place):
    start, begin, end = jnp.int32(0), jnp.int32(0), jnp.int32(0)
    for d in range(lengths.shape[1]):
        stop = start + lengths[z, d]
        inside = start <= place
        begin = jnp.where(inside, start, begin)
        end = jnp.where(inside, stop, end)
        start = stop
    return begin, end


def doc_starts(lengths, z, stream):
    place = lax.broadcasted_iota(jnp.int32, (8, stream), 1)
    start, row = jnp.int32(0), jnp.zeros((8, stream), jnp.int32)
    for d in range(lengths.shape[1]):
        row = jnp.where(place >= start, start, row)
        start = start + lengths[z, d]
    return row


def attend_kernel(heads, size, members, bq, bk, ids, lengths, proj, *refs):
    outs, (kept, sent, vt, doc) = refs[:members], refs[members:]
    stream = proj.shape[0]
    z, j = ids[0], ids[1]
    doc[...] = doc_starts(lengths, z, stream)
    for h in range(heads):
        vt[h] = proj[:, (2 * heads + h) * LANES : (2 * heads + h + 1) * LANES].T

    def one_query_block(qb, _):
        rows = at(qb * bq, bq)
        qpos = qb * bq + lax.broadcasted_iota(jnp.int32, (1, bq), 1)
        queries = [proj[rows, h * LANES : (h + 1) * LANES] for h in range(heads)]

        def one_key_block(kb, carry):
            keys = at(kb * bk, bk)
            kpos = kb * bk + lax.broadcasted_iota(jnp.int32, (bk, bq), 0)
            allowed = (kpos <= qpos) & (kpos >= doc[0:1, rows])
            new = []
            for h in range(heads):
                top, total, acc = carry[h]
                k = proj[keys, (heads + h) * LANES : (heads + h + 1) * LANES]
                s = jnp.where(allowed, nt(k, queries[h]), MASKED)
                top2 = jnp.maximum(top, jnp.max(s, axis=0, keepdims=True))
                p = jnp.exp(s - top2)
                alpha = jnp.exp(top - top2)
                total = total * alpha + jnp.sum(p, axis=0, keepdims=True)
                acc = acc * alpha + nn(vt[h, :, keys], p.astype(BF))
                new.append((top2, total, acc))
            return tuple(new)

        zero = (
            jnp.full((1, bq), MASKED, F32),
            jnp.zeros((1, bq), F32),
            jnp.zeros((LANES, bq), F32),
        )
        begin, _ = doc_bounds(lengths, z, qb * bq)
        end = (qb * bq + bq + bk - 1) // bk
        carry = lax.fori_loop(begin // bk, end, one_key_block, (zero,) * heads)
        for h in range(heads):
            top, total, acc = carry[h]
            o = acc / total
            kept[h, :LANES, rows] = o
            kept[h, LANES:, rows] = jnp.broadcast_to(top + jnp.log(total), (8, bq))
            low = o[:size].astype(BF)
            for part in range(bq // LANES):
                block = qb * (bq // LANES) + part
                lanes = at(block // members * LANES, LANES)
                sent[(block % members) ^ j, h * size : (h + 1) * size, lanes] = low[
                    :, part * LANES : (part + 1) * LANES
                ]
        return 0

    lax.fori_loop(0, stream // bq, one_query_block, 0)
    for kj in range(members):
        outs[kj][...] = sent[kj]


def store_weights(heads, size, count, scale_sum, full, out):
    rows = out.shape[0] // count
    pad = WIDE - 3 * heads * size
    s = scale_sum[:size, :pad]
    high = s.astype(BF)
    rest = (s - high.astype(F32)).astype(BF)
    lane = lax.broadcasted_iota(jnp.int32, (size, pad), 1)
    tail = jnp.where(lane == 0, high, jnp.where(lane == 1, rest, jnp.zeros_like(rest)))
    tail = [tail, jnp.zeros((rows - size, pad), BF)] if rows > size else [tail]
    tail = jnp.concatenate(tail, axis=0)
    for n in range(count):
        block = full[n * rows : (n + 1) * rows, :].astype(BF)
        out[n * rows : (n + 1) * rows, :] = jnp.concatenate(
            [block[:, h * LANES : h * LANES + size] for h in range(3 * heads)] + [tail], axis=1
        )


def attend_back_kernel(heads, size, members, bq, bk, ids, lengths, proj, kept, scale, w, normed, *refs):
    pieces = refs[:members]
    grads, there, weights, dot_, do_, kt, dqt, delta, doc, rows_ref, full = refs[members:]
    stream = proj.shape[0]
    groups = pieces[0].shape[1] // LANES
    z, j = ids[0], ids[1]
    doc[...] = doc_starts(lengths, z, stream)
    for h in range(heads):
        kt[h] = proj[:, (heads + h) * LANES : (heads + h + 1) * LANES].T
        dot_[h, size:, :] = jnp.zeros((LANES - size, stream), BF)
        for kj in range(members):
            for g in range(groups):
                lanes = at((g * members + (j ^ kj)) * LANES, LANES)
                dot_[h, :size, lanes] = pieces[kj][
                    h * size : (h + 1) * size, g * LANES : (g + 1) * LANES
                ]
        do_[h] = dot_[h].T
        delta[h] = jnp.broadcast_to(
            jnp.sum(dot_[h].astype(F32) * kept[h, :LANES, :], axis=0, keepdims=True), (8, stream)
        )
        dqt[h] = jnp.zeros((LANES, stream), F32)

    def one_key_block(kb, _):
        keys = at(kb * bk, bk)
        kpos = kb * bk + lax.broadcasted_iota(jnp.int32, (bk, bq), 0)
        ks = [proj[keys, (heads + h) * LANES : (heads + h + 1) * LANES] for h in range(heads)]
        vs = [
            proj[keys, (2 * heads + h) * LANES : (2 * heads + h + 1) * LANES] for h in range(heads)
        ]

        def one_query_block(qb, carry):
            rows = at(qb * bq, bq)
            qpos = qb * bq + lax.broadcasted_iota(jnp.int32, (1, bq), 1)
            allowed = (kpos <= qpos) & (kpos >= doc[0:1, rows])
            new = []
            for h in range(heads):
                dk, dv = carry[h]
                q = proj[rows, h * LANES : (h + 1) * LANES]
                p = jnp.exp(nt(ks[h], q) - kept[h, LANES : LANES + 1, rows])
                p = jnp.where(allowed, p, 0.0)
                dp = nn(vs[h], dot_[h, :, rows])
                ds = (p * (dp - delta[h, 0:1, rows])).astype(BF)
                dv = dv + nn(p.astype(BF), do_[h, rows, :])
                dk = dk + nn(ds, q)
                dqt[h, :, rows] += nn(kt[h, :, keys], ds)
                new.append((dk, dv))
            return tuple(new)

        _, final = doc_bounds(lengths, z, kb * bk + bk - 1)
        zero = jnp.zeros((bk, LANES), F32)
        carry = lax.fori_loop(
            kb * bk // bq, (final + bq - 1) // bq, one_query_block, ((zero, zero),) * heads
        )
        for h in range(heads):
            for n in range(2):
                cols = ((n + 1) * heads + h) * LANES
                grads[keys, cols : cols + LANES] = carry[h][n].astype(BF)
        return 0

    lax.fori_loop(0, stream // bk, one_key_block, 0)
    total = jnp.zeros((1, LANES), F32)
    for h in range(heads):
        dq = dqt[h].T
        q = proj[:, h * LANES : (h + 1) * LANES].astype(F32)
        total = total + jnp.sum(dq * q, axis=0, keepdims=True)
        grads[:, h * LANES : (h + 1) * LANES] = (dq * scale[...]).astype(BF)
    _, _, half, width = there.shape

    def one_member(kj, _):
        y = nn(input_rows(ids, grads, rows_ref, kj, 1, members, half), w[...])
        there[kj] = y.reshape(groups, half, width).astype(BF)
        return 0

    lax.fori_loop(0, members, one_member, 0)
    total = jnp.broadcast_to(total / scale[...], (LANES, LANES)).T
    full[...] = tn(normed[...], grads[...])
    store_weights(heads, size, groups * members, total, full, weights)


def out_kernel(ids, *refs):
    pieces, (w, ob_t, part) = refs[:-3], refs[-3:]
    mine = pieces[0].shape[0]
    for kj in range(len(pieces)):
        ob_t[at((ids[1] ^ kj) * mine, mine, 16), :] = pieces[kj][...]
    part[...] = nt(ob_t[...].T, w[...]).astype(BF)


def mlp_kernel(groups, ids, *refs):
    x_own, x_other = refs[0], refs[1]
    g_own, g_other, attn, attn_other, up, down, gains = refs[2:9]
    hidden, normed, act, grad_up, cot, part, back = refs[9:]
    half = x_own.shape[1]
    z, c = ids[0], ids[2]
    for kz in range(groups):
        for kc in range(2):
            rows = at((z ^ kz) * (2 * half) + (c ^ kc) * half, half)
            hidden[rows, :] = (x_other if kc else x_own)[kz].astype(F32) + (
                attn[rows, :].astype(F32) + attn_other[rows, :].astype(F32)
            )
            cot[rows, :] = (g_other if kc else g_own)[kz]
    step = hidden.shape[0] // 2

    def block(n, _):
        rows = at(n * step, step)
        h = hidden[rows, :]
        xn = (h * inverse_rms(h) * gains[1:2, :]).astype(BF)
        u = nn(xn, up[...])
        sigma = jax.nn.sigmoid(u)
        a = (u * sigma).astype(BF)
        da = nn(cot[rows, :], down[...])
        du = (da * sigma * (1.0 + u * (1.0 - sigma))).astype(BF)
        part[rows, :] = nt(a, down[...]).astype(BF)
        back[rows, :] = nt(du, up[...]).astype(BF)
        normed[rows, :] = xn
        act[rows, :] = a
        grad_up[rows, :] = du
        return 0

    lax.fori_loop(0, 2, block, 0)


def hidden_kernel(groups, members, ids, *refs):
    hidden, cot, part, part_other, back, back_other, w, gains = refs[:8]
    low, dh_half = refs[8:10]
    pieces, out = refs[10 : 10 + members], refs[10 + members : 10 + members + groups]
    dh, lay, do_t = refs[10 + members + groups :]
    rows_all = hidden.shape[0]
    half = rows_all // groups // 2
    mine = pieces[0].shape[0]
    z, j, c = ids[0], ids[1], ids[2]
    step = rows_all // groups

    def block(n, _):
        rows = at(n * step, step)
        h = hidden[rows, :]
        scale = inverse_rms(h)
        grad = back[rows, :].astype(F32) + back_other[rows, :].astype(F32)
        weighted = grad * gains[1:2, :]
        d = (
            cot[rows, :].astype(F32)
            + scale * weighted
            - h * scale**3 * jnp.mean(weighted * h, axis=-1, keepdims=True)
        )
        dh[rows, :] = d
        low[rows, :] = d.astype(BF)
        lay[rows, :] = (
            h + (part[rows, :].astype(F32) + part_other[rows, :].astype(F32))
        ).astype(BF)
        return 0

    lax.fori_loop(0, groups, block, 0)
    do_t[...] = nn(low[...], w[...]).T.astype(BF)
    for kj in range(members):
        pieces[kj][...] = do_t[at((j ^ kj) * mine, mine, 16), :]
    for g in range(groups):
        out[g][...] = lay[at((z ^ g) * 2 * half + c * half, half), :]
        dh_half[g] = dh[at(g * 2 * half + c * half, half), :]


def by_member(ids, full, out, first=0):
    groups, rows, _ = out[0].shape
    for kj in range(len(out)):
        for g in range(groups):
            where = at((g * len(out) + (ids[1] ^ kj)) * rows, rows, 16)
            out[kj][g, :, first : first + full.shape[1]] = full[where, :]


def feed_weights_kernel(ids, normed, grad_up, cot, act, *refs):
    out, full = refs[:-1], refs[-1]
    full[...] = tn(normed[...], grad_up[...]).astype(BF)
    by_member(ids, full, out)
    full[...] = tn(cot[...], act[...]).astype(BF)
    by_member(ids, full, out, full.shape[1])


def out_weights_kernel(ids, low, ob_t, *refs):
    out, full = refs[:-1], refs[-1]
    full[...] = tn(low[...], ob_t[...].T).astype(BF)
    by_member(ids, full, out)


def sum_members_kernel(*refs):
    total = refs[0][...].astype(F32)
    for part in refs[1:-1]:
        total = total + part[...].astype(F32)
    refs[-1][...] = total.astype(BF)


def sum_split_kernel(members, ids, *refs):
    parts, out, tmp = refs[:members], refs[members:-1], refs[-1]
    total = parts[0][...].astype(F32)
    for part in parts[1:]:
        total = total + part[...].astype(F32)
    tmp[...] = total.astype(BF)
    for kz in range(len(out)):
        out[kz][...] = tmp[ids[0] ^ kz]


def rows_kernel(groups, parts, up, *refs):
    outs, (grad_up, grad_down, grad_out, gain) = refs[:groups], refs[groups:]
    cols = up.shape[1]
    total = parts[0].astype(F32)
    for g in range(1, parts.shape[0]):
        total = total + parts[g].astype(F32)
    grad_up[...] = total[:, :cols]
    grad_down[...] = total[:, cols:].T
    term = jnp.sum(total[:, :cols] * up[...].astype(F32), axis=1, keepdims=True)
    gain[...] = jnp.broadcast_to(term, gain.shape)
    total = outs[0][...].astype(F32)
    for part in outs[1:]:
        total = total + part[...].astype(F32)
    grad_out[...] = total.T


def input_rows(ids, grads, rows_ref, kj, which, members, half):
    for g in range(rows_ref.shape[0] // half):
        base = (g * members + (ids[1] ^ kj)) * 2 + (ids[2] ^ which)
        rows_ref[g * half : (g + 1) * half, :] = grads[at(base * half, half), :]
    return rows_ref[...]


def input_here_kernel(ids, grads, w, other, *refs):
    out, rows_ref = refs[:-1], refs[-1]
    members, (groups, half, width) = len(out), out[0].shape
    for kj in reversed(range(members)):
        y = nn(input_rows(ids, grads, rows_ref, kj, 0, members, half), w[...])
        y = y + other[kj].reshape(groups * half, width).astype(F32)
        out[kj][...] = y.reshape(groups, half, width).astype(BF)


def qkv_sum_kernel(ids, parts, *refs):
    out, tmp = refs[:-1], refs[-1]
    total = parts[0].astype(F32)
    for g in range(1, parts.shape[0]):
        total = total + parts[g].astype(F32)
    tmp[...] = total
    rows = out[0].shape[0]
    for kj in range(len(out)):
        out[kj][...] = tmp[at((ids[1] ^ kj) * rows, rows, 16), :].astype(BF)


def qkv_rows_kernel(mine, ids, *refs):
    members = len(refs) - 8
    pieces, (query, key, value, dq, dk, dv, small, tmp) = refs[:members], refs[members:]
    for kj in range(members):
        tmp[ids[1] ^ kj] = pieces[kj][...].astype(F32)
    gain = None
    for n, (w, dw) in enumerate(((query, dq), (key, dk), (value, dv))):
        dw[...] = jnp.concatenate(
            [tmp[k][:, n * mine : (n + 1) * mine] for k in range(members)], axis=1
        )
        term = jnp.sum(dw[...] * w[...].astype(F32), axis=1, keepdims=True)
        gain = term if gain is None else gain + term
    scale = tmp[0][:, 3 * mine : 3 * mine + 2]
    for k in range(1, members):
        scale = scale + tmp[k][:, 3 * mine : 3 * mine + 2]
    scale = jnp.sum(scale, axis=1, keepdims=True)
    lane = lax.broadcasted_iota(jnp.int32, small.shape, 1)
    small[...] = jnp.where(lane == 0, gain, jnp.where(lane == 1, scale, 0.0))


def tokens_kernel(groups, ids, *refs):
    x, dh, gains = refs[:3]
    parts, out = refs[3:-groups], refs[-groups:]
    z = ids[0]
    for kz in range(groups):
        grad = parts[0][z ^ kz].astype(F32)
        for part in parts[1:]:
            grad = grad + part[z ^ kz].astype(F32)
        xx = x[kz].astype(F32)
        scale = inverse_rms(xx)
        weighted = grad * gains[0:1, :]
        out[kz][...] = (
            dh[z ^ kz]
            + scale * weighted
            - xx * scale**3 * jnp.mean(weighted * xx, axis=-1, keepdims=True)
        ).astype(BF)


def stream_per_group(
    tokens,
    cotangent,
    doc_lengths,
    w_query,
    w_key,
    w_value,
    w_out,
    w_up,
    w_down,
    gain_attn,
    gain_mlp,
    query_scale,
):
    groups, tok_rows, width = tokens.shape
    count = lax.axis_size("ctx")
    members = count // groups
    size = query_scale.shape[0]
    local = w_query.shape[1]
    shard = width // count
    heads = local // size // members
    half = tok_rows // 2
    stream = tok_rows * count
    mine = heads * size
    rows = groups * tok_rows
    padded = 3 * heads * LANES
    me = lax.axis_index("ctx")
    ids = jnp.stack([me // members, me % members, lax.axis_index("tp")]).astype(jnp.int32)

    planes = [[g * members + k for k in range(members)] for g in range(groups)]
    lines = [[g * members + k for g in range(groups)] for k in range(members)]

    def across(a, mask):
        return lax.ppermute(a, "ctx", [(i, i ^ mask) for i in range(count)])

    def shift(a, by):
        pairs = [(i, i + by * members) for i in range(count)]
        return lax.ppermute(a, "ctx", [(i, k) for i, k in pairs if 0 <= k < count])

    def swap(a):
        return lax.ppermute(a, "tp", [(0, 1), (1, 0)])

    def to_groups(parts):
        return [parts[0]] + [across(parts[k], k * members) for k in range(1, groups)]

    def to_members(parts):
        return [parts[0]] + [across(parts[k], k) for k in range(1, members)]

    def exchange(a, teams):
        return lax.all_to_all(a, "ctx", 0, 0, axis_index_groups=teams, tiled=True)

    def tie(*values):
        return lax.optimization_barrier(values)

    def quarter(own, beside, above):
        cut = groups // 2
        return jnp.concatenate([across(above[:cut], 1), across(beside[cut:], 2)])

    packed = call(
        functools.partial(pack_kernel, mine),
        (struct((shard, WIDE), BF),) * members,
        "svvvv",
        scratch=[pltpu.VMEM((members, shard, WIDE), BF)],
        moved=shard * WIDE * members * 4,
    )(ids, w_query, w_key, w_value, jnp.stack([gain_attn, gain_mlp], axis=1))
    own = jnp.stack(to_groups(split(ids, tokens)))

    shards = call(
        stack_kernel,
        struct((groups, shard, 3 * local), BF),
        "vvv",
        moved=groups * shard * local * 8,
    )(w_up, w_out.T, w_down.T)
    own, packed, shards = tie(own, packed, shards)
    shards = exchange(shards, lines)
    cols = to_members(packed)
    late, cols = tie(own, cols)
    pieces = to_members([own] * (members - 1) + [late])
    pieces, cols, shards = tie(pieces, jnp.stack(cols), shards)
    cols = jnp.concatenate([cols] * groups)

    cols = exchange(cols, lines).reshape(groups, members, shard, WIDE)
    others = [swap(piece) for piece in pieces]
    if members == 4:
        beside, above = across(shards, 1), across(shards, 2)
        cols, others, beside, above = tie(cols, others, beside, above)
        shards = [shards, beside, above, quarter(shards, beside, above)]
    else:
        cols, others, shards = tie(cols, others, to_members([shards] * members))
    pieces = pieces + others
    g_parts, cols = tie(split(ids, cotangent), cols)
    g_own = to_groups(g_parts)
    w_qkv, w_qkv_t, gains = call(
        functools.partial(spread_kernel, heads, size),
        (struct((width, padded), BF), struct((padded, width), BF), struct((8, width), F32)),
        "sv",
        scratch=[pltpu.VMEM((width, WIDE), BF)],
        moved=width * padded * 6,
    )(ids, cols)
    scale_row = jnp.pad(query_scale, (0, LANES - size), constant_values=1.0)[None, :]
    scale_all = jnp.concatenate(
        [scale_row] * heads + [jnp.ones((1, 2 * heads * LANES), F32)], axis=1
    )

    proj, normed = call(
        functools.partial(project_kernel, members, 512),
        (struct((stream, padded), BF), struct((stream, width), BF)),
        "s" + "v" * (2 * members + 3),
        flops=2 * stream * width * padded,
        moved=stream * width * 4,
    )(ids, *pieces, w_qkv, gains, scale_all)

    bq, bk = 512, 512
    *sent, kept = call(
        functools.partial(attend_kernel, heads, size, members, bq, bk),
        (struct((mine, rows), BF),) * members + (struct((heads, LANES + 8, stream), F32),),
        "ssv",
        scratch=[
            pltpu.VMEM((members, mine, rows), BF),
            pltpu.VMEM((heads, LANES, stream), BF),
            pltpu.VMEM((8, stream), jnp.int32),
        ],
        flops=2 * stream * stream * LANES * heads,
        moved=stream * LANES * heads * 10,
    )(ids, doc_lengths, proj)
    sent, shards, g_own = tie(sent, shards, g_own)
    arrived = to_members(sent)
    g_own = jnp.stack(g_own)
    g_other = swap(g_own)
    up_full, out_t, down_t = call(
        order_kernel,
        (struct((width, local), BF),) * 3,
        "s" + "v" * members,
        moved=width * local * 12,
    )(ids, *shards)

    ob_t, attn = call(
        out_kernel,
        (struct((local, rows), BF), struct((rows, width), BF)),
        "s" + "v" * (members + 1),
        flops=2 * rows * local * width,
        moved=local * width * 4,
    )(ids, *arrived, out_t)
    hidden, normed_two, activated, grad_up_raw, cot, part, back = call(
        functools.partial(mlp_kernel, groups),
        (
            struct((rows, width), F32),
            struct((rows, width), BF),
            struct((rows, local), BF),
            struct((rows, local), BF),
            struct((rows, width), BF),
            struct((rows, width), BF),
            struct((rows, width), BF),
        ),
        "s" + "v" * 9,
        flops=8 * rows * local * width,
        moved=local * width * 12,
    )(ids, pieces[0], pieces[members], g_own, g_other, attn, swap(attn), up_full, down_t, gains)
    back_other, part_other = swap(back), swap(part)
    feed_grads = call(
        feed_weights_kernel,
        (struct((groups, shard, 2 * local), BF),) * members,
        "svvvv",
        scratch=[pltpu.VMEM((width, local), BF)],
        flops=4 * rows * local * width,
        moved=local * width * 8,
    )(ids, normed_two, grad_up_raw, cot, activated)
    back_other, part_other, feed_grads = tie(back_other, part_other, feed_grads)
    hidden_low, dh_half, *results = call(
        functools.partial(hidden_kernel, groups, members),
        (struct((rows, width), BF), struct((groups, half, width), F32))
        + (struct((mine, rows), BF),) * members
        + (struct((half, width), BF),) * groups,
        "s" + "v" * 8,
        scratch=[
            pltpu.VMEM((rows, width), F32),
            pltpu.VMEM((rows, width), BF),
            pltpu.VMEM((local, rows), BF),
        ],
        flops=2 * rows * local * width,
        moved=local * width * 12,
    )(ids, hidden, cot, part, part_other, back, back_other, out_t, gains)
    do_pieces, out_parts = to_members(results[:members]), results[members:]
    out_grads = call(
        out_weights_kernel,
        (struct((groups, shard, local), BF),) * members,
        "svv",
        scratch=[pltpu.VMEM((width, local), BF)],
        flops=2 * rows * local * width,
        moved=local * width * 4,
    )(ids, hidden_low, ob_t)
    do_pieces, out_grads, out_parts, feed_grads = tie(do_pieces, out_grads, out_parts, feed_grads)

    feed_grads = to_members(feed_grads)
    out_own = to_groups(out_parts)

    grads, there, qkv_parts = call(
        functools.partial(attend_back_kernel, heads, size, members, bq, bk),
        (
            struct((stream, padded), BF),
            struct((members, groups, half, width), BF),
            struct((width, WIDE), BF),
        ),
        "ssvvvvv" + "v" * members,
        scratch=[
            pltpu.VMEM((heads, LANES, stream), BF),
            pltpu.VMEM((heads, stream, LANES), BF),
            pltpu.VMEM((heads, LANES, stream), BF),
            pltpu.VMEM((heads, LANES, stream), F32),
            pltpu.VMEM((heads, 8, stream), F32),
            pltpu.VMEM((8, stream), jnp.int32),
            pltpu.VMEM((groups * half, padded), BF),
            pltpu.VMEM((width, padded), F32),
        ],
        flops=5 * stream * stream * LANES * heads,
        moved=stream * LANES * heads * 20,
    )(ids, doc_lengths, proj, kept, scale_row, w_qkv_t, normed, *do_pieces)
    there, grads, qkv_parts, feed_grads, out_own[1], out_own[2], out_grads = tie(
        there, grads, qkv_parts, feed_grads, out_own[1], out_own[2], out_grads
    )

    there = swap(there)
    here = call(
        input_here_kernel,
        (struct((groups, half, width), BF),) * members,
        "svvv",
        scratch=[pltpu.VMEM((groups * half, padded), BF)],
        flops=stream * width * padded,
        moved=stream * width * 2,
    )(ids, grads, w_qkv_t, there)
    here, feed_grads, qkv_parts = tie(here, feed_grads, qkv_parts)
    sums = to_members(here)
    qkv_parts = exchange(qkv_parts, lines).reshape(groups, width // groups, WIDE)
    feed_grads = call(
        sum_members_kernel,
        struct((groups, shard, 2 * local), BF),
        "v" * members,
        moved=groups * shard * local * 24,
    )(*feed_grads)
    sums, feed_grads = tie(sums, feed_grads)
    grad_x = call(
        functools.partial(tokens_kernel, groups),
        (struct((half, width), BF),) * groups,
        "svvv" + "v" * len(sums),
        moved=groups * half * width * 12,
    )(ids, pieces[0], dh_half, gains, *sums)
    grad_x, qkv_parts, out_own = tie(grad_x, qkv_parts, out_own)
    gx_own = to_groups(grad_x)
    out_own = jnp.stack(out_own)
    layer_out = assemble(ids, out_own, swap(out_own), BF)
    qkv_parts = call(
        qkv_sum_kernel,
        (struct((shard, WIDE), BF),) * members,
        "sv",
        scratch=[pltpu.VMEM((width // groups, WIDE), F32)],
        moved=width * WIDE * 4,
    )(ids, qkv_parts)
    gx_own, qkv_parts, layer_out, out_grads, feed_grads = tie(
        gx_own, qkv_parts, layer_out, out_grads, feed_grads
    )
    feed_grads = exchange(feed_grads, lines)
    out_grads = to_members(out_grads)
    qkv_parts = to_members(qkv_parts)
    out_grads = call(
        functools.partial(sum_split_kernel, members),
        (struct((shard, local), BF),) * groups,
        "s" + "v" * members,
        scratch=[pltpu.VMEM((groups, shard, local), BF)],
        moved=groups * shard * local * 12,
    )(ids, *out_grads)
    out_grads = to_groups(out_grads)
    gx_other = [swap(piece) for piece in gx_own]
    grad_up, grad_down, grad_out, gain_two = call(
        functools.partial(rows_kernel, groups),
        (struct((shard, local), F32),)
        + (struct((local, shard), F32),) * 2
        + (struct((shard, LANES), F32),),
        "v" * (groups + 2),
        moved=shard * local * 36,
    )(feed_grads, w_up, *out_grads)
    grad_q, grad_k, grad_v, small = call(
        functools.partial(qkv_rows_kernel, mine),
        (struct((shard, local), F32),) * 3 + (struct((shard, LANES), F32),),
        "s" + "v" * (members + 3),
        scratch=[pltpu.VMEM((members, shard, WIDE), F32)],
        moved=shard * local * 24,
    )(ids, *qkv_parts, w_query, w_key, w_value)
    lane = lax.broadcasted_iota(jnp.int32, small.shape, 1)
    small = jnp.where(lane == 2, gain_two, small)
    small = small + swap(small)
    gx_other, small = tie(gx_other, small)
    grad_tokens = call(
        functools.partial(place_kernel, groups),
        struct((groups, tok_rows, width), F32),
        "s" + "v" * (2 * groups),
        moved=rows * width * 8,
    )(ids, *gx_own, *gx_other)
    return (
        layer_out,
        grad_tokens,
        grad_q,
        grad_k,
        grad_v,
        grad_out,
        grad_up,
        grad_down,
        small[:, 0] / gain_attn.astype(F32),
        small[:, 2] / gain_mlp.astype(F32),
        small[:size, 1],
    )


def fits(shapes, mesh):
    groups, stream, width = shapes[0].shape
    count, cores = mesh.shape["ctx"], mesh.shape["tp"]
    size = shapes[11].shape[0]
    if cores != 2 or count % groups:
        return False
    members = count // groups
    local_heads = shapes[3].shape[1] // cores // size
    return (
        groups & (groups - 1) == 0
        and members & (members - 1) == 0
        and members % 2 == 0
        and local_heads % members == 0
        and stream // count == LANES
        and stream % 512 == 0
        and size % 16 == 0
        and size <= LANES
        and size <= width // count
        and width // count % 16 == 0
        and 3 * local_heads // members * size + 2 <= WIDE
        and 3 * local_heads // members * size >= WIDE - LANES
        and width % (LANES * 2) == 0
    )


def segment_of(starts, positions):
    return jnp.sum((starts[None, :] <= positions[:, None]).astype(jnp.int32), axis=1)


def contract_rows(left, right):
    return lax.dot_general(
        left, right, (((0,), (0,)), ((), ())), preferred_element_type=jnp.float32
    )


def contract_cols(left, right):
    return lax.dot_general(
        left, right, (((1,), (1,)), ((), ())), preferred_element_type=jnp.float32
    )


def per_device(
    tokens,
    cotangent,
    doc_lengths,
    w_query,
    w_key,
    w_value,
    w_out,
    w_up,
    w_down,
    gain_attn,
    gain_mlp,
    query_scale,
):
    micro_count, tok_rows, model_width = tokens.shape
    head_size = query_scale.shape[0]
    local_cols = w_query.shape[1]
    head_count = local_cols // head_size
    stream = tok_rows * lax.axis_size("ctx")
    key_block = min(512, stream)
    block_count = stream // key_block
    positions = lax.axis_index("ctx") * tok_rows + jnp.arange(tok_rows, dtype=jnp.int32)
    local_sums = None
    scale_sum = jnp.zeros((head_size,), jnp.float32)
    outputs = []
    input_grads = []
    for micro_step in range(micro_count):
        gathered = (
            lax.all_gather(w_query, "ctx", axis=0, tiled=True),
            lax.all_gather(w_key, "ctx", axis=0, tiled=True),
            lax.all_gather(w_value, "ctx", axis=0, tiled=True),
            lax.all_gather(w_up, "ctx", axis=0, tiled=True),
            lax.all_gather(gain_attn, "ctx", axis=0, tiled=True),
            lax.all_gather(gain_mlp, "ctx", axis=0, tiled=True),
            lax.all_gather(w_out, "ctx", axis=1, tiled=True),
            lax.all_gather(w_down, "ctx", axis=1, tiled=True),
        )
        w_qkv = jnp.concatenate([gathered[0], gathered[1], gathered[2]], axis=1)
        up_full = gathered[3]
        gain_one = gathered[4].astype(jnp.float32)
        gain_two = gathered[5].astype(jnp.float32)
        out_full = gathered[6]
        down_full = gathered[7]
        lengths = doc_lengths[micro_step]
        starts = jnp.cumsum(lengths) - lengths
        query_seg = segment_of(starts, positions)
        stream_in = tokens[micro_step].astype(jnp.float32)
        scale_one = inverse_rms(stream_in)
        normed_one = (stream_in * scale_one * gain_one).astype(jnp.bfloat16)
        projected = jnp.dot(normed_one, w_qkv, preferred_element_type=jnp.float32)
        query_raw = projected[:, :local_cols].reshape(tok_rows, head_count, head_size)
        query_heads = (query_raw * query_scale).astype(jnp.bfloat16)
        key_local = projected[:, local_cols : 2 * local_cols].astype(jnp.bfloat16)
        value_local = projected[:, 2 * local_cols :].astype(jnp.bfloat16)
        row_top = jnp.full((head_count, tok_rows), MASKED, jnp.float32)
        key_piece = lax.all_gather(key_local, "ctx", axis=0, tiled=True)
        value_piece = lax.all_gather(value_local, "ctx", axis=0, tiled=True)
        length = key_piece.shape[0]
        key_pos = jnp.arange(length, dtype=jnp.int32)
        allowed = (key_pos[None, :] <= positions[:, None]) & (
            segment_of(starts, key_pos)[None, :] == query_seg[:, None]
        )
        scores = jnp.einsum(
            "qhd,khd->hqk",
            query_heads,
            key_piece.reshape(length, head_count, head_size),
            preferred_element_type=jnp.float32,
        )
        scores = jnp.where(allowed[None], scores, MASKED)
        new_top = jnp.maximum(row_top, jnp.max(scores, axis=-1))
        probs = jnp.where(allowed[None], jnp.exp(scores - new_top[:, :, None]), 0.0)
        row_sum = jnp.sum(probs, axis=-1)
        update = jnp.einsum(
            "hqk,khd->qhd",
            probs.astype(jnp.bfloat16),
            value_piece.reshape(length, head_count, head_size),
            preferred_element_type=jnp.float32,
        )
        weighted = update
        row_top, row_sum, weighted = (new_top, row_sum, weighted)
        attn_heads = weighted / jnp.transpose(row_sum)[:, :, None]
        log_total = row_top + jnp.log(row_sum)
        attn_low = attn_heads.reshape(tok_rows, local_cols).astype(jnp.bfloat16)
        attn_out = lax.psum(
            jnp.dot(attn_low, out_full, preferred_element_type=jnp.float32).astype(jnp.bfloat16),
            "tp",
        ).astype(jnp.float32)
        hidden = stream_in + attn_out
        scale_two = inverse_rms(hidden)
        normed_two = (hidden * scale_two * gain_two).astype(jnp.bfloat16)
        up_raw = jnp.dot(normed_two, up_full, preferred_element_type=jnp.float32)
        activated = jax.nn.silu(up_raw).astype(jnp.bfloat16)
        mlp_out = lax.psum(
            jnp.dot(activated, down_full, preferred_element_type=jnp.float32).astype(jnp.bfloat16),
            "tp",
        ).astype(jnp.float32)
        outputs.append((hidden + mlp_out).astype(jnp.bfloat16))
        grad_out = cotangent[micro_step]
        grad_down = contract_rows(activated, grad_out)
        grad_act = contract_cols(grad_out, down_full)
        sigma = jax.nn.sigmoid(up_raw)
        grad_up_raw = (grad_act * sigma * (1.0 + up_raw * (1.0 - sigma))).astype(jnp.bfloat16)
        grad_up = contract_rows(normed_two, grad_up_raw)
        grad_normed_two = lax.psum(
            contract_cols(grad_up_raw, up_full).astype(jnp.bfloat16), "tp"
        ).astype(jnp.float32)
        grad_gain_two = jnp.sum(grad_normed_two * hidden * scale_two, axis=0)
        weighted_two = grad_normed_two * gain_two
        grad_hidden = (
            grad_out.astype(jnp.float32)
            + scale_two * weighted_two
            - hidden * scale_two**3 * jnp.mean(weighted_two * hidden, axis=-1, keepdims=True)
        )
        hidden_low = grad_hidden.astype(jnp.bfloat16)
        grad_out_proj = contract_rows(attn_low, hidden_low)
        grad_attn = (
            contract_cols(hidden_low, out_full)
            .astype(jnp.bfloat16)
            .reshape(tok_rows, head_count, head_size)
        )
        delta = jnp.einsum("qhd,qhd->hq", grad_attn.astype(jnp.float32), attn_heads)
        key_all, value_all = (
            lax.all_gather(key_local, "ctx", axis=0, tiled=True),
            lax.all_gather(value_local, "ctx", axis=0, tiled=True),
        )

        def block_terms(key_piece, value_piece, offset):
            key_heads = key_piece.reshape(key_block, head_count, head_size)
            value_heads = value_piece.reshape(key_block, head_count, head_size)
            key_pos = offset + jnp.arange(key_block, dtype=jnp.int32)
            allowed = (key_pos[None, :] <= positions[:, None]) & (
                segment_of(starts, key_pos)[None, :] == query_seg[:, None]
            )
            scores = jnp.einsum(
                "qhd,khd->hqk", query_heads, key_heads, preferred_element_type=jnp.float32
            )
            probs = jnp.where(allowed[None], jnp.exp(scores - log_total[:, :, None]), 0.0)
            grad_probs = jnp.einsum(
                "qhd,khd->hqk", grad_attn, value_heads, preferred_element_type=jnp.float32
            )
            grad_scores = (probs * (grad_probs - delta[:, :, None])).astype(jnp.bfloat16)
            return (key_heads, probs, grad_scores)

        key_blocks = (
            key_all.reshape(block_count, key_block, local_cols),
            value_all.reshape(block_count, key_block, local_cols),
            jnp.arange(block_count, dtype=jnp.int32) * key_block,
        )
        zero_query = jnp.zeros((tok_rows, head_count, head_size), jnp.float32)

        def grad_block(grad_query, packed):
            key_heads, probs, grad_scores = block_terms(packed[0], packed[1], packed[2])
            grad_value = jnp.einsum(
                "hqk,qhd->khd",
                probs.astype(jnp.bfloat16),
                grad_attn,
                preferred_element_type=jnp.float32,
            )
            grad_query = grad_query + jnp.einsum(
                "hqk,khd->qhd", grad_scores, key_heads, preferred_element_type=jnp.float32
            )
            grad_key = jnp.einsum(
                "hqk,qhd->khd", grad_scores, query_heads, preferred_element_type=jnp.float32
            )
            return (
                grad_query,
                (
                    grad_key.reshape(key_block, local_cols),
                    grad_value.reshape(key_block, local_cols),
                ),
            )

        grad_query, (key_terms, value_terms) = lax.scan(grad_block, zero_query, key_blocks)
        key_grad, value_grad = (
            lax.psum_scatter(
                key_terms.reshape(stream, local_cols).astype(jnp.bfloat16),
                "ctx",
                scatter_dimension=0,
                tiled=True,
            ).astype(jnp.float32),
            lax.psum_scatter(
                value_terms.reshape(stream, local_cols).astype(jnp.bfloat16),
                "ctx",
                scatter_dimension=0,
                tiled=True,
            ).astype(jnp.float32),
        )
        grad_query_raw = (
            (grad_query * query_scale).astype(jnp.bfloat16).reshape(tok_rows, local_cols)
        )
        scale_part = jnp.sum(grad_query * query_raw, axis=(0, 1))
        grad_cols = jnp.concatenate(
            [grad_query_raw, key_grad.astype(jnp.bfloat16), value_grad.astype(jnp.bfloat16)], axis=1
        )
        grad_qkv = contract_rows(normed_one, grad_cols)
        grad_normed_one, scale_total = (
            lax.psum(contract_cols(grad_cols, w_qkv).astype(jnp.bfloat16), "tp").astype(
                jnp.float32
            ),
            lax.psum(scale_part.astype(jnp.bfloat16), "tp").astype(jnp.float32),
        )
        scale_sum = scale_sum + scale_total
        grad_gain_one = jnp.sum(grad_normed_one * stream_in * scale_one, axis=0)
        weighted_one = grad_normed_one * gain_one
        input_grads.append(
            grad_hidden
            + scale_one * weighted_one
            - stream_in * scale_one**3 * jnp.mean(weighted_one * stream_in, axis=-1, keepdims=True)
        )
        grads = (
            grad_qkv[:, :local_cols],
            grad_qkv[:, local_cols : 2 * local_cols],
            grad_qkv[:, 2 * local_cols :],
            grad_up,
            grad_gain_one,
            grad_gain_two,
            grad_out_proj,
            grad_down,
        )
        shares = (
            lax.psum_scatter(
                grads[0].astype(jnp.bfloat16), "ctx", scatter_dimension=0, tiled=True
            ).astype(jnp.float32),
            lax.psum_scatter(
                grads[1].astype(jnp.bfloat16), "ctx", scatter_dimension=0, tiled=True
            ).astype(jnp.float32),
            lax.psum_scatter(
                grads[2].astype(jnp.bfloat16), "ctx", scatter_dimension=0, tiled=True
            ).astype(jnp.float32),
            lax.psum_scatter(
                grads[3].astype(jnp.bfloat16), "ctx", scatter_dimension=0, tiled=True
            ).astype(jnp.float32),
            lax.psum_scatter(
                grads[4].astype(jnp.bfloat16), "ctx", scatter_dimension=0, tiled=True
            ).astype(jnp.float32),
            lax.psum_scatter(
                grads[5].astype(jnp.bfloat16), "ctx", scatter_dimension=0, tiled=True
            ).astype(jnp.float32),
            lax.psum_scatter(
                grads[6].astype(jnp.bfloat16), "ctx", scatter_dimension=1, tiled=True
            ).astype(jnp.float32),
            lax.psum_scatter(
                grads[7].astype(jnp.bfloat16), "ctx", scatter_dimension=1, tiled=True
            ).astype(jnp.float32),
        )
        local_sums = (
            shares
            if local_sums is None
            else tuple((total + extra for total, extra in zip(local_sums, shares)))
        )
    scale_grad = lax.psum(scale_sum, "ctx")
    return (
        jnp.stack(outputs),
        jnp.stack(input_grads),
        local_sums[0],
        local_sums[1],
        local_sums[2],
        local_sums[6],
        local_sums[3],
        local_sums[7],
        local_sums[4],
        local_sums[5],
        scale_grad,
    )


def solution(mesh):
    in_specs = (
        P(None, "ctx", None),
        P(None, "ctx", None),
        P(),
        P("ctx", "tp"),
        P("ctx", "tp"),
        P("ctx", "tp"),
        P("tp", "ctx"),
        P("ctx", "tp"),
        P("tp", "ctx"),
        P("ctx"),
        P("ctx"),
        P(),
    )
    out_specs = (
        P(None, "ctx", None),
        P(None, "ctx", None),
        P("ctx", "tp"),
        P("ctx", "tp"),
        P("ctx", "tp"),
        P("tp", "ctx"),
        P("ctx", "tp"),
        P("tp", "ctx"),
        P("ctx"),
        P("ctx"),
        P(),
    )

    def run(*arrays):
        body = stream_per_group if fits(arrays, mesh) else per_device
        return jax.shard_map(
            body, mesh=mesh, in_specs=in_specs, out_specs=out_specs, check_vma=False
        )(*arrays)

    return run
```

profile of v0, /device:TPU:0, one launch (start us, length us, event | category | flops | bytes accessed | tf_op | source)
XLA Modules:
  0.0 326.5 jit_solution(18220538175369816549)
XLA Ops:
  2.7 3.1 collective-permute-start
  5.8 2.6 collective-permute-start.1
  12.5 8.4 %collective-permute-done.1 = bf16[64,1280]{1,0:T(8,128)(2,1)S(1)} collective-permute-done((bf16[64,1280]{1,0:T(8,128)(2,1)S(1)}, bf16[64,1280]{1,0:T(8,128)(2,1)S(1)}, u32[]{:S(2)}, u32[]{:S(2)}) %collective-permute-start.1) | collective-permute-done | bytes 163872 | tf_op jit(solution)/shard_map/ppermute | solution.py:582
  20.9 4.9 %all-to-all-start = ((bf16[4,80,1920]{2,1,0:T(8,128)(2,1)}), bf16[4,80,1920]{2,1,0:T(8,128)(2,1)S(1)}, u32[]{:S(2)}, u32[]{:S(2)}) async-start(bf16[4,80,1920]{2,1,0:T(8,128)(2,1)} %shard_map.205), calls=%async_computation | async-start | bytes 2457600 | tf_op jit(solution)/shard_map/all_to_all | solution.py:598
  35.7 12.6 %collective-permute-done.3.refs_1_ = bf16[4,64,1280]{2,1,0:T(8,128)(2,1)S(1)} collective-permute-done((bf16[4,64,1280]{2,1,0:T(8,128)(2,1)S(1)}, bf16[4,64,1280]{2,1,0:T(8,128)(2,1)S(1)}, u32[]{:S(2)}, u32[]{:S(2)}) %collective-permute-start.3) | collective-permute-done | bytes 655392 | tf_op jit(solution)/shard_map/ppermute | solution.py:582
  48.3 13.1 %collective-permute-done.4.refs_2_ = bf16[4,64,1280]{2,1,0:T(8,128)(2,1)S(1)} collective-permute-done((bf16[4,64,1280]{2,1,0:T(8,128)(2,1)S(1)}, bf16[4,64,1280]{2,1,0:T(8,128)(2,1)S(1)}, u32[]{:S(2)}, u32[]{:S(2)}) %collective-permute-start.4) | collective-permute-done | bytes 655392 | tf_op jit(solution)/shard_map/ppermute | solution.py:582
  63.5 4.8 %all-to-all-start.1 = ((bf16[16,80,512]{2,1,0:T(8,128)(2,1)}), bf16[16,80,512]{2,1,0:T(8,128)(2,1)S(1)}, u32[]{:S(2)}, u32[]{:S(2)}) async-start(bf16[16,80,512]{2,1,0:T(8,128)(2,1)} %pad_maximum_fusion), calls=%async_computation.1 | async-start | bytes 2621440 | tf_op jit(solution)/shard_map/all_to_all | solution.py:598
  74.8 22.9 %collective-permute-done.13.refs_1_ = bf16[4,80,1920]{2,1,0:T(8,128)(2,1)S(1)} collective-permute-done((bf16[4,80,1920]{2,1,0:T(8,128)(2,1)S(1)}, bf16[4,80,1920]{2,1,0:T(8,128)(2,1)S(1)}, u32[]{:S(2)}, u32[]{:S(2)}) %collective-permute-start.13) | collective-permute-done | bytes 1228832 | tf_op jit(solution)/shard_map/ppermute | solution.py:582
  108.0 2.4 collective-permute-start.18
  111.6 7.4 %shard_map.208 = (bf16[2048,768]{1,0:T(8,128)(2,1)S(1)}, bf16[2048,1280]{1,0:T(8,128)(2,1)S(1)}) custom-call(s32[3]{0:T(128)S(1)} %pad_add_fusion.ids, bf16[4,64,1280]{2,1,0:T(8,128)(2,1)S(1)} %pad_maximum_fusion.2.refs_0_, bf16[4,64,1280]{2,1,0:T(8,128)(2,1)S(1)} %copy-done.32, bf16[4,64,1280]{2,1,0:T(8,128)(2,1)S(1)} %copy-done.34, ...), custom_call_target="tpu_custom_call" | custom-call | flops 4026531840 | bytes 10485760 | tf_op jit(solution)/shard_map/pallas_call | solution.py:653
  119.0 11.4 %shard_map.209 = (bf16[160,512]{1,0:T(8,128)(2,1)S(1)}, bf16[160,512]{1,0:T(8,128)(2,1)S(1)}, bf16[160,512]{1,0:T(8,128)(2,1)S(1)}, bf16[160,512]{1,0:T(8,128)(2,1)S(1)}, f32[2,136,2048]{2,1,0:T(8,128)S(1)}) custom-call(s32[3]{0:T(128)S(1)} %pad_add_fusion.ids, s32[4,8]{1,0:T(4,128)S(1)} %copy-done.57, bf16[2048,768]{1,0:T(8,128)(2,1)S(1)} %get-tuple-element.245.proj), custom_call_target="tpu_custom_call" | custom-call | flops 2147483648 | bytes 5242880 | tf_op jit(solution)/shard_map/pallas_call | solution.py:662
  137.6 2.6 collective-permute-done.22.refs_2_
  142.7 3.3 %collective-permute-done.20.refs_3_ = bf16[4,64,1280]{2,1,0:T(8,128)(2,1)S(1)} collective-permute-done((bf16[4,64,1280]{2,1,0:T(8,128)(2,1)S(1)}, bf16[4,64,1280]{2,1,0:T(8,128)(2,1)S(1)}, u32[]{:S(2)}, u32[]{:S(2)}) %collective-permute-start.20) | collective-permute-done | bytes 655392 | tf_op jit(solution)/shard_map/ppermute | solution.py:589
  146.0 5.9 %shard_map.212 = (f32[512,1280]{1,0:T(8,128)S(1)}, bf16[512,1280]{1,0:T(8,128)(2,1)S(1)}, bf16[512,640]{1,0:T(8,128)(2,1)S(1)}, bf16[512,640]{1,0:T(8,128)(2,1)S...) custom-call(s32[3]{0:T(128)S(1)} %pad_add_fusion.ids, ...), custom_call_target="tpu_custom_call" | custom-call | flops 3355443200 | bytes 9830400 | tf_op jit(solution)/shard_map/pallas_call | solution.py:692
  152.5 3.0 shard_map.213
  156.9 3.7 %shard_map.214 = (bf16[512,1280]{1,0:T(8,128)(2,1)S(1)}, f32[4,64,1280]{2,1,0:T(8,128)S(1)}, bf16[160,512]{1,0:T(8,128)(2,1)S(1)}, bf16[160,512]{1,0:T(8,128)(2,...) custom-call(s32[3]{0:T(128)S(1)} %pad_add_fusion.ids, ...), custom_call_target="tpu_custom_call" | custom-call | flops 838860800 | bytes 9830400 | tf_op jit(solution)/shard_map/pallas_call | solution.py:717
  174.4 4.9 %collective-permute-start.33 = (bf16[64,1280]{1,0:T(8,128)(2,1)S(1)}, bf16[64,1280]{1,0:T(8,128)(2,1)S(1)}, u32[]{:S(2)}, u32[]{:S(2)}) collective-permute-start(bf16[64,1280]{1,0:T(8,128)(2,1)S(1)} %get-tuple-element.318), channel_id=1, source_target_pairs={{0,8},{2,10},{4,12},{6,14},{8,0},{10,2},{12,4},{14,6},{16,24},{18,... | collective-permute-start | bytes 491528 | tf_op jit(solution)/shard_map/ppermute | solution.py:582
  180.2 25.3 %shard_map.216 = (bf16[2048,768]{1,0:T(8,128)(2,1)S(1)}, bf16[4,4,64,1280]{3,2,1,0:T(8,128)(2,1)S(1)}, bf16[1280,512]{1,0:T(8,128)(2,1)}) custom-call(s32[3]{0:T(128)S(1)} %pad_add_fusion.ids, s32[4,8]{1,0:T(4,128)S(1)} %copy-done.57, bf16[2048,768]{1,0:T(8,128)(2,1)S(1)} %get-tuple-element.245.proj, f32[2,136,2048]{2,1,0:T(8,128)S(1)} %get-tuple-element.286.kept, ...), custom_call_target="tpu_custom_call" | custom-call | flops 5368709120 | bytes 10485760 | tf_op jit(solution)/shard_map/pallas_call | solution.py:745
  205.6 2.8 collective-permute-done.32.refs_3_
  208.4 4.9 %collective-permute-done.35.other = bf16[4,4,64,1280]{3,2,1,0:T(8,128)(2,1)S(1)} collective-permute-done((bf16[4,4,64,1280]{3,2,1,0:T(8,128)(2,1)S(1)}, bf16[4,4,64,1280]{3,2,1,0:T(8,128)(2,1)S(1)}, u32[]{:S(2)}, u32[]{:S(2)}) %collective-permute-start.35) | collective-permute-done | bytes 2621472 | tf_op jit(solution)/shard_map/ppermute | solution.py:589
  213.3 2.7 shard_map.217
  218.6 7.1 %all-to-all-start.2 = ((bf16[4,320,512]{2,1,0:T(8,128)(2,1)}), bf16[4,320,512]{2,1,0:T(8,128)(2,1)S(1)}, u32[]{:S(2)}, u32[]{:S(2)}) async-start(bf16[4,320,512]{2,1,0:T(8,128)(2,1)} %bitcast.21), calls=%async_computation.2 | async-start | bytes 2621440 | tf_op jit(solution)/shard_map/all_to_all | solution.py:598
  229.3 3.8 %collective-permute-start.39 = (bf16[64,1280]{1,0:T(8,128)(2,1)}, bf16[64,1280]{1,0:T(8,128)(2,1)}, u32[]{:S(2)}, u32[]{:S(2)}) collective-permute-start(bf16[64,1280]{1,0:T(8,128)(2,1)} %copy-done.48), channel_id=1, source_target_pairs={{0,24},{2,26},{4,28},{6,30},{8,16},{10,18},{12,20},{14,22},{16,8},... | collective-permute-start | bytes 491528 | tf_op jit(solution)/shard_map/ppermute | solution.py:582
  237.9 5.7 %collective-permute-done.36.refs_4_ = bf16[4,64,1280]{2,1,0:T(8,128)(2,1)S(1)} collective-permute-done((bf16[4,64,1280]{2,1,0:T(8,128)(2,1)}, bf16[4,64,1280]{2,1,0:T(8,128)(2,1)S(1)}, u32[]{:S(2)}, u32[]{:S(2)}) %collective-permute-start.36) | collective-permute-done | bytes 655392 | tf_op jit(solution)/shard_map/ppermute | solution.py:582
  243.6 14.0 %collective-permute-done.37.refs_5_ = bf16[4,64,1280]{2,1,0:T(8,128)(2,1)S(1)} collective-permute-done((bf16[4,64,1280]{2,1,0:T(8,128)(2,1)}, bf16[4,64,1280]{2,1,0:T(8,128)(2,1)S(1)}, u32[]{:S(2)}, u32[]{:S(2)}) %collective-permute-start.37) | collective-permute-done | bytes 655392 | tf_op jit(solution)/shard_map/ppermute | solution.py:582
  263.2 3.3 %collective-permute-start.40 = (bf16[64,1280]{1,0:T(8,128)(2,1)}, bf16[64,1280]{1,0:T(8,128)(2,1)S(1)}, u32[]{:S(2)}, u32[]{:S(2)}) collective-permute-start(bf16[64,1280]{1,0:T(8,128)(2,1)} %copy-done.52), channel_id=1, source_target_pairs={{0,8},{2,10},{4,12},{6,14},{8,0},{10,2},{12,4},{14,6},{16,24},{18,... | collective-permute-start | bytes 491528 | tf_op jit(solution)/shard_map/ppermute | solution.py:582
  266.6 2.4 collective-permute-start.42
  273.9 7.8 %collective-permute-done.41.refs_2_ = bf16[64,1280]{1,0:T(8,128)(2,1)S(1)} collective-permute-done((bf16[64,1280]{1,0:T(8,128)(2,1)}, bf16[64,1280]{1,0:T(8,128)(2,1)S(1)}, u32[]{:S(2)}, u32[]{:S(2)}) %collective-permute-start.41) | collective-permute-done | bytes 163872 | tf_op jit(solution)/shard_map/ppermute | solution.py:582
  281.7 4.7 %all-to-all-start.3 = ((bf16[4,80,1280]{2,1,0:T(8,128)(2,1)}), bf16[4,80,1280]{2,1,0:T(8,128)(2,1)S(1)}, u32[]{:S(2)}, u32[]{:S(2)}) async-start(bf16[4,80,1280]{2,1,0:T(8,128)(2,1)} %shard_map.218), calls=%async_computation.3 | async-start | bytes 1638400 | tf_op jit(solution)/shard_map/all_to_all | solution.py:598
  292.3 6.7 %collective-permute-done.48.refs_1_ = bf16[4,80,640]{2,1,0:T(8,128)(2,1)S(1)} collective-permute-done((bf16[4,80,640]{2,1,0:T(8,128)(2,1)}, bf16[4,80,640]{2,1,0:T(8,128)(2,1)S(1)}, u32[]{:S(2)}, u32[]{:S(2)}) %collective-permute-start.48) | collective-permute-done | bytes 409632 | tf_op jit(solution)/shard_map/ppermute | solution.py:582
  300.8 7.8 %collective-permute-done.49.refs_2_ = bf16[4,80,640]{2,1,0:T(8,128)(2,1)S(1)} collective-permute-done((bf16[4,80,640]{2,1,0:T(8,128)(2,1)}, bf16[4,80,640]{2,1,0:T(8,128)(2,1)S(1)}, u32[]{:S(2)}, u32[]{:S(2)}) %collective-permute-start.49) | collective-permute-done | bytes 409632 | tf_op jit(solution)/shard_map/ppermute | solution.py:582
  309.6 2.6 collective-permute-start.51
  (265 shorter events, 106.4 us)
Async XLA Ops:
  5.8 15.0 %collective-permute-start.1 = (bf16[64,1280]{1,0:T(8,128)(2,1)S(1)}, bf16[64,1280]{1,0:T(8,128)(2,1)S(1)}, u32[]{:S(2)}, u32[]{:S(2)}) collective-permute-start(bf16[64,1280]{1,0:T(8,128)(2,1)S(1)} %get-tuple-element.210), channel_id=1, source_target_pairs={{0,16},{2,18},{4,20},{6,22},{8,24},{10,26},{12,28},{14,30},{16,0},... | collective-permute-start | bytes 491528 | tf_op jit(solution)/shard_map/ppermute | solution.py:582
  20.9 41.3 %all-to-all-start = ((bf16[4,80,1920]{2,1,0:T(8,128)(2,1)}), bf16[4,80,1920]{2,1,0:T(8,128)(2,1)S(1)}, u32[]{:S(2)}, u32[]{:S(2)}) async-start(bf16[4,80,1920]{2,1,0:T(8,128)(2,1)} %shard_map.205), calls=%async_computation | async-start | bytes 2457600 | tf_op jit(solution)/shard_map/all_to_all | solution.py:598
  29.4 18.9 %collective-permute-start.3 = (bf16[4,64,1280]{2,1,0:T(8,128)(2,1)S(1)}, bf16[4,64,1280]{2,1,0:T(8,128)(2,1)S(1)}, u32[]{:S(2)}, u32[]{:S(2)}) collective-permute-start(bf16[4,64,1280]{2,1,0:T(8,128)(2,1)S(1)} %pad_maximum_fusion.2.refs_0_), channel_id=1, source_target_pairs={{0,2},{2,0},{4,6},{6,4},{8,10},{10,8},{12,14},{14,12},{16,18},{18,... | collective-permute-start | bytes 1966088 | tf_op jit(solution)/shard_map/ppermute | solution.py:582
  30.9 30.5 %collective-permute-start.4 = (bf16[4,64,1280]{2,1,0:T(8,128)(2,1)S(1)}, bf16[4,64,1280]{2,1,0:T(8,128)(2,1)S(1)}, u32[]{:S(2)}, u32[]{:S(2)}) collective-permute-start(bf16[4,64,1280]{2,1,0:T(8,128)(2,1)S(1)} %pad_maximum_fusion.2.refs_0_), channel_id=1, source_target_pairs={{0,4},{2,6},{4,0},{6,2},{8,12},{10,14},{12,8},{14,10},{16,20},{18,... | collective-permute-start | bytes 1966088 | tf_op jit(solution)/shard_map/ppermute | solution.py:582
  35.2 27.1 %collective-permute-start.8 = (bf16[4,64,1280]{2,1,0:T(8,128)(2,1)S(1)}, bf16[4,64,1280]{2,1,0:T(8,128)(2,1)}, u32[]{:S(2)}, u32[]{:S(2)}) collective-permute-start(bf16[4,64,1280]{2,1,0:T(8,128)(2,1)S(1)} %pad_maximum_fusion.2.refs_0_), channel_id=1, source_target_pairs={{0,6},{2,4},{4,2},{6,0},{8,14},{10,12},{12,10},{14,8},{16,22},{18,... | collective-permute-start | bytes 1966088 | tf_op jit(solution)/shard_map/ppermute | solution.py:582
  63.5 35.3 %all-to-all-start.1 = ((bf16[16,80,512]{2,1,0:T(8,128)(2,1)}), bf16[16,80,512]{2,1,0:T(8,128)(2,1)S(1)}, u32[]{:S(2)}, u32[]{:S(2)}) async-start(bf16[16,80,512]{2,1,0:T(8,128)(2,1)} %pad_maximum_fusion), calls=%async_computation.1 | async-start | bytes 2621440 | tf_op jit(solution)/shard_map/all_to_all | solution.py:598
  68.3 29.4 %collective-permute-start.13 = (bf16[4,80,1920]{2,1,0:T(8,128)(2,1)S(1)}, bf16[4,80,1920]{2,1,0:T(8,128)(2,1)S(1)}, u32[]{:S(2)}, u32[]{:S(2)}) collective-permute-start(bf16[4,80,1920]{2,1,0:T(8,128)(2,1)S(1)} %all-to-all-done.refs_0_), channel_id=1, source_target_pairs={{0,2},{2,0},{4,6},{6,4},{8,10},{10,8},{12,14},{14,12},{16,18},{18,... | collective-permute-start | bytes 3686408 | tf_op jit(solution)/shard_map/ppermute | solution.py:582
  68.3 30.5 %collective-permute-start.14 = (bf16[4,80,1920]{2,1,0:T(8,128)(2,1)S(1)}, bf16[4,80,1920]{2,1,0:T(8,128)(2,1)}, u32[]{:S(2)}, u32[]{:S(2)}) collective-permute-start(bf16[4,80,1920]{2,1,0:T(8,128)(2,1)S(1)} %all-to-all-done.refs_0_), channel_id=1, source_target_pairs={{0,4},{2,6},{4,0},{6,2},{8,12},{10,14},{12,8},{14,10},{16,20},{18,... | collective-permute-start | bytes 3686408 | tf_op jit(solution)/shard_map/ppermute | solution.py:582
  100.0 30.4 %collective-permute-start.15 = (bf16[2,80,1920]{2,1,0:T(8,128)(2,1)S(1)}, bf16[2,80,1920]{2,1,0:T(8,128)(2,1)S(1)}, u32[]{:S(2)}, u32[]{:S(2)}) collective-permute-start(bf16[2,80,1920]{2,1,0:T(8,128)(2,1)S(1)} %slice.15), channel_id=1, source_target_pairs={{0,2},{2,0},{4,6},{6,4},{8,10},{10,8},{12,14},{14,12},{16,18},{18,... | collective-permute-start | bytes 1843208 | tf_op jit(solution)/shard_map/ppermute | solution.py:582
  100.9 29.5 %collective-permute-start.16 = (bf16[2,80,1920]{2,1,0:T(8,128)(2,1)S(1)}, bf16[2,80,1920]{2,1,0:T(8,128)(2,1)S(1)}, u32[]{:S(2)}, u32[]{:S(2)}) collective-permute-start(bf16[2,80,1920]{2,1,0:T(8,128)(2,1)S(1)} %slice.16), channel_id=1, source_target_pairs={{0,4},{2,6},{4,0},{6,2},{8,12},{10,14},{12,8},{14,10},{16,20},{18,... | collective-permute-start | bytes 1843208 | tf_op jit(solution)/shard_map/ppermute | solution.py:582
  105.9 24.6 %collective-permute-start.17 = (bf16[64,1280]{1,0:T(8,128)(2,1)S(1)}, bf16[64,1280]{1,0:T(8,128)(2,1)S(1)}, u32[]{:S(2)}, u32[]{:S(2)}) collective-permute-start(bf16[64,1280]{1,0:T(8,128)(2,1)S(1)} %get-tuple-element.253), channel_id=1, source_target_pairs={{0,8},{2,10},{4,12},{6,14},{8,0},{10,2},{12,4},{14,6},{16,24},{18,... | collective-permute-start | bytes 491528 | tf_op jit(solution)/shard_map/ppermute | solution.py:582
  108.0 22.5 %collective-permute-start.18 = (bf16[64,1280]{1,0:T(8,128)(2,1)S(1)}, bf16[64,1280]{1,0:T(8,128)(2,1)S(1)}, u32[]{:S(2)}, u32[]{:S(2)}) collective-permute-start(bf16[64,1280]{1,0:T(8,128)(2,1)S(1)} %get-tuple-element.254), channel_id=1, source_target_pairs={{0,16},{2,18},{4,20},{6,22},{8,24},{10,26},{12,28},{14,30},{16,0},... | collective-permute-start | bytes 491528 | tf_op jit(solution)/shard_map/ppermute | solution.py:582
  110.4 20.2 %collective-permute-start.19 = (bf16[64,1280]{1,0:T(8,128)(2,1)S(1)}, bf16[64,1280]{1,0:T(8,128)(2,1)S(1)}, u32[]{:S(2)}, u32[]{:S(2)}) collective-permute-start(bf16[64,1280]{1,0:T(8,128)(2,1)S(1)} %get-tuple-element.255), channel_id=1, source_target_pairs={{0,24},{2,26},{4,28},{6,30},{8,16},{10,18},{12,20},{14,22},{16,8},... | collective-permute-start | bytes 491528 | tf_op jit(solution)/shard_map/ppermute | solution.py:582
  170.9 34.6 %collective-permute-start.30 = (bf16[4,80,1280]{2,1,0:T(8,128)(2,1)S(1)}, bf16[4,80,1280]{2,1,0:T(8,128)(2,1)S(1)}, u32[]{:S(2)}, u32[]{:S(2)}) collective-permute-start(bf16[4,80,1280]{2,1,0:T(8,128)(2,1)S(1)} %get-tuple-element.315), channel_id=1, source_target_pairs={{0,2},{2,0},{4,6},{6,4},{8,10},{10,8},{12,14},{14,12},{16,18},{18,... | collective-permute-start | bytes 2457608 | tf_op jit(solution)/shard_map/ppermute | solution.py:582
  172.2 33.3 %collective-permute-start.31 = (bf16[4,80,1280]{2,1,0:T(8,128)(2,1)S(1)}, bf16[4,80,1280]{2,1,0:T(8,128)(2,1)S(1)}, u32[]{:S(2)}, u32[]{:S(2)}) collective-permute-start(bf16[4,80,1280]{2,1,0:T(8,128)(2,1)S(1)} %get-tuple-element.316), channel_id=1, source_target_pairs={{0,4},{2,6},{4,0},{6,2},{8,12},{10,14},{12,8},{14,10},{16,20},{18,... | collective-permute-start | bytes 2457608 | tf_op jit(solution)/shard_map/ppermute | solution.py:582
  173.2 35.1 %collective-permute-start.32 = (bf16[4,80,1280]{2,1,0:T(8,128)(2,1)S(1)}, bf16[4,80,1280]{2,1,0:T(8,128)(2,1)S(1)}, u32[]{:S(2)}, u32[]{:S(2)}) collective-permute-start(bf16[4,80,1280]{2,1,0:T(8,128)(2,1)S(1)} %get-tuple-element.317), channel_id=1, source_target_pairs={{0,6},{2,4},{4,2},{6,0},{8,14},{10,12},{12,10},{14,8},{16,22},{18,... | collective-permute-start | bytes 2457608 | tf_op jit(solution)/shard_map/ppermute | solution.py:582
  174.4 31.1 %collective-permute-start.33 = (bf16[64,1280]{1,0:T(8,128)(2,1)S(1)}, bf16[64,1280]{1,0:T(8,128)(2,1)S(1)}, u32[]{:S(2)}, u32[]{:S(2)}) collective-permute-start(bf16[64,1280]{1,0:T(8,128)(2,1)S(1)} %get-tuple-element.318), channel_id=1, source_target_pairs={{0,8},{2,10},{4,12},{6,14},{8,0},{10,2},{12,4},{14,6},{16,24},{18,... | collective-permute-start | bytes 491528 | tf_op jit(solution)/shard_map/ppermute | solution.py:582
  179.3 26.2 %collective-permute-start.34 = (bf16[64,1280]{1,0:T(8,128)(2,1)S(1)}, bf16[64,1280]{1,0:T(8,128)(2,1)S(1)}, u32[]{:S(2)}, u32[]{:S(2)}) collective-permute-start(bf16[64,1280]{1,0:T(8,128)(2,1)S(1)} %get-tuple-element.319), channel_id=1, source_target_pairs={{0,16},{2,18},{4,20},{6,22},{8,24},{10,26},{12,28},{14,30},{16,0},... | collective-permute-start | bytes 491528 | tf_op jit(solution)/shard_map/ppermute | solution.py:582
  218.6 43.3 %all-to-all-start.2 = ((bf16[4,320,512]{2,1,0:T(8,128)(2,1)}), bf16[4,320,512]{2,1,0:T(8,128)(2,1)S(1)}, u32[]{:S(2)}, u32[]{:S(2)}) async-start(bf16[4,320,512]{2,1,0:T(8,128)(2,1)} %bitcast.21), calls=%async_computation.2 | async-start | bytes 2621440 | tf_op jit(solution)/shard_map/all_to_all | solution.py:598
  225.8 17.8 %collective-permute-start.36 = (bf16[4,64,1280]{2,1,0:T(8,128)(2,1)}, bf16[4,64,1280]{2,1,0:T(8,128)(2,1)S(1)}, u32[]{:S(2)}, u32[]{:S(2)}) collective-permute-start(bf16[4,64,1280]{2,1,0:T(8,128)(2,1)} %copy-done.43), channel_id=1, source_target_pairs={{0,2},{2,0},{4,6},{6,4},{8,10},{10,8},{12,14},{14,12},{16,18},{18,... | collective-permute-start | bytes 1966088 | tf_op jit(solution)/shard_map/ppermute | solution.py:582
  227.1 30.5 %collective-permute-start.37 = (bf16[4,64,1280]{2,1,0:T(8,128)(2,1)}, bf16[4,64,1280]{2,1,0:T(8,128)(2,1)S(1)}, u32[]{:S(2)}, u32[]{:S(2)}) collective-permute-start(bf16[4,64,1280]{2,1,0:T(8,128)(2,1)} %copy-done.42), channel_id=1, source_target_pairs={{0,4},{2,6},{4,0},{6,2},{8,12},{10,14},{12,8},{14,10},{16,20},{18,... | collective-permute-start | bytes 1966088 | tf_op jit(solution)/shard_map/ppermute | solution.py:582
  228.1 29.5 %collective-permute-start.38 = (bf16[4,64,1280]{2,1,0:T(8,128)(2,1)}, bf16[4,64,1280]{2,1,0:T(8,128)(2,1)S(1)}, u32[]{:S(2)}, u32[]{:S(2)}) collective-permute-start(bf16[4,64,1280]{2,1,0:T(8,128)(2,1)} %copy-done.41), channel_id=1, source_target_pairs={{0,6},{2,4},{4,2},{6,0},{8,14},{10,12},{12,10},{14,8},{16,22},{18,... | collective-permute-start | bytes 1966088 | tf_op jit(solution)/shard_map/ppermute | solution.py:582
  229.3 30.5 %collective-permute-start.39 = (bf16[64,1280]{1,0:T(8,128)(2,1)}, bf16[64,1280]{1,0:T(8,128)(2,1)}, u32[]{:S(2)}, u32[]{:S(2)}) collective-permute-start(bf16[64,1280]{1,0:T(8,128)(2,1)} %copy-done.48), channel_id=1, source_target_pairs={{0,24},{2,26},{4,28},{6,30},{8,16},{10,18},{12,20},{14,22},{16,8},... | collective-permute-start | bytes 491528 | tf_op jit(solution)/shard_map/ppermute | solution.py:582
  266.5 15.2 %collective-permute-start.41 = (bf16[64,1280]{1,0:T(8,128)(2,1)}, bf16[64,1280]{1,0:T(8,128)(2,1)S(1)}, u32[]{:S(2)}, u32[]{:S(2)}) collective-permute-start(bf16[64,1280]{1,0:T(8,128)(2,1)} %copy-done.51), channel_id=1, source_target_pairs={{0,16},{2,18},{4,20},{6,22},{8,24},{10,26},{12,28},{14,30},{16,0},... | collective-permute-start | bytes 491528 | tf_op jit(solution)/shard_map/ppermute | solution.py:582
  266.6 15.1 %collective-permute-start.42 = (bf16[64,1280]{1,0:T(8,128)(2,1)S(1)}, bf16[64,1280]{1,0:T(8,128)(2,1)S(1)}, u32[]{:S(2)}, u32[]{:S(2)}) collective-permute-start(bf16[64,1280]{1,0:T(8,128)(2,1)S(1)} %copy-done.50), channel_id=1, source_target_pairs={{0,24},{2,26},{4,28},{6,30},{8,16},{10,18},{12,20},{14,22},{16,8},... | collective-permute-start | bytes 491528 | tf_op jit(solution)/shard_map/ppermute | solution.py:582
  281.7 38.7 %all-to-all-start.3 = ((bf16[4,80,1280]{2,1,0:T(8,128)(2,1)}), bf16[4,80,1280]{2,1,0:T(8,128)(2,1)S(1)}, u32[]{:S(2)}, u32[]{:S(2)}) async-start(bf16[4,80,1280]{2,1,0:T(8,128)(2,1)} %shard_map.218), calls=%async_computation.3 | async-start | bytes 1638400 | tf_op jit(solution)/shard_map/all_to_all | solution.py:598
  286.4 12.6 %collective-permute-start.48 = (bf16[4,80,640]{2,1,0:T(8,128)(2,1)}, bf16[4,80,640]{2,1,0:T(8,128)(2,1)S(1)}, u32[]{:S(2)}, u32[]{:S(2)}) collective-permute-start(bf16[4,80,640]{2,1,0:T(8,128)(2,1)} %copy-done.47), channel_id=1, source_target_pairs={{0,2},{2,0},{4,6},{6,4},{8,10},{10,8},{12,14},{14,12},{16,18},{18,... | collective-permute-start | bytes 1228808 | tf_op jit(solution)/shard_map/ppermute | solution.py:582
  287.8 20.9 %collective-permute-start.49 = (bf16[4,80,640]{2,1,0:T(8,128)(2,1)}, bf16[4,80,640]{2,1,0:T(8,128)(2,1)S(1)}, u32[]{:S(2)}, u32[]{:S(2)}) collective-permute-start(bf16[4,80,640]{2,1,0:T(8,128)(2,1)} %copy-done.46), channel_id=1, source_target_pairs={{0,4},{2,6},{4,0},{6,2},{8,12},{10,14},{12,8},{14,10},{16,20},{18,... | collective-permute-start | bytes 1228808 | tf_op jit(solution)/shard_map/ppermute | solution.py:582
  288.8 19.9 %collective-permute-start.50 = (bf16[4,80,640]{2,1,0:T(8,128)(2,1)S(1)}, bf16[4,80,640]{2,1,0:T(8,128)(2,1)S(1)}, u32[]{:S(2)}, u32[]{:S(2)}) collective-permute-start(bf16[4,80,640]{2,1,0:T(8,128)(2,1)S(1)} %copy-done.45), channel_id=1, source_target_pairs={{0,6},{2,4},{4,2},{6,0},{8,14},{10,12},{12,10},{14,8},{16,22},{18,... | collective-permute-start | bytes 1228808 | tf_op jit(solution)/shard_map/ppermute | solution.py:582
  289.9 23.9 %collective-permute-start.54 = (bf16[80,512]{1,0:T(8,128)(2,1)S(1)}, bf16[80,512]{1,0:T(8,128)(2,1)S(1)}, u32[]{:S(2)}, u32[]{:S(2)}) collective-permute-start(bf16[80,512]{1,0:T(8,128)(2,1)S(1)} %copy-done.56), channel_id=1, source_target_pairs={{0,2},{2,0},{4,6},{6,4},{8,10},{10,8},{12,14},{14,12},{16,18},{18,... | collective-permute-start | bytes 245768 | tf_op jit(solution)/shard_map/ppermute | solution.py:582
  291.3 23.5 %collective-permute-start.55 = (bf16[80,512]{1,0:T(8,128)(2,1)S(1)}, bf16[80,512]{1,0:T(8,128)(2,1)S(1)}, u32[]{:S(2)}, u32[]{:S(2)}) collective-permute-start(bf16[80,512]{1,0:T(8,128)(2,1)S(1)} %copy-done.54), channel_id=1, source_target_pairs={{0,4},{2,6},{4,0},{6,2},{8,12},{10,14},{12,8},{14,10},{16,20},{18,... | collective-permute-start | bytes 245768 | tf_op jit(solution)/shard_map/ppermute | solution.py:582
  299.0 15.7 %collective-permute-start.56 = (bf16[80,512]{1,0:T(8,128)(2,1)S(1)}, bf16[80,512]{1,0:T(8,128)(2,1)S(1)}, u32[]{:S(2)}, u32[]{:S(2)}) collective-permute-start(bf16[80,512]{1,0:T(8,128)(2,1)S(1)} %get-tuple-element.392), channel_id=1, source_target_pairs={{0,6},{2,4},{4,2},{6,0},{8,14},{10,12},{12,10},{14,8},{16,22},{18,... | collective-permute-start | bytes 245768 | tf_op jit(solution)/shard_map/ppermute | solution.py:582
  (94 other events, 717.9 us)
where the time goes:
time: 328 us; the launch traced here: 327 us
  waiting for transfers between devices  130 us (40%)
  starting transfers between devices  87.1 us (27%)
  Pallas kernels  81 us (25%)
  local copies, waits for them, and re-layouts  23.9 us (7%)
  other arithmetic  3.35 us (1%)
    ppermute x43, waiting for transfers between devices, across(): return lax.ppermute(a, 'ctx', [(i, i ^ mask) for i in range(count)])  117 us
    ppermute x43, starting transfers between devices, across(): return lax.ppermute(a, 'ctx', [(i, i ^ mask) for i in range(count)])  63 us
    pallas_call x1, Pallas kernels, stream_per_group(): call(functools.partial(attend_back_kernel, heads, size, members, bq, bk),...  25.3 us
    unnamed x130, local copies, waits for them, and re-layouts  21.8 us
    all_to_all x4, starting transfers between devices, exchange(): return lax.all_to_all(a, 'ctx', 0, 0, axis_index_groups=teams, tiled=True)  21.6 us
    pallas_call x1, Pallas kernels, stream_per_group(): call(functools.partial(attend_kernel, heads, size, members, bq, bk), (str...  11.4 us
    ppermute x15, waiting for transfers between devices, swap(): return lax.ppermute(a, 'tp', [(0, 1), (1, 0)])  10.4 us
    pallas_call x1, Pallas kernels, stream_per_group(): call(functools.partial(project_kernel, members, 512), (struct((stream, pa...  7.38 us
  transfers between devices with their start and end apart: 62, of which 26 were waited for; matrix products, arithmetic and copies ran while one was open for 1% of the time, Pallas kernels for 20%

commit v1 on v0

--- a/solution.py
+++ b/solution.py
@@ -785,15 +785,19 @@
         "v" * members,
         moved=groups * shard * local * 24,
     )(*feed_grads)
-    sums, feed_grads = tie(sums, feed_grads)
+    sums, feed_grads, out_grads = tie(sums, feed_grads, out_grads)
     grad_x = call(
         functools.partial(tokens_kernel, groups),
         (struct((half, width), BF),) * groups,
         "svvv" + "v" * len(sums),
         moved=groups * half * width * 12,
     )(ids, pieces[0], dh_half, gains, *sums)
-    grad_x, qkv_parts, out_own = tie(grad_x, qkv_parts, out_own)
+    grad_x, qkv_parts, out_own, feed_grads, out_grads = tie(
+        grad_x, qkv_parts, out_own, feed_grads, out_grads
+    )
+    feed_grads = exchange(feed_grads, lines)
     gx_own = to_groups(grad_x)
+    out_grads = to_members(out_grads)
     out_own = jnp.stack(out_own)
     layer_out = assemble(ids, out_own, swap(out_own), BF)
     qkv_parts = call(
@@ -803,11 +807,7 @@
         scratch=[pltpu.VMEM((width // groups, WIDE), F32)],
         moved=width * WIDE * 4,
     )(ids, qkv_parts)
-    gx_own, qkv_parts, layer_out, out_grads, feed_grads = tie(
-        gx_own, qkv_parts, layer_out, out_grads, feed_grads
-    )
-    feed_grads = exchange(feed_grads, lines)
-    out_grads = to_members(out_grads)
+    gx_own, qkv_parts, layer_out, out_grads = tie(gx_own, qkv_parts, layer_out, out_grads)
     qkv_parts = to_members(qkv_parts)
     out_grads = call(
         functools.partial(sum_split_kernel, members),

time: 328 us -> 324 us (0.988)
  Pallas kernels: 81 us -> 90.9 us
  waiting for transfers between devices: 130 us -> 121 us
    ppermute x43, waiting for transfers between devices: 117 us -> 110 us  [across(): return lax.ppermute(a, 'ctx', [(i, i ^ mask) for i in range(count)])]
    pallas_call x1, Pallas kernels: 25.3 us -> 29.7 us  [stream_per_group(): call(functools.partial(attend_back_kernel, heads, size, members, bq, bk),...]
    pallas_call x1, Pallas kernels: 11.4 us -> 15.5 us  [stream_per_group(): call(functools.partial(attend_kernel, heads, size, members, bq, bk), (str...]
    unnamed x130 -> x124, local copies, waits for them, and re-layouts: 21.8 us -> 20.3 us
  transfers between devices with their start and end apart: 62 -> 62, of which waited for: 26 -> 23; matrix products, arithmetic and copies ran while one was open for 1% -> 1% of each run, Pallas kernels for 20% -> 23%
where the time goes in v1:
time: 324 us; the launch traced here: 323 us
  waiting for transfers between devices  121 us (37%)
  Pallas kernels  90.9 us (28%)
  starting transfers between devices  84.2 us (26%)
  local copies, waits for them, and re-layouts  22.4 us (7%)
    ppermute x43, waiting for transfers between devices, across(): return lax.ppermute(a, 'ctx', [(i, i ^ mask) for i in range(count)])  110 us
    ppermute x43, starting transfers between devices, across(): return lax.ppermute(a, 'ctx', [(i, i ^ mask) for i in range(count)])  62 us
    pallas_call x1, Pallas kernels, stream_per_group(): call(functools.partial(attend_back_kernel, heads, size, members, bq, bk),...  29.7 us
    unnamed x124, local copies, waits for them, and re-layouts  20.3 us
    all_to_all x4, starting transfers between devices, exchange(): return lax.all_to_all(a, 'ctx', 0, 0, axis_index_groups=teams, tiled=True)  19.2 us
    pallas_call x1, Pallas kernels, stream_per_group(): call(functools.partial(attend_kernel, heads, size, members, bq, bk), (str...  15.5 us
    ppermute x15, waiting for transfers between devices, swap(): return lax.ppermute(a, 'tp', [(0, 1), (1, 0)])  10.4 us
    pallas_call x1, Pallas kernels, stream_per_group(): call(functools.partial(project_kernel, members, 512), (struct((stream, pa...  7.38 us
  transfers between devices with their start and end apart: 62, of which 23 were waited for; matrix products, arithmetic and copies ran while one was open for 1% of the time, Pallas kernels for 23%

profile of v1, /device:TPU:0, one launch (start us, length us, event | category | flops | bytes accessed | tf_op | source)
XLA Modules:
  0.0 323.3 jit_solution(11666620461642836153)
XLA Ops:
  2.7 3.1 collective-permute-start
  5.8 2.6 collective-permute-start.1
  12.5 8.4 %collective-permute-done.1 = bf16[64,1280]{1,0:T(8,128)(2,1)S(1)} collective-permute-done((bf16[64,1280]{1,0:T(8,128)(2,1)S(1)}, bf16[64,1280]{1,0:T(8,128)(2,1)S(1)}, u32[]{:S(2)}, u32[]{:S(2)}) %collective-permute-start.1) | collective-permute-done | bytes 163872 | tf_op jit(solution)/shard_map/ppermute | solution.py:582
  20.9 4.9 %all-to-all-start = ((bf16[4,80,1920]{2,1,0:T(8,128)(2,1)}), bf16[4,80,1920]{2,1,0:T(8,128)(2,1)S(1)}, u32[]{:S(2)}, u32[]{:S(2)}) async-start(bf16[4,80,1920]{2,1,0:T(8,128)(2,1)} %shard_map.205), calls=%async_computation | async-start | bytes 2457600 | tf_op jit(solution)/shard_map/all_to_all | solution.py:598
  35.7 12.6 %collective-permute-done.3.refs_1_ = bf16[4,64,1280]{2,1,0:T(8,128)(2,1)S(1)} collective-permute-done((bf16[4,64,1280]{2,1,0:T(8,128)(2,1)S(1)}, bf16[4,64,1280]{2,1,0:T(8,128)(2,1)S(1)}, u32[]{:S(2)}, u32[]{:S(2)}) %collective-permute-start.3) | collective-permute-done | bytes 655392 | tf_op jit(solution)/shard_map/ppermute | solution.py:582
  48.3 13.1 %collective-permute-done.4.refs_2_ = bf16[4,64,1280]{2,1,0:T(8,128)(2,1)S(1)} collective-permute-done((bf16[4,64,1280]{2,1,0:T(8,128)(2,1)S(1)}, bf16[4,64,1280]{2,1,0:T(8,128)(2,1)S(1)}, u32[]{:S(2)}, u32[]{:S(2)}) %collective-permute-start.4) | collective-permute-done | bytes 655392 | tf_op jit(solution)/shard_map/ppermute | solution.py:582
  63.5 4.8 %all-to-all-start.1 = ((bf16[16,80,512]{2,1,0:T(8,128)(2,1)}), bf16[16,80,512]{2,1,0:T(8,128)(2,1)S(1)}, u32[]{:S(2)}, u32[]{:S(2)}) async-start(bf16[16,80,512]{2,1,0:T(8,128)(2,1)} %pad_maximum_fusion), calls=%async_computation.1 | async-start | bytes 2621440 | tf_op jit(solution)/shard_map/all_to_all | solution.py:598
  74.8 22.9 %collective-permute-done.13.refs_1_ = bf16[4,80,1920]{2,1,0:T(8,128)(2,1)S(1)} collective-permute-done((bf16[4,80,1920]{2,1,0:T(8,128)(2,1)S(1)}, bf16[4,80,1920]{2,1,0:T(8,128)(2,1)S(1)}, u32[]{:S(2)}, u32[]{:S(2)}) %collective-permute-start.13) | collective-permute-done | bytes 1228832 | tf_op jit(solution)/shard_map/ppermute | solution.py:582
  108.0 2.4 collective-permute-start.18
  111.6 7.4 %shard_map.208 = (bf16[2048,768]{1,0:T(8,128)(2,1)S(1)}, bf16[2048,1280]{1,0:T(8,128)(2,1)S(1)}) custom-call(s32[3]{0:T(128)S(1)} %pad_add_fusion.ids, bf16[4,64,1280]{2,1,0:T(8,128)(2,1)S(1)} %pad_maximum_fusion.2.refs_0_, bf16[4,64,1280]{2,1,0:T(8,128)(2,1)S(1)} %copy-done.33, bf16[4,64,1280]{2,1,0:T(8,128)(2,1)S(1)} %copy-done.35, ...), custom_call_target="tpu_custom_call" | custom-call | flops 4026531840 | bytes 10485760 | tf_op jit(solution)/shard_map/pallas_call | solution.py:653
  119.0 15.5 %shard_map.209 = (bf16[160,512]{1,0:T(8,128)(2,1)S(1)}, bf16[160,512]{1,0:T(8,128)(2,1)S(1)}, bf16[160,512]{1,0:T(8,128)(2,1)S(1)}, bf16[160,512]{1,0:T(8,128)(2,1)S(1)}, f32[2,136,2048]{2,1,0:T(8,128)S(1)}) custom-call(s32[3]{0:T(128)S(1)} %pad_add_fusion.ids, s32[4,8]{1,0:T(4,128)S(1)} %copy-done.52, bf16[2048,768]{1,0:T(8,128)(2,1)S(1)} %get-tuple-element.253.proj), custom_call_target="tpu_custom_call" | custom-call | flops 2147483648 | bytes 5242880 | tf_op jit(solution)/shard_map/pallas_call | solution.py:662
  141.7 2.6 collective-permute-done.22.refs_2_
  146.8 3.3 %collective-permute-done.20.refs_3_ = bf16[4,64,1280]{2,1,0:T(8,128)(2,1)S(1)} collective-permute-done((bf16[4,64,1280]{2,1,0:T(8,128)(2,1)S(1)}, bf16[4,64,1280]{2,1,0:T(8,128)(2,1)S(1)}, u32[]{:S(2)}, u32[]{:S(2)}) %collective-permute-start.20) | collective-permute-done | bytes 655392 | tf_op jit(solution)/shard_map/ppermute | solution.py:589
  150.1 5.9 %shard_map.212 = (f32[512,1280]{1,0:T(8,128)S(1)}, bf16[512,1280]{1,0:T(8,128)(2,1)S(1)}, bf16[512,640]{1,0:T(8,128)(2,1)S(1)}, bf16[512,640]{1,0:T(8,128)(2,1)S...) custom-call(s32[3]{0:T(128)S(1)} %pad_add_fusion.ids, ...), custom_call_target="tpu_custom_call" | custom-call | flops 3355443200 | bytes 9830400 | tf_op jit(solution)/shard_map/pallas_call | solution.py:692
  156.6 3.0 shard_map.213
  161.0 3.7 %shard_map.214 = (bf16[512,1280]{1,0:T(8,128)(2,1)S(1)}, f32[4,64,1280]{2,1,0:T(8,128)S(1)}, bf16[160,512]{1,0:T(8,128)(2,1)S(1)}, bf16[160,512]{1,0:T(8,128)(2,...) custom-call(s32[3]{0:T(128)S(1)} %pad_add_fusion.ids, ...), custom_call_target="tpu_custom_call" | custom-call | flops 838860800 | bytes 9830400 | tf_op jit(solution)/shard_map/pallas_call | solution.py:717
  168.3 2.8 shard_map.215
  172.6 2.4 collective-permute-done.29.refs_3_
  178.5 4.1 %collective-permute-start.34 = (bf16[64,1280]{1,0:T(8,128)(2,1)S(1)}, bf16[64,1280]{1,0:T(8,128)(2,1)S(1)}, u32[]{:S(2)}, u32[]{:S(2)}) collective-permute-start(bf16[64,1280]{1,0:T(8,128)(2,1)S(1)} %get-tuple-element.327), channel_id=1, source_target_pairs={{0,16},{2,18},{4,20},{6,22},{8,24},{10,26},{12,28},{14,30},{16,0},... | collective-permute-start | bytes 491528 | tf_op jit(solution)/shard_map/ppermute | solution.py:582
  182.6 29.7 %shard_map.216 = (bf16[2048,768]{1,0:T(8,128)(2,1)S(1)}, bf16[4,4,64,1280]{3,2,1,0:T(8,128)(2,1)S(1)}, bf16[1280,512]{1,0:T(8,128)(2,1)S(1)}) custom-call(s32[3]{0:T(128)S(1)} %pad_add_fusion.ids, s32[4,8]{1,0:T(4,128)S(1)} %copy-done.52, bf16[2048,768]{1,0:T(8,128)(2,1)S(1)} %get-tuple-element.253.proj, f32[2,136,2048]{2,1,0:T(8,128)S(1)} %get-tuple-element.294.kept, ...), custom_call_target="tpu_custom_call" | custom-call | flops 5368709120 | bytes 10485760 | tf_op jit(solution)/shard_map/pallas_call | solution.py:745
  212.5 4.9 %collective-permute-done.35.other = bf16[4,4,64,1280]{3,2,1,0:T(8,128)(2,1)S(1)} collective-permute-done((bf16[4,4,64,1280]{3,2,1,0:T(8,128)(2,1)S(1)}, bf16[4,4,64,1280]{3,2,1,0:T(8,128)(2,1)S(1)}, u32[]{:S(2)}, u32[]{:S(2)}) %collective-permute-start.35) | collective-permute-done | bytes 2621472 | tf_op jit(solution)/shard_map/ppermute | solution.py:589
  217.4 2.7 shard_map.217
  222.8 4.8 %all-to-all-start.2 = ((bf16[4,320,512]{2,1,0:T(8,128)(2,1)}), bf16[4,320,512]{2,1,0:T(8,128)(2,1)S(1)}, u32[]{:S(2)}, u32[]{:S(2)}) async-start(bf16[4,320,512]{2,1,0:T(8,128)(2,1)} %bitcast.28), calls=%async_computation.2 | async-start | bytes 2621440 | tf_op jit(solution)/shard_map/all_to_all | solution.py:598
  231.1 3.8 %collective-permute-start.39 = (bf16[64,1280]{1,0:T(8,128)(2,1)}, bf16[64,1280]{1,0:T(8,128)(2,1)}, u32[]{:S(2)}, u32[]{:S(2)}) collective-permute-start(bf16[64,1280]{1,0:T(8,128)(2,1)} %copy-done.47), channel_id=1, source_target_pairs={{0,24},{2,26},{4,28},{6,30},{8,16},{10,18},{12,20},{14,22},{16,8},... | collective-permute-start | bytes 491528 | tf_op jit(solution)/shard_map/ppermute | solution.py:582
  239.7 5.8 %collective-permute-done.36.refs_4_ = bf16[4,64,1280]{2,1,0:T(8,128)(2,1)S(1)} collective-permute-done((bf16[4,64,1280]{2,1,0:T(8,128)(2,1)}, bf16[4,64,1280]{2,1,0:T(8,128)(2,1)S(1)}, u32[]{:S(2)}, u32[]{:S(2)}) %collective-permute-start.36) | collective-permute-done | bytes 655392 | tf_op jit(solution)/shard_map/ppermute | solution.py:582
  245.4 14.0 %collective-permute-done.37.refs_5_ = bf16[4,64,1280]{2,1,0:T(8,128)(2,1)S(1)} collective-permute-done((bf16[4,64,1280]{2,1,0:T(8,128)(2,1)}, bf16[4,64,1280]{2,1,0:T(8,128)(2,1)S(1)}, u32[]{:S(2)}, u32[]{:S(2)}) %collective-permute-start.37) | collective-permute-done | bytes 655392 | tf_op jit(solution)/shard_map/ppermute | solution.py:582
  263.7 4.6 %all-to-all-start.3 = ((bf16[4,80,1280]{2,1,0:T(8,128)(2,1)}), bf16[4,80,1280]{2,1,0:T(8,128)(2,1)S(1)}, u32[]{:S(2)}, u32[]{:S(2)}) async-start(bf16[4,80,1280]{2,1,0:T(8,128)(2,1)} %shard_map.218), calls=%async_computation.3 | async-start | bytes 1638400 | tf_op jit(solution)/shard_map/all_to_all | solution.py:598
  275.2 9.9 %collective-permute-done.40.refs_1_ = bf16[64,1280]{1,0:T(8,128)(2,1)S(1)} collective-permute-done((bf16[64,1280]{1,0:T(8,128)(2,1)S(1)}, bf16[64,1280]{1,0:T(8,128)(2,1)S(1)}, u32[]{:S(2)}, u32[]{:S(2)}) %collective-permute-start.40) | collective-permute-done | bytes 163872 | tf_op jit(solution)/shard_map/ppermute | solution.py:582
  285.1 4.1 %collective-permute-start.41 = (bf16[64,1280]{1,0:T(8,128)(2,1)}, bf16[64,1280]{1,0:T(8,128)(2,1)S(1)}, u32[]{:S(2)}, u32[]{:S(2)}) collective-permute-start(bf16[64,1280]{1,0:T(8,128)(2,1)} %get-tuple-element.375), channel_id=1, source_target_pairs={{0,16},{2,18},{4,20},{6,22},{8,24},{10,26},{12,28},{14,30},{16,0},... | collective-permute-start | bytes 491528 | tf_op jit(solution)/shard_map/ppermute | solution.py:582
  291.9 7.9 %collective-permute-done.41.refs_2_ = bf16[64,1280]{1,0:T(8,128)(2,1)S(1)} collective-permute-done((bf16[64,1280]{1,0:T(8,128)(2,1)}, bf16[64,1280]{1,0:T(8,128)(2,1)S(1)}, u32[]{:S(2)}, u32[]{:S(2)}) %collective-permute-start.41) | collective-permute-done | bytes 163872 | tf_op jit(solution)/shard_map/ppermute | solution.py:582
  304.3 3.3 %collective-permute-start.51 = (bf16[80,640]{1,0:T(8,128)(2,1)S(1)}, bf16[80,640]{1,0:T(8,128)(2,1)S(1)}, u32[]{:S(2)}, u32[]{:S(2)}) collective-permute-start(bf16[80,640]{1,0:T(8,128)(2,1)S(1)} %get-tuple-element.401), channel_id=1, source_target_pairs={{0,8},{2,10},{4,12},{6,14},{8,0},{10,2},{12,4},{14,6},{16,24},{18,... | collective-permute-start | bytes 307208 | tf_op jit(solution)/shard_map/ppermute | solution.py:582
  312.5 4.2 %collective-permute-done.52.refs_2_ = bf16[80,640]{1,0:T(8,128)(2,1)S(1)} collective-permute-done((bf16[80,640]{1,0:T(8,128)(2,1)S(1)}, bf16[80,640]{1,0:T(8,128)(2,1)S(1)}, u32[]{:S(2)}, u32[]{:S(2)}) %collective-permute-start.52) | collective-permute-done | bytes 102432 | tf_op jit(solution)/shard_map/ppermute | solution.py:582
  (259 shorter events, 96.8 us)
Async XLA Ops:
  5.8 15.0 %collective-permute-start.1 = (bf16[64,1280]{1,0:T(8,128)(2,1)S(1)}, bf16[64,1280]{1,0:T(8,128)(2,1)S(1)}, u32[]{:S(2)}, u32[]{:S(2)}) collective-permute-start(bf16[64,1280]{1,0:T(8,128)(2,1)S(1)} %get-tuple-element.218), channel_id=1, source_target_pairs={{0,16},{2,18},{4,20},{6,22},{8,24},{10,26},{12,28},{14,30},{16,0},... | collective-permute-start | bytes 491528 | tf_op jit(solution)/shard_map/ppermute | solution.py:582
  8.4 12.5 %collective-permute-start.2 = (bf16[64,1280]{1,0:T(8,128)(2,1)S(1)}, bf16[64,1280]{1,0:T(8,128)(2,1)S(1)}, u32[]{:S(2)}, u32[]{:S(2)}) collective-permute-start(bf16[64,1280]{1,0:T(8,128)(2,1)S(1)} %get-tuple-element.219), channel_id=1, source_target_pairs={{0,24},{2,26},{4,28},{6,30},{8,16},{10,18},{12,20},{14,22},{16,8},... | collective-permute-start | bytes 491528 | tf_op jit(solution)/shard_map/ppermute | solution.py:582
  20.9 41.3 %all-to-all-start = ((bf16[4,80,1920]{2,1,0:T(8,128)(2,1)}), bf16[4,80,1920]{2,1,0:T(8,128)(2,1)S(1)}, u32[]{:S(2)}, u32[]{:S(2)}) async-start(bf16[4,80,1920]{2,1,0:T(8,128)(2,1)} %shard_map.205), calls=%async_computation | async-start | bytes 2457600 | tf_op jit(solution)/shard_map/all_to_all | solution.py:598
  29.4 18.9 %collective-permute-start.3 = (bf16[4,64,1280]{2,1,0:T(8,128)(2,1)S(1)}, bf16[4,64,1280]{2,1,0:T(8,128)(2,1)S(1)}, u32[]{:S(2)}, u32[]{:S(2)}) collective-permute-start(bf16[4,64,1280]{2,1,0:T(8,128)(2,1)S(1)} %pad_maximum_fusion.2.refs_0_), channel_id=1, source_target_pairs={{0,2},{2,0},{4,6},{6,4},{8,10},{10,8},{12,14},{14,12},{16,18},{18,... | collective-permute-start | bytes 1966088 | tf_op jit(solution)/shard_map/ppermute | solution.py:582
  30.9 30.5 %collective-permute-start.4 = (bf16[4,64,1280]{2,1,0:T(8,128)(2,1)S(1)}, bf16[4,64,1280]{2,1,0:T(8,128)(2,1)S(1)}, u32[]{:S(2)}, u32[]{:S(2)}) collective-permute-start(bf16[4,64,1280]{2,1,0:T(8,128)(2,1)S(1)} %pad_maximum_fusion.2.refs_0_), channel_id=1, source_target_pairs={{0,4},{2,6},{4,0},{6,2},{8,12},{10,14},{12,8},{14,10},{16,20},{18,... | collective-permute-start | bytes 1966088 | tf_op jit(solution)/shard_map/ppermute | solution.py:582
  35.2 27.1 %collective-permute-start.8 = (bf16[4,64,1280]{2,1,0:T(8,128)(2,1)S(1)}, bf16[4,64,1280]{2,1,0:T(8,128)(2,1)}, u32[]{:S(2)}, u32[]{:S(2)}) collective-permute-start(bf16[4,64,1280]{2,1,0:T(8,128)(2,1)S(1)} %pad_maximum_fusion.2.refs_0_), channel_id=1, source_target_pairs={{0,6},{2,4},{4,2},{6,0},{8,14},{10,12},{12,10},{14,8},{16,22},{18,... | collective-permute-start | bytes 1966088 | tf_op jit(solution)/shard_map/ppermute | solution.py:582
  63.5 35.3 %all-to-all-start.1 = ((bf16[16,80,512]{2,1,0:T(8,128)(2,1)}), bf16[16,80,512]{2,1,0:T(8,128)(2,1)S(1)}, u32[]{:S(2)}, u32[]{:S(2)}) async-start(bf16[16,80,512]{2,1,0:T(8,128)(2,1)} %pad_maximum_fusion), calls=%async_computation.1 | async-start | bytes 2621440 | tf_op jit(solution)/shard_map/all_to_all | solution.py:598
  68.3 29.4 %collective-permute-start.13 = (bf16[4,80,1920]{2,1,0:T(8,128)(2,1)S(1)}, bf16[4,80,1920]{2,1,0:T(8,128)(2,1)S(1)}, u32[]{:S(2)}, u32[]{:S(2)}) collective-permute-start(bf16[4,80,1920]{2,1,0:T(8,128)(2,1)S(1)} %all-to-all-done.refs_0_), channel_id=1, source_target_pairs={{0,2},{2,0},{4,6},{6,4},{8,10},{10,8},{12,14},{14,12},{16,18},{18,... | collective-permute-start | bytes 3686408 | tf_op jit(solution)/shard_map/ppermute | solution.py:582
  68.3 30.5 %collective-permute-start.14 = (bf16[4,80,1920]{2,1,0:T(8,128)(2,1)S(1)}, bf16[4,80,1920]{2,1,0:T(8,128)(2,1)}, u32[]{:S(2)}, u32[]{:S(2)}) collective-permute-start(bf16[4,80,1920]{2,1,0:T(8,128)(2,1)S(1)} %all-to-all-done.refs_0_), channel_id=1, source_target_pairs={{0,4},{2,6},{4,0},{6,2},{8,12},{10,14},{12,8},{14,10},{16,20},{18,... | collective-permute-start | bytes 3686408 | tf_op jit(solution)/shard_map/ppermute | solution.py:582
  100.0 34.5 %collective-permute-start.15 = (bf16[2,80,1920]{2,1,0:T(8,128)(2,1)S(1)}, bf16[2,80,1920]{2,1,0:T(8,128)(2,1)S(1)}, u32[]{:S(2)}, u32[]{:S(2)}) collective-permute-start(bf16[2,80,1920]{2,1,0:T(8,128)(2,1)S(1)} %slice.15), channel_id=1, source_target_pairs={{0,2},{2,0},{4,6},{6,4},{8,10},{10,8},{12,14},{14,12},{16,18},{18,... | collective-permute-start | bytes 1843208 | tf_op jit(solution)/shard_map/ppermute | solution.py:582
  100.9 33.6 %collective-permute-start.16 = (bf16[2,80,1920]{2,1,0:T(8,128)(2,1)S(1)}, bf16[2,80,1920]{2,1,0:T(8,128)(2,1)S(1)}, u32[]{:S(2)}, u32[]{:S(2)}) collective-permute-start(bf16[2,80,1920]{2,1,0:T(8,128)(2,1)S(1)} %slice.16), channel_id=1, source_target_pairs={{0,4},{2,6},{4,0},{6,2},{8,12},{10,14},{12,8},{14,10},{16,20},{18,... | collective-permute-start | bytes 1843208 | tf_op jit(solution)/shard_map/ppermute | solution.py:582
  105.9 28.7 %collective-permute-start.17 = (bf16[64,1280]{1,0:T(8,128)(2,1)S(1)}, bf16[64,1280]{1,0:T(8,128)(2,1)S(1)}, u32[]{:S(2)}, u32[]{:S(2)}) collective-permute-start(bf16[64,1280]{1,0:T(8,128)(2,1)S(1)} %get-tuple-element.261), channel_id=1, source_target_pairs={{0,8},{2,10},{4,12},{6,14},{8,0},{10,2},{12,4},{14,6},{16,24},{18,... | collective-permute-start | bytes 491528 | tf_op jit(solution)/shard_map/ppermute | solution.py:582
  108.0 26.6 %collective-permute-start.18 = (bf16[64,1280]{1,0:T(8,128)(2,1)S(1)}, bf16[64,1280]{1,0:T(8,128)(2,1)S(1)}, u32[]{:S(2)}, u32[]{:S(2)}) collective-permute-start(bf16[64,1280]{1,0:T(8,128)(2,1)S(1)} %get-tuple-element.262), channel_id=1, source_target_pairs={{0,16},{2,18},{4,20},{6,22},{8,24},{10,26},{12,28},{14,30},{16,0},... | collective-permute-start | bytes 491528 | tf_op jit(solution)/shard_map/ppermute | solution.py:582
  110.4 24.3 %collective-permute-start.19 = (bf16[64,1280]{1,0:T(8,128)(2,1)S(1)}, bf16[64,1280]{1,0:T(8,128)(2,1)S(1)}, u32[]{:S(2)}, u32[]{:S(2)}) collective-permute-start(bf16[64,1280]{1,0:T(8,128)(2,1)S(1)} %get-tuple-element.263), channel_id=1, source_target_pairs={{0,24},{2,26},{4,28},{6,30},{8,16},{10,18},{12,20},{14,22},{16,8},... | collective-permute-start | bytes 491528 | tf_op jit(solution)/shard_map/ppermute | solution.py:582
  175.0 37.3 %collective-permute-start.30 = (bf16[4,80,1280]{2,1,0:T(8,128)(2,1)S(1)}, bf16[4,80,1280]{2,1,0:T(8,128)(2,1)S(1)}, u32[]{:S(2)}, u32[]{:S(2)}) collective-permute-start(bf16[4,80,1280]{2,1,0:T(8,128)(2,1)S(1)} %get-tuple-element.323), channel_id=1, source_target_pairs={{0,2},{2,0},{4,6},{6,4},{8,10},{10,8},{12,14},{14,12},{16,18},{18,... | collective-permute-start | bytes 2457608 | tf_op jit(solution)/shard_map/ppermute | solution.py:582
  176.3 36.1 %collective-permute-start.31 = (bf16[4,80,1280]{2,1,0:T(8,128)(2,1)S(1)}, bf16[4,80,1280]{2,1,0:T(8,128)(2,1)S(1)}, u32[]{:S(2)}, u32[]{:S(2)}) collective-permute-start(bf16[4,80,1280]{2,1,0:T(8,128)(2,1)S(1)} %get-tuple-element.324), channel_id=1, source_target_pairs={{0,4},{2,6},{4,0},{6,2},{8,12},{10,14},{12,8},{14,10},{16,20},{18,... | collective-permute-start | bytes 2457608 | tf_op jit(solution)/shard_map/ppermute | solution.py:582
  177.3 35.1 %collective-permute-start.32 = (bf16[4,80,1280]{2,1,0:T(8,128)(2,1)S(1)}, bf16[4,80,1280]{2,1,0:T(8,128)(2,1)S(1)}, u32[]{:S(2)}, u32[]{:S(2)}) collective-permute-start(bf16[4,80,1280]{2,1,0:T(8,128)(2,1)S(1)} %get-tuple-element.325), channel_id=1, source_target_pairs={{0,6},{2,4},{4,2},{6,0},{8,14},{10,12},{12,10},{14,8},{16,22},{18,... | collective-permute-start | bytes 2457608 | tf_op jit(solution)/shard_map/ppermute | solution.py:582
  178.5 33.8 %collective-permute-start.33 = (bf16[64,1280]{1,0:T(8,128)(2,1)S(1)}, bf16[64,1280]{1,0:T(8,128)(2,1)S(1)}, u32[]{:S(2)}, u32[]{:S(2)}) collective-permute-start(bf16[64,1280]{1,0:T(8,128)(2,1)S(1)} %get-tuple-element.326), channel_id=1, source_target_pairs={{0,8},{2,10},{4,12},{6,14},{8,0},{10,2},{12,4},{14,6},{16,24},{18,... | collective-permute-start | bytes 491528 | tf_op jit(solution)/shard_map/ppermute | solution.py:582
  178.5 33.8 %collective-permute-start.34 = (bf16[64,1280]{1,0:T(8,128)(2,1)S(1)}, bf16[64,1280]{1,0:T(8,128)(2,1)S(1)}, u32[]{:S(2)}, u32[]{:S(2)}) collective-permute-start(bf16[64,1280]{1,0:T(8,128)(2,1)S(1)} %get-tuple-element.327), channel_id=1, source_target_pairs={{0,16},{2,18},{4,20},{6,22},{8,24},{10,26},{12,28},{14,30},{16,0},... | collective-permute-start | bytes 491528 | tf_op jit(solution)/shard_map/ppermute | solution.py:582
  222.8 40.9 %all-to-all-start.2 = ((bf16[4,320,512]{2,1,0:T(8,128)(2,1)}), bf16[4,320,512]{2,1,0:T(8,128)(2,1)S(1)}, u32[]{:S(2)}, u32[]{:S(2)}) async-start(bf16[4,320,512]{2,1,0:T(8,128)(2,1)} %bitcast.28), calls=%async_computation.2 | async-start | bytes 2621440 | tf_op jit(solution)/shard_map/all_to_all | solution.py:598
  227.6 17.8 %collective-permute-start.36 = (bf16[4,64,1280]{2,1,0:T(8,128)(2,1)}, bf16[4,64,1280]{2,1,0:T(8,128)(2,1)S(1)}, u32[]{:S(2)}, u32[]{:S(2)}) collective-permute-start(bf16[4,64,1280]{2,1,0:T(8,128)(2,1)} %copy-done.44), channel_id=1, source_target_pairs={{0,2},{2,0},{4,6},{6,4},{8,10},{10,8},{12,14},{14,12},{16,18},{18,... | collective-permute-start | bytes 1966088 | tf_op jit(solution)/shard_map/ppermute | solution.py:582
  228.9 30.5 %collective-permute-start.37 = (bf16[4,64,1280]{2,1,0:T(8,128)(2,1)}, bf16[4,64,1280]{2,1,0:T(8,128)(2,1)S(1)}, u32[]{:S(2)}, u32[]{:S(2)}) collective-permute-start(bf16[4,64,1280]{2,1,0:T(8,128)(2,1)} %copy-done.43), channel_id=1, source_target_pairs={{0,4},{2,6},{4,0},{6,2},{8,12},{10,14},{12,8},{14,10},{16,20},{18,... | collective-permute-start | bytes 1966088 | tf_op jit(solution)/shard_map/ppermute | solution.py:582
  229.9 29.5 %collective-permute-start.38 = (bf16[4,64,1280]{2,1,0:T(8,128)(2,1)}, bf16[4,64,1280]{2,1,0:T(8,128)(2,1)S(1)}, u32[]{:S(2)}, u32[]{:S(2)}) collective-permute-start(bf16[4,64,1280]{2,1,0:T(8,128)(2,1)} %copy-done.42), channel_id=1, source_target_pairs={{0,6},{2,4},{4,2},{6,0},{8,14},{10,12},{12,10},{14,8},{16,22},{18,... | collective-permute-start | bytes 1966088 | tf_op jit(solution)/shard_map/ppermute | solution.py:582
  231.1 32.3 %collective-permute-start.39 = (bf16[64,1280]{1,0:T(8,128)(2,1)}, bf16[64,1280]{1,0:T(8,128)(2,1)}, u32[]{:S(2)}, u32[]{:S(2)}) collective-permute-start(bf16[64,1280]{1,0:T(8,128)(2,1)} %copy-done.47), channel_id=1, source_target_pairs={{0,24},{2,26},{4,28},{6,30},{8,16},{10,18},{12,20},{14,22},{16,8},... | collective-permute-start | bytes 491528 | tf_op jit(solution)/shard_map/ppermute | solution.py:582
  263.7 52.9 %all-to-all-start.3 = ((bf16[4,80,1280]{2,1,0:T(8,128)(2,1)}), bf16[4,80,1280]{2,1,0:T(8,128)(2,1)S(1)}, u32[]{:S(2)}, u32[]{:S(2)}) async-start(bf16[4,80,1280]{2,1,0:T(8,128)(2,1)} %shard_map.218), calls=%async_computation.3 | async-start | bytes 1638400 | tf_op jit(solution)/shard_map/all_to_all | solution.py:598
  269.4 19.8 %collective-permute-start.43 = (bf16[4,64,1280]{2,1,0:T(8,128)(2,1)S(1)}, bf16[4,64,1280]{2,1,0:T(8,128)(2,1)S(1)}, u32[]{:S(2)}, u32[]{:S(2)}) collective-permute-start(bf16[4,64,1280]{2,1,0:T(8,128)(2,1)S(1)} %pad_maximum_fusion.4.own), channel_id=1, source_target_pairs={{0,1},{1,0},{2,3},{3,2},{4,5},{5,4},{6,7},{7,6},{8,9},{9,8},{10,11... | collective-permute-start | bytes 1966088 | tf_op jit(solution)/shard_map/ppermute | solution.py:589
  269.5 30.3 %collective-permute-start.44 = (bf16[4,80,640]{2,1,0:T(8,128)(2,1)}, bf16[4,80,640]{2,1,0:T(8,128)(2,1)S(1)}, u32[]{:S(2)}, u32[]{:S(2)}) collective-permute-start(bf16[4,80,640]{2,1,0:T(8,128)(2,1)} %get-tuple-element.387), channel_id=1, source_target_pairs={{0,2},{2,0},{4,6},{6,4},{8,10},{10,8},{12,14},{14,12},{16,18},{18,... | collective-permute-start | bytes 1228808 | tf_op jit(solution)/shard_map/ppermute | solution.py:582
  270.8 29.0 %collective-permute-start.45 = (bf16[4,80,640]{2,1,0:T(8,128)(2,1)}, bf16[4,80,640]{2,1,0:T(8,128)(2,1)S(1)}, u32[]{:S(2)}, u32[]{:S(2)}) collective-permute-start(bf16[4,80,640]{2,1,0:T(8,128)(2,1)} %get-tuple-element.388), channel_id=1, source_target_pairs={{0,4},{2,6},{4,0},{6,2},{8,12},{10,14},{12,8},{14,10},{16,20},{18,... | collective-permute-start | bytes 1228808 | tf_op jit(solution)/shard_map/ppermute | solution.py:582
  271.9 27.9 %collective-permute-start.46 = (bf16[4,80,640]{2,1,0:T(8,128)(2,1)S(1)}, bf16[4,80,640]{2,1,0:T(8,128)(2,1)S(1)}, u32[]{:S(2)}, u32[]{:S(2)}) collective-permute-start(bf16[4,80,640]{2,1,0:T(8,128)(2,1)S(1)} %copy-done.46), channel_id=1, source_target_pairs={{0,6},{2,4},{4,2},{6,0},{8,14},{10,12},{12,10},{14,8},{16,22},{18,... | collective-permute-start | bytes 1228808 | tf_op jit(solution)/shard_map/ppermute | solution.py:582
  273.0 12.1 %collective-permute-start.40 = (bf16[64,1280]{1,0:T(8,128)(2,1)S(1)}, bf16[64,1280]{1,0:T(8,128)(2,1)S(1)}, u32[]{:S(2)}, u32[]{:S(2)}) collective-permute-start(bf16[64,1280]{1,0:T(8,128)(2,1)S(1)} %copy-done.51), channel_id=1, source_target_pairs={{0,8},{2,10},{4,12},{6,14},{8,0},{10,2},{12,4},{14,6},{16,24},{18,... | collective-permute-start | bytes 491528 | tf_op jit(solution)/shard_map/ppermute | solution.py:582
  285.1 14.7 %collective-permute-start.41 = (bf16[64,1280]{1,0:T(8,128)(2,1)}, bf16[64,1280]{1,0:T(8,128)(2,1)S(1)}, u32[]{:S(2)}, u32[]{:S(2)}) collective-permute-start(bf16[64,1280]{1,0:T(8,128)(2,1)} %get-tuple-element.375), channel_id=1, source_target_pairs={{0,16},{2,18},{4,20},{6,22},{8,24},{10,26},{12,28},{14,30},{16,0},... | collective-permute-start | bytes 491528 | tf_op jit(solution)/shard_map/ppermute | solution.py:582
  289.2 10.6 %collective-permute-start.42 = (bf16[64,1280]{1,0:T(8,128)(2,1)S(1)}, bf16[64,1280]{1,0:T(8,128)(2,1)S(1)}, u32[]{:S(2)}, u32[]{:S(2)}) collective-permute-start(bf16[64,1280]{1,0:T(8,128)(2,1)S(1)} %copy-done.49), channel_id=1, source_target_pairs={{0,24},{2,26},{4,28},{6,30},{8,16},{10,18},{12,20},{14,22},{16,8},... | collective-permute-start | bytes 491528 | tf_op jit(solution)/shard_map/ppermute | solution.py:582
  (91 other events, 663.7 us)

commit v2 on v1

--- a/solution.py
+++ b/solution.py
@@ -269,7 +269,9 @@
 
 def attend_back_kernel(heads, size, members, bq, bk, ids, lengths, proj, kept, scale, w, normed, *refs):
     pieces = refs[:members]
-    grads, there, weights, dot_, do_, kt, dqt, delta, doc, rows_ref, full = refs[members:]
+    grads, there = refs[members : members + 2]
+    weights, refs = refs[members + 2 : -9], refs[-9:]
+    dot_, do_, kt, dqt, delta, doc, rows_ref, full, padless = refs
     stream = proj.shape[0]
     groups = pieces[0].shape[1] // LANES
     z, j = ids[0], ids[1]
@@ -343,7 +345,10 @@
     lax.fori_loop(0, members, one_member, 0)
     total = jnp.broadcast_to(total / scale[...], (LANES, LANES)).T
     full[...] = tn(normed[...], grads[...])
-    store_weights(heads, size, groups * members, total, full, weights)
+    store_weights(heads, size, groups * members, total, full, padless)
+    rows = weights[0].shape[0]
+    for kz in range(groups):
+        weights[kz][...] = padless[at((z ^ kz) * rows, rows, 16), :]
 
 
 def out_kernel(ids, *refs):
@@ -472,13 +477,13 @@
     for g in range(1, parts.shape[0]):
         total = total + parts[g].astype(F32)
     grad_up[...] = total[:, :cols]
-    grad_down[...] = total[:, cols:].T
+    grad_down[...] = total[:, cols:]
     term = jnp.sum(total[:, :cols] * up[...].astype(F32), axis=1, keepdims=True)
     gain[...] = jnp.broadcast_to(term, gain.shape)
     total = outs[0][...].astype(F32)
     for part in outs[1:]:
         total = total + part[...].astype(F32)
-    grad_out[...] = total.T
+    grad_out[...] = total
 
 
 def input_rows(ids, grads, rows_ref, kj, which, members, half):
@@ -497,11 +502,11 @@
         out[kj][...] = y.reshape(groups, half, width).astype(BF)
 
 
-def qkv_sum_kernel(ids, parts, *refs):
-    out, tmp = refs[:-1], refs[-1]
-    total = parts[0].astype(F32)
-    for g in range(1, parts.shape[0]):
-        total = total + parts[g].astype(F32)
+def qkv_sum_kernel(groups, ids, *refs):
+    parts, out, tmp = refs[:groups], refs[groups:-1], refs[-1]
+    total = parts[0][...].astype(F32)
+    for part in parts[1:]:
+        total = total + part[...].astype(F32)
     tmp[...] = total
     rows = out[0].shape[0]
     for kj in range(len(out)):
@@ -737,18 +742,21 @@
         flops=2 * rows * local * width,
         moved=local * width * 4,
     )(ids, hidden_low, ob_t)
-    do_pieces, out_grads, out_parts, feed_grads = tie(do_pieces, out_grads, out_parts, feed_grads)
+    out_own = [across(part, members) if kz == 1 else part for kz, part in enumerate(out_parts)]
+    do_pieces, out_grads, out_own, feed_grads = tie(do_pieces, out_grads, out_own, feed_grads)
 
     feed_grads = to_members(feed_grads)
-    out_own = to_groups(out_parts)
-
-    grads, there, qkv_parts = call(
+    out_own = [
+        across(part, kz * members) if kz > 1 else part for kz, part in enumerate(out_own)
+    ]
+
+    grads, there, *qkv_parts = call(
         functools.partial(attend_back_kernel, heads, size, members, bq, bk),
         (
             struct((stream, padded), BF),
             struct((members, groups, half, width), BF),
-            struct((width, WIDE), BF),
-        ),
+        )
+        + (struct((width // groups, WIDE), BF),) * groups,
         "ssvvvvv" + "v" * members,
         scratch=[
             pltpu.VMEM((heads, LANES, stream), BF),
@@ -759,15 +767,18 @@
             pltpu.VMEM((8, stream), jnp.int32),
             pltpu.VMEM((groups * half, padded), BF),
             pltpu.VMEM((width, padded), F32),
+            pltpu.VMEM((width, WIDE), BF),
         ],
         flops=5 * stream * stream * LANES * heads,
         moved=stream * LANES * heads * 20,
     )(ids, doc_lengths, proj, kept, scale_row, w_qkv_t, normed, *do_pieces)
-    there, grads, qkv_parts, feed_grads, out_own[1], out_own[2], out_grads = tie(
-        there, grads, qkv_parts, feed_grads, out_own[1], out_own[2], out_grads
+    there, grads, qkv_parts, feed_grads, out_own, out_grads = tie(
+        there, grads, qkv_parts, feed_grads, out_own, out_grads
     )
 
     there = swap(there)
+    out_own = jnp.stack(out_own)
+    out_other = swap(out_own)
     here = call(
         input_here_kernel,
         (struct((groups, half, width), BF),) * members,
@@ -776,38 +787,44 @@
         flops=stream * width * padded,
         moved=stream * width * 2,
     )(ids, grads, w_qkv_t, there)
-    here, feed_grads, qkv_parts = tie(here, feed_grads, qkv_parts)
+    qkv_parts = [
+        across(part, members) if kz == 1 else part for kz, part in enumerate(qkv_parts)
+    ]
+    here, feed_grads, qkv_parts, out_own, out_other = tie(
+        here, feed_grads, qkv_parts, out_own, out_other
+    )
+    layer_out = assemble(ids, out_own, out_other, BF)
     sums = to_members(here)
-    qkv_parts = exchange(qkv_parts, lines).reshape(groups, width // groups, WIDE)
+    qkv_parts = [
+        across(part, kz * members) if kz > 1 else part for kz, part in enumerate(qkv_parts)
+    ]
     feed_grads = call(
         sum_members_kernel,
         struct((groups, shard, 2 * local), BF),
         "v" * members,
         moved=groups * shard * local * 24,
     )(*feed_grads)
-    sums, feed_grads, out_grads = tie(sums, feed_grads, out_grads)
+    sums, feed_grads, out_grads, qkv_parts, layer_out = tie(
+        sums, feed_grads, out_grads, qkv_parts, layer_out
+    )
     grad_x = call(
         functools.partial(tokens_kernel, groups),
         (struct((half, width), BF),) * groups,
         "svvv" + "v" * len(sums),
         moved=groups * half * width * 12,
     )(ids, pieces[0], dh_half, gains, *sums)
-    grad_x, qkv_parts, out_own, feed_grads, out_grads = tie(
-        grad_x, qkv_parts, out_own, feed_grads, out_grads
-    )
+    grad_x, qkv_parts, feed_grads, out_grads = tie(grad_x, qkv_parts, feed_grads, out_grads)
     feed_grads = exchange(feed_grads, lines)
     gx_own = to_groups(grad_x)
     out_grads = to_members(out_grads)
-    out_own = jnp.stack(out_own)
-    layer_out = assemble(ids, out_own, swap(out_own), BF)
     qkv_parts = call(
-        qkv_sum_kernel,
+        functools.partial(qkv_sum_kernel, groups),
         (struct((shard, WIDE), BF),) * members,
-        "sv",
+        "s" + "v" * groups,
         scratch=[pltpu.VMEM((width // groups, WIDE), F32)],
         moved=width * WIDE * 4,
-    )(ids, qkv_parts)
-    gx_own, qkv_parts, layer_out, out_grads = tie(gx_own, qkv_parts, layer_out, out_grads)
+    )(ids, *qkv_parts)
+    gx_own, qkv_parts, out_grads = tie(gx_own, qkv_parts, out_grads)
     qkv_parts = to_members(qkv_parts)
     out_grads = call(
         functools.partial(sum_split_kernel, members),
@@ -820,9 +837,7 @@
     gx_other = [swap(piece) for piece in gx_own]
     grad_up, grad_down, grad_out, gain_two = call(
         functools.partial(rows_kernel, groups),
-        (struct((shard, local), F32),)
-        + (struct((local, shard), F32),) * 2
-        + (struct((shard, LANES), F32),),
+        (struct((shard, local), F32),) * 3 + (struct((shard, LANES), F32),),
         "v" * (groups + 2),
         moved=shard * local * 36,
     )(feed_grads, w_up, *out_grads)
@@ -849,9 +864,9 @@
         grad_q,
         grad_k,
         grad_v,
-        grad_out,
+        grad_out.T,
         grad_up,
-        grad_down,
+        grad_down.T,
         small[:, 0] / gain_attn.astype(F32),
         small[:, 2] / gain_mlp.astype(F32),
         small[:size, 1],

time: 324 us -> 319 us (0.985)
  local copies, waits for them, and re-layouts: 22.4 us -> 13 us
  waiting for transfers between devices: 121 us -> 129 us
    unnamed x124 -> x64, local copies, waits for them, and re-layouts: 20.3 us -> 9.73 us
    ppermute x43 -> x46, waiting for transfers between devices: 110 us -> 119 us  [across(): return lax.ppermute(a, 'ctx', [(i, i ^ mask) for i in range(count)])]
    all_to_all x4 -> x3, starting transfers between devices: 19.2 us -> 15.4 us  [exchange(): return lax.all_to_all(a, 'ctx', 0, 0, axis_index_groups=teams, tiled=True)]
    ppermute x43 -> x46, starting transfers between devices: 62 us -> 64.2 us  [across(): return lax.ppermute(a, 'ctx', [(i, i ^ mask) for i in range(count)])]
  transfers between devices with their start and end apart: 62 -> 64, of which waited for: 23 -> 27; matrix products, arithmetic and copies ran while one was open for 1% -> 1% of each run, Pallas kernels for 23% -> 23%
where the time goes in v2:
time: 319 us
  waiting for transfers between devices  129 us (40%)
  Pallas kernels  90.9 us (28%)
  starting transfers between devices  83.1 us (26%)
  local copies, waits for them, and re-layouts  13 us (4%)
    ppermute x46, waiting for transfers between devices, across(): return lax.ppermute(a, 'ctx', [(i, i ^ mask) for i in range(count)])  119 us
    ppermute x46, starting transfers between devices, across(): return lax.ppermute(a, 'ctx', [(i, i ^ mask) for i in range(count)])  64.2 us
    pallas_call x1, Pallas kernels, stream_per_group(): call(functools.partial(attend_back_kernel, heads, size, members, bq, bk),...  29.7 us
    pallas_call x1, Pallas kernels, stream_per_group(): call(functools.partial(attend_kernel, heads, size, members, bq, bk), (str...  15.5 us
    all_to_all x3, starting transfers between devices, exchange(): return lax.all_to_all(a, 'ctx', 0, 0, axis_index_groups=teams, tiled=True)  15.4 us
    ppermute x15, waiting for transfers between devices, swap(): return lax.ppermute(a, 'tp', [(0, 1), (1, 0)])  9.93 us
    unnamed x64, local copies, waits for them, and re-layouts  9.73 us
    pallas_call x1, Pallas kernels, stream_per_group(): call(functools.partial(project_kernel, members, 512), (struct((stream, pa...  7.25 us
  transfers between devices with their start and end apart: 64, of which 27 were waited for; matrix products, arithmetic and copies ran while one was open for 1% of the time, Pallas kernels for 23%

profile of v2, /device:TPU:0, one launch (start us, length us, event | category | flops | bytes accessed | tf_op | source)
XLA Modules:
  0.0 319.0 jit_solution(13538598204530953869)
XLA Ops:
  2.7 5.1 %collective-permute-start.2 = (bf16[64,1280]{1,0:T(8,128)(2,1)S(1)}, bf16[64,1280]{1,0:T(8,128)(2,1)S(1)}, u32[]{:S(2)}, u32[]{:S(2)}) collective-permute-start(bf16[64,1280]{1,0:T(8,128)(2,1)S(1)} %get-tuple-element.235), channel_id=1, source_target_pairs={{0,24},{2,26},{4,28},{6,30},{8,16},{10,18},{12,20},{14,22},{16,8},... | collective-permute-start | bytes 491528 | tf_op jit(solution)/shard_map/ppermute | solution.py:587
  10.5 2.5 collective-permute-done.2
  13.0 8.8 %collective-permute-done.1 = bf16[64,1280]{1,0:T(8,128)(2,1)S(1)} collective-permute-done((bf16[64,1280]{1,0:T(8,128)(2,1)S(1)}, bf16[64,1280]{1,0:T(8,128)(2,1)S(1)}, u32[]{:S(2)}, u32[]{:S(2)}) %collective-permute-start.1) | collective-permute-done | bytes 163872 | tf_op jit(solution)/shard_map/ppermute | solution.py:587
  21.8 3.8 %all-to-all-start = ((bf16[4,80,1920]{2,1,0:T(8,128)(2,1)}), bf16[4,80,1920]{2,1,0:T(8,128)(2,1)S(1)}, u32[]{:S(2)}, u32[]{:S(2)}) async-start(bf16[4,80,1920]{2,1,0:T(8,128)(2,1)} %shard_map.205), calls=%async_computation | async-start | bytes 2457600 | tf_op jit(solution)/shard_map/all_to_all | solution.py:603
  35.4 12.6 %collective-permute-done.3.refs_1_ = bf16[4,64,1280]{2,1,0:T(8,128)(2,1)S(1)} collective-permute-done((bf16[4,64,1280]{2,1,0:T(8,128)(2,1)S(1)}, bf16[4,64,1280]{2,1,0:T(8,128)(2,1)S(1)}, u32[]{:S(2)}, u32[]{:S(2)}) %collective-permute-start.3) | collective-permute-done | bytes 655392 | tf_op jit(solution)/shard_map/ppermute | solution.py:587
  47.9 13.3 %collective-permute-done.4.refs_2_ = bf16[4,64,1280]{2,1,0:T(8,128)(2,1)S(1)} collective-permute-done((bf16[4,64,1280]{2,1,0:T(8,128)(2,1)S(1)}, bf16[4,64,1280]{2,1,0:T(8,128)(2,1)S(1)}, u32[]{:S(2)}, u32[]{:S(2)}) %collective-permute-start.4) | collective-permute-done | bytes 655392 | tf_op jit(solution)/shard_map/ppermute | solution.py:587
  63.3 5.1 %all-to-all-start.1 = ((bf16[16,80,512]{2,1,0:T(8,128)(2,1)}), bf16[16,80,512]{2,1,0:T(8,128)(2,1)S(1)}, u32[]{:S(2)}, u32[]{:S(2)}) async-start(bf16[16,80,512]{2,1,0:T(8,128)(2,1)} %pad_maximum_fusion), calls=%async_computation.1 | async-start | bytes 2621440 | tf_op jit(solution)/shard_map/all_to_all | solution.py:603
  74.9 23.0 %collective-permute-done.13.refs_1_ = bf16[4,80,1920]{2,1,0:T(8,128)(2,1)S(1)} collective-permute-done((bf16[4,80,1920]{2,1,0:T(8,128)(2,1)S(1)}, bf16[4,80,1920]{2,1,0:T(8,128)(2,1)S(1)}, u32[]{:S(2)}, u32[]{:S(2)}) %collective-permute-start.13) | collective-permute-done | bytes 1228832 | tf_op jit(solution)/shard_map/ppermute | solution.py:587
  108.0 2.4 collective-permute-start.18
  111.5 7.3 %shard_map.208 = (bf16[2048,768]{1,0:T(8,128)(2,1)S(1)}, bf16[2048,1280]{1,0:T(8,128)(2,1)S(1)}) custom-call(s32[3]{0:T(128)S(1)} %pad_add_fusion.ids, bf16[4,64,1280]{2,1,0:T(8,128)(2,1)S(1)} %pad_maximum_fusion.2.refs_0_, bf16[4,64,1280]{2,1,0:T(8,128)(2,1)S(1)} %copy-done.16, bf16[4,64,1280]{2,1,0:T(8,128)(2,1)S(1)} %copy-done.18, ...), custom_call_target="tpu_custom_call" | custom-call | flops 4026531840 | bytes 10485760 | tf_op jit(solution)/shard_map/pallas_call | solution.py:658
  118.8 15.5 %shard_map.209 = (bf16[160,512]{1,0:T(8,128)(2,1)S(1)}, bf16[160,512]{1,0:T(8,128)(2,1)S(1)}, bf16[160,512]{1,0:T(8,128)(2,1)S(1)}, bf16[160,512]{1,0:T(8,128)(2,1)S(1)}, f32[2,136,2048]{2,1,0:T(8,128)S(1)}) custom-call(s32[3]{0:T(128)S(1)} %pad_add_fusion.ids, s32[4,8]{1,0:T(4,128)S(1)} %copy-done.28, bf16[2048,768]{1,0:T(8,128)(2,1)S(1)} %get-tuple-element.269.proj), custom_call_target="tpu_custom_call" | custom-call | flops 2147483648 | bytes 5242880 | tf_op jit(solution)/shard_map/pallas_call | solution.py:667
  141.5 2.6 collective-permute-done.22.refs_2_
  146.6 3.3 %collective-permute-done.20.refs_3_ = bf16[4,64,1280]{2,1,0:T(8,128)(2,1)S(1)} collective-permute-done((bf16[4,64,1280]{2,1,0:T(8,128)(2,1)S(1)}, bf16[4,64,1280]{2,1,0:T(8,128)(2,1)S(1)}, u32[]{:S(2)}, u32[]{:S(2)}) %collective-permute-start.20) | collective-permute-done | bytes 655392 | tf_op jit(solution)/shard_map/ppermute | solution.py:594
  149.9 6.0 %shard_map.212 = (f32[512,1280]{1,0:T(8,128)S(1)}, bf16[512,1280]{1,0:T(8,128)(2,1)S(1)}, bf16[512,640]{1,0:T(8,128)(2,1)S(1)}, bf16[512,640]{1,0:T(8,128)(2,1)S...) custom-call(s32[3]{0:T(128)S(1)} %pad_add_fusion.ids, ...), custom_call_target="tpu_custom_call" | custom-call | flops 3355443200 | bytes 9830400 | tf_op jit(solution)/shard_map/pallas_call | solution.py:697
  156.5 3.0 shard_map.213
  160.9 3.8 %shard_map.214 = (bf16[512,1280]{1,0:T(8,128)(2,1)S(1)}, f32[4,64,1280]{2,1,0:T(8,128)S(1)}, bf16[160,512]{1,0:T(8,128)(2,1)S(1)}, bf16[160,512]{1,0:T(8,128)(2,...) custom-call(s32[3]{0:T(128)S(1)} %pad_add_fusion.ids, ...), custom_call_target="tpu_custom_call" | custom-call | flops 838860800 | bytes 9830400 | tf_op jit(solution)/shard_map/pallas_call | solution.py:722
  169.0 2.9 shard_map.215
  172.0 2.9 collective-permute-done.29.refs_3_
  179.4 2.5 collective-permute-start.35
  181.9 29.7 %shard_map.216 = (bf16[2048,768]{1,0:T(8,128)(2,1)S(1)}, bf16[4,4,64,1280]{3,2,1,0:T(8,128)(2,1)S(1)}, bf16[320,512]{1,0:T(8,128)(2,1)S(1)}, bf16[320,512]{1,0:T...) custom-call(s32[3]{0:T(128)S(1)} %pad_add_fusion.ids, s32[4,8]{1,0:T(4,128)S(1)} %copy-done.28, ...), custom_call_target="tpu_custom_call" | custom-call | flops 5368709120 | bytes 10485760 | tf_op jit(solution)/shard_map/pallas_call | solution.py:753
  213.9 3.4 %collective-permute-done.36.other = bf16[4,4,64,1280]{3,2,1,0:T(8,128)(2,1)S(1)} collective-permute-done((bf16[4,4,64,1280]{3,2,1,0:T(8,128)(2,1)S(1)}, bf16[4,4,64,1280]{3,2,1,0:T(8,128)(2,1)S(1)}, u32[]{:S(2)}, u32[]{:S(2)}) %collective-permute-start.36) | collective-permute-done | bytes 2621472 | tf_op jit(solution)/shard_map/ppermute | solution.py:594
  217.3 2.8 shard_map.217
  220.1 2.6 collective-permute-done.37.refs_1_
  232.7 17.5 %collective-permute-done.42.refs_2_ = bf16[320,512]{1,0:T(8,128)(2,1)S(1)} collective-permute-done((bf16[320,512]{1,0:T(8,128)(2,1)S(1)}, bf16[320,512]{1,0:T(8,128)(2,1)S(1)}, u32[]{:S(2)}, u32[]{:S(2)}) %collective-permute-start.42) | collective-permute-done | bytes 327712 | tf_op jit(solution)/shard_map/ppermute | solution.py:587
  250.2 3.5 %collective-permute-done.40.refs_5_ = bf16[4,64,1280]{2,1,0:T(8,128)(2,1)S(1)} collective-permute-done((bf16[4,64,1280]{2,1,0:T(8,128)(2,1)S(1)}, bf16[4,64,1280]{2,1,0:T(8,128)(2,1)S(1)}, u32[]{:S(2)}, u32[]{:S(2)}) %collective-permute-start.40) | collective-permute-done | bytes 655392 | tf_op jit(solution)/shard_map/ppermute | solution.py:587
  257.6 6.6 %all-to-all-start.2 = ((bf16[4,80,1280]{2,1,0:T(8,128)(2,1)}), bf16[4,80,1280]{2,1,0:T(8,128)(2,1)S(1)}, u32[]{:S(2)}, u32[]{:S(2)}) async-start(bf16[4,80,1280]{2,1,0:T(8,128)(2,1)} %shard_map.218), calls=%async_computation.2 | async-start | bytes 1638400 | tf_op jit(solution)/shard_map/all_to_all | solution.py:603
  269.7 2.4 collective-permute-start.45
  272.1 10.1 %collective-permute-done.44.refs_1_ = bf16[64,1280]{1,0:T(8,128)(2,1)S(1)} collective-permute-done((bf16[64,1280]{1,0:T(8,128)(2,1)S(1)}, bf16[64,1280]{1,0:T(8,128)(2,1)S(1)}, u32[]{:S(2)}, u32[]{:S(2)}) %collective-permute-start.44) | collective-permute-done | bytes 163872 | tf_op jit(solution)/shard_map/ppermute | solution.py:587
  282.2 3.9 %collective-permute-start.46 = (bf16[64,1280]{1,0:T(8,128)(2,1)}, bf16[64,1280]{1,0:T(8,128)(2,1)S(1)}, u32[]{:S(2)}, u32[]{:S(2)}) collective-permute-start(bf16[64,1280]{1,0:T(8,128)(2,1)} %copy-done.25), channel_id=1, source_target_pairs={{0,24},{2,26},{4,28},{6,30},{8,16},{10,18},{12,20},{14,22},{16,8},... | collective-permute-start | bytes 491528 | tf_op jit(solution)/shard_map/ppermute | solution.py:587
  286.9 9.8 %collective-permute-done.45.refs_2_ = bf16[64,1280]{1,0:T(8,128)(2,1)S(1)} collective-permute-done((bf16[64,1280]{1,0:T(8,128)(2,1)}, bf16[64,1280]{1,0:T(8,128)(2,1)S(1)}, u32[]{:S(2)}, u32[]{:S(2)}) %collective-permute-start.45) | collective-permute-done | bytes 163872 | tf_op jit(solution)/shard_map/ppermute | solution.py:587
  299.0 3.1 collective-permute-start.54
  302.2 2.4 collective-permute-start.56
  (203 shorter events, 94.1 us)
Async XLA Ops:
  7.8 13.9 %collective-permute-start.1 = (bf16[64,1280]{1,0:T(8,128)(2,1)S(1)}, bf16[64,1280]{1,0:T(8,128)(2,1)S(1)}, u32[]{:S(2)}, u32[]{:S(2)}) collective-permute-start(bf16[64,1280]{1,0:T(8,128)(2,1)S(1)} %get-tuple-element.234), channel_id=1, source_target_pairs={{0,16},{2,18},{4,20},{6,22},{8,24},{10,26},{12,28},{14,30},{16,0},... | collective-permute-start | bytes 491528 | tf_op jit(solution)/shard_map/ppermute | solution.py:587
  7.8 13.9 %collective-permute-start = (bf16[64,1280]{1,0:T(8,128)(2,1)S(1)}, bf16[64,1280]{1,0:T(8,128)(2,1)S(1)}, u32[]{:S(2)}, u32[]{:S(2)}) collective-permute-start(bf16[64,1280]{1,0:T(8,128)(2,1)S(1)} %get-tuple-element.233), channel_id=1, source_target_pairs={{0,8},{2,10},{4,12},{6,14},{8,0},{10,2},{12,4},{14,6},{16,24},{18,... | collective-permute-start | bytes 491528 | tf_op jit(solution)/shard_map/ppermute | solution.py:587
  21.8 40.3 %all-to-all-start = ((bf16[4,80,1920]{2,1,0:T(8,128)(2,1)}), bf16[4,80,1920]{2,1,0:T(8,128)(2,1)S(1)}, u32[]{:S(2)}, u32[]{:S(2)}) async-start(bf16[4,80,1920]{2,1,0:T(8,128)(2,1)} %shard_map.205), calls=%async_computation | async-start | bytes 2457600 | tf_op jit(solution)/shard_map/all_to_all | solution.py:603
  29.1 18.9 %collective-permute-start.3 = (bf16[4,64,1280]{2,1,0:T(8,128)(2,1)S(1)}, bf16[4,64,1280]{2,1,0:T(8,128)(2,1)S(1)}, u32[]{:S(2)}, u32[]{:S(2)}) collective-permute-start(bf16[4,64,1280]{2,1,0:T(8,128)(2,1)S(1)} %pad_maximum_fusion.2.refs_0_), channel_id=1, source_target_pairs={{0,2},{2,0},{4,6},{6,4},{8,10},{10,8},{12,14},{14,12},{16,18},{18,... | collective-permute-start | bytes 1966088 | tf_op jit(solution)/shard_map/ppermute | solution.py:587
  30.5 30.7 %collective-permute-start.4 = (bf16[4,64,1280]{2,1,0:T(8,128)(2,1)S(1)}, bf16[4,64,1280]{2,1,0:T(8,128)(2,1)S(1)}, u32[]{:S(2)}, u32[]{:S(2)}) collective-permute-start(bf16[4,64,1280]{2,1,0:T(8,128)(2,1)S(1)} %pad_maximum_fusion.2.refs_0_), channel_id=1, source_target_pairs={{0,4},{2,6},{4,0},{6,2},{8,12},{10,14},{12,8},{14,10},{16,20},{18,... | collective-permute-start | bytes 1966088 | tf_op jit(solution)/shard_map/ppermute | solution.py:587
  34.9 27.2 %collective-permute-start.8 = (bf16[4,64,1280]{2,1,0:T(8,128)(2,1)S(1)}, bf16[4,64,1280]{2,1,0:T(8,128)(2,1)}, u32[]{:S(2)}, u32[]{:S(2)}) collective-permute-start(bf16[4,64,1280]{2,1,0:T(8,128)(2,1)S(1)} %pad_maximum_fusion.2.refs_0_), channel_id=1, source_target_pairs={{0,6},{2,4},{4,2},{6,0},{8,14},{10,12},{12,10},{14,8},{16,22},{18,... | collective-permute-start | bytes 1966088 | tf_op jit(solution)/shard_map/ppermute | solution.py:587
  63.3 35.5 %all-to-all-start.1 = ((bf16[16,80,512]{2,1,0:T(8,128)(2,1)}), bf16[16,80,512]{2,1,0:T(8,128)(2,1)S(1)}, u32[]{:S(2)}, u32[]{:S(2)}) async-start(bf16[16,80,512]{2,1,0:T(8,128)(2,1)} %pad_maximum_fusion), calls=%async_computation.1 | async-start | bytes 2621440 | tf_op jit(solution)/shard_map/all_to_all | solution.py:603
  68.4 29.4 %collective-permute-start.13 = (bf16[4,80,1920]{2,1,0:T(8,128)(2,1)S(1)}, bf16[4,80,1920]{2,1,0:T(8,128)(2,1)S(1)}, u32[]{:S(2)}, u32[]{:S(2)}) collective-permute-start(bf16[4,80,1920]{2,1,0:T(8,128)(2,1)S(1)} %all-to-all-done.refs_0_), channel_id=1, source_target_pairs={{0,2},{2,0},{4,6},{6,4},{8,10},{10,8},{12,14},{14,12},{16,18},{18,... | collective-permute-start | bytes 3686408 | tf_op jit(solution)/shard_map/ppermute | solution.py:587
  68.4 30.5 %collective-permute-start.14 = (bf16[4,80,1920]{2,1,0:T(8,128)(2,1)S(1)}, bf16[4,80,1920]{2,1,0:T(8,128)(2,1)}, u32[]{:S(2)}, u32[]{:S(2)}) collective-permute-start(bf16[4,80,1920]{2,1,0:T(8,128)(2,1)S(1)} %all-to-all-done.refs_0_), channel_id=1, source_target_pairs={{0,4},{2,6},{4,0},{6,2},{8,12},{10,14},{12,8},{14,10},{16,20},{18,... | collective-permute-start | bytes 3686408 | tf_op jit(solution)/shard_map/ppermute | solution.py:587
  100.1 34.2 %collective-permute-start.16 = (bf16[2,80,1920]{2,1,0:T(8,128)(2,1)S(1)}, bf16[2,80,1920]{2,1,0:T(8,128)(2,1)S(1)}, u32[]{:S(2)}, u32[]{:S(2)}) collective-permute-start(bf16[2,80,1920]{2,1,0:T(8,128)(2,1)S(1)} %slice.16), channel_id=1, source_target_pairs={{0,4},{2,6},{4,0},{6,2},{8,12},{10,14},{12,8},{14,10},{16,20},{18,... | collective-permute-start | bytes 1843208 | tf_op jit(solution)/shard_map/ppermute | solution.py:587
  102.4 31.9 %collective-permute-start.15 = (bf16[2,80,1920]{2,1,0:T(8,128)(2,1)S(1)}, bf16[2,80,1920]{2,1,0:T(8,128)(2,1)S(1)}, u32[]{:S(2)}, u32[]{:S(2)}) collective-permute-start(bf16[2,80,1920]{2,1,0:T(8,128)(2,1)S(1)} %slice.15), channel_id=1, source_target_pairs={{0,2},{2,0},{4,6},{6,4},{8,10},{10,8},{12,14},{14,12},{16,18},{18,... | collective-permute-start | bytes 1843208 | tf_op jit(solution)/shard_map/ppermute | solution.py:587
  105.9 28.6 %collective-permute-start.17 = (bf16[64,1280]{1,0:T(8,128)(2,1)S(1)}, bf16[64,1280]{1,0:T(8,128)(2,1)S(1)}, u32[]{:S(2)}, u32[]{:S(2)}) collective-permute-start(bf16[64,1280]{1,0:T(8,128)(2,1)S(1)} %get-tuple-element.280), channel_id=1, source_target_pairs={{0,8},{2,10},{4,12},{6,14},{8,0},{10,2},{12,4},{14,6},{16,24},{18,... | collective-permute-start | bytes 491528 | tf_op jit(solution)/shard_map/ppermute | solution.py:587
  108.0 26.5 %collective-permute-start.18 = (bf16[64,1280]{1,0:T(8,128)(2,1)S(1)}, bf16[64,1280]{1,0:T(8,128)(2,1)S(1)}, u32[]{:S(2)}, u32[]{:S(2)}) collective-permute-start(bf16[64,1280]{1,0:T(8,128)(2,1)S(1)} %get-tuple-element.281), channel_id=1, source_target_pairs={{0,16},{2,18},{4,20},{6,22},{8,24},{10,26},{12,28},{14,30},{16,0},... | collective-permute-start | bytes 491528 | tf_op jit(solution)/shard_map/ppermute | solution.py:587
  110.3 24.2 %collective-permute-start.19 = (bf16[64,1280]{1,0:T(8,128)(2,1)S(1)}, bf16[64,1280]{1,0:T(8,128)(2,1)S(1)}, u32[]{:S(2)}, u32[]{:S(2)}) collective-permute-start(bf16[64,1280]{1,0:T(8,128)(2,1)S(1)} %get-tuple-element.282), channel_id=1, source_target_pairs={{0,24},{2,26},{4,28},{6,30},{8,16},{10,18},{12,20},{14,22},{16,8},... | collective-permute-start | bytes 491528 | tf_op jit(solution)/shard_map/ppermute | solution.py:587
  174.9 36.7 %collective-permute-start.31 = (bf16[4,80,1280]{2,1,0:T(8,128)(2,1)S(1)}, bf16[4,80,1280]{2,1,0:T(8,128)(2,1)S(1)}, u32[]{:S(2)}, u32[]{:S(2)}) collective-permute-start(bf16[4,80,1280]{2,1,0:T(8,128)(2,1)S(1)} %get-tuple-element.341), channel_id=1, source_target_pairs={{0,2},{2,0},{4,6},{6,4},{8,10},{10,8},{12,14},{14,12},{16,18},{18,... | collective-permute-start | bytes 2457608 | tf_op jit(solution)/shard_map/ppermute | solution.py:587
  176.2 35.4 %collective-permute-start.32 = (bf16[4,80,1280]{2,1,0:T(8,128)(2,1)S(1)}, bf16[4,80,1280]{2,1,0:T(8,128)(2,1)S(1)}, u32[]{:S(2)}, u32[]{:S(2)}) collective-permute-start(bf16[4,80,1280]{2,1,0:T(8,128)(2,1)S(1)} %get-tuple-element.342), channel_id=1, source_target_pairs={{0,4},{2,6},{4,0},{6,2},{8,12},{10,14},{12,8},{14,10},{16,20},{18,... | collective-permute-start | bytes 2457608 | tf_op jit(solution)/shard_map/ppermute | solution.py:587
  177.3 35.1 %collective-permute-start.33 = (bf16[4,80,1280]{2,1,0:T(8,128)(2,1)S(1)}, bf16[4,80,1280]{2,1,0:T(8,128)(2,1)S(1)}, u32[]{:S(2)}, u32[]{:S(2)}) collective-permute-start(bf16[4,80,1280]{2,1,0:T(8,128)(2,1)S(1)} %get-tuple-element.343), channel_id=1, source_target_pairs={{0,6},{2,4},{4,2},{6,0},{8,14},{10,12},{12,10},{14,8},{16,22},{18,... | collective-permute-start | bytes 2457608 | tf_op jit(solution)/shard_map/ppermute | solution.py:587
  178.4 33.2 %collective-permute-start.34 = (bf16[64,1280]{1,0:T(8,128)(2,1)S(1)}, bf16[64,1280]{1,0:T(8,128)(2,1)S(1)}, u32[]{:S(2)}, u32[]{:S(2)}) collective-permute-start(bf16[64,1280]{1,0:T(8,128)(2,1)S(1)} %get-tuple-element.346), channel_id=1, source_target_pairs={{0,16},{2,18},{4,20},{6,22},{8,24},{10,26},{12,28},{14,30},{16,0},... | collective-permute-start | bytes 491528 | tf_op jit(solution)/shard_map/ppermute | solution.py:587
  179.4 32.2 %collective-permute-start.35 = (bf16[64,1280]{1,0:T(8,128)(2,1)S(1)}, bf16[64,1280]{1,0:T(8,128)(2,1)S(1)}, u32[]{:S(2)}, u32[]{:S(2)}) collective-permute-start(bf16[64,1280]{1,0:T(8,128)(2,1)S(1)} %get-tuple-element.347), channel_id=1, source_target_pairs={{0,24},{2,26},{4,28},{6,30},{8,16},{10,18},{12,20},{14,22},{16,8},... | collective-permute-start | bytes 491528 | tf_op jit(solution)/shard_map/ppermute | solution.py:587
  222.8 27.5 %collective-permute-start.39 = (bf16[4,64,1280]{2,1,0:T(8,128)(2,1)S(1)}, bf16[4,64,1280]{2,1,0:T(8,128)(2,1)S(1)}, u32[]{:S(2)}, u32[]{:S(2)}) collective-permute-start(bf16[4,64,1280]{2,1,0:T(8,128)(2,1)S(1)} %get-tuple-element.371), channel_id=1, source_target_pairs={{0,2},{2,0},{4,6},{6,4},{8,10},{10,8},{12,14},{14,12},{16,18},{18,... | collective-permute-start | bytes 1966088 | tf_op jit(solution)/shard_map/ppermute | solution.py:587
  224.1 29.6 %collective-permute-start.40 = (bf16[4,64,1280]{2,1,0:T(8,128)(2,1)S(1)}, bf16[4,64,1280]{2,1,0:T(8,128)(2,1)S(1)}, u32[]{:S(2)}, u32[]{:S(2)}) collective-permute-start(bf16[4,64,1280]{2,1,0:T(8,128)(2,1)S(1)} %get-tuple-element.372), channel_id=1, source_target_pairs={{0,4},{2,6},{4,0},{6,2},{8,12},{10,14},{12,8},{14,10},{16,20},{18,... | collective-permute-start | bytes 1966088 | tf_op jit(solution)/shard_map/ppermute | solution.py:587
  225.1 28.6 %collective-permute-start.41 = (bf16[4,64,1280]{2,1,0:T(8,128)(2,1)S(1)}, bf16[4,64,1280]{2,1,0:T(8,128)(2,1)S(1)}, u32[]{:S(2)}, u32[]{:S(2)}) collective-permute-start(bf16[4,64,1280]{2,1,0:T(8,128)(2,1)S(1)} %get-tuple-element.373), channel_id=1, source_target_pairs={{0,6},{2,4},{4,2},{6,0},{8,14},{10,12},{12,10},{14,8},{16,22},{18,... | collective-permute-start | bytes 1966088 | tf_op jit(solution)/shard_map/ppermute | solution.py:587
  226.2 24.0 %collective-permute-start.42 = (bf16[320,512]{1,0:T(8,128)(2,1)S(1)}, bf16[320,512]{1,0:T(8,128)(2,1)S(1)}, u32[]{:S(2)}, u32[]{:S(2)}) collective-permute-start(bf16[320,512]{1,0:T(8,128)(2,1)S(1)} %get-tuple-element.384), channel_id=1, source_target_pairs={{0,16},{2,18},{4,20},{6,22},{8,24},{10,26},{12,28},{14,30},{16,0},... | collective-permute-start | bytes 983048 | tf_op jit(solution)/shard_map/ppermute | solution.py:587
  228.6 21.7 %collective-permute-start.43 = (bf16[320,512]{1,0:T(8,128)(2,1)S(1)}, bf16[320,512]{1,0:T(8,128)(2,1)S(1)}, u32[]{:S(2)}, u32[]{:S(2)}) collective-permute-start(bf16[320,512]{1,0:T(8,128)(2,1)S(1)} %get-tuple-element.385), channel_id=1, source_target_pairs={{0,24},{2,26},{4,28},{6,30},{8,16},{10,18},{12,20},{14,22},{16,8},... | collective-permute-start | bytes 983048 | tf_op jit(solution)/shard_map/ppermute | solution.py:587
  257.6 55.7 %all-to-all-start.2 = ((bf16[4,80,1280]{2,1,0:T(8,128)(2,1)}), bf16[4,80,1280]{2,1,0:T(8,128)(2,1)S(1)}, u32[]{:S(2)}, u32[]{:S(2)}) async-start(bf16[4,80,1280]{2,1,0:T(8,128)(2,1)} %shard_map.218), calls=%async_computation.2 | async-start | bytes 1638400 | tf_op jit(solution)/shard_map/all_to_all | solution.py:603
  264.2 32.5 %collective-permute-start.47 = (bf16[4,80,640]{2,1,0:T(8,128)(2,1)}, bf16[4,80,640]{2,1,0:T(8,128)(2,1)S(1)}, u32[]{:S(2)}, u32[]{:S(2)}) collective-permute-start(bf16[4,80,640]{2,1,0:T(8,128)(2,1)} %get-tuple-element.420), channel_id=1, source_target_pairs={{0,2},{2,0},{4,6},{6,4},{8,10},{10,8},{12,14},{14,12},{16,18},{18,... | collective-permute-start | bytes 1228808 | tf_op jit(solution)/shard_map/ppermute | solution.py:587
  265.5 31.2 %collective-permute-start.48 = (bf16[4,80,640]{2,1,0:T(8,128)(2,1)}, bf16[4,80,640]{2,1,0:T(8,128)(2,1)S(1)}, u32[]{:S(2)}, u32[]{:S(2)}) collective-permute-start(bf16[4,80,640]{2,1,0:T(8,128)(2,1)} %get-tuple-element.421), channel_id=1, source_target_pairs={{0,4},{2,6},{4,0},{6,2},{8,12},{10,14},{12,8},{14,10},{16,20},{18,... | collective-permute-start | bytes 1228808 | tf_op jit(solution)/shard_map/ppermute | solution.py:587
  266.5 30.2 %collective-permute-start.49 = (bf16[4,80,640]{2,1,0:T(8,128)(2,1)}, bf16[4,80,640]{2,1,0:T(8,128)(2,1)S(1)}, u32[]{:S(2)}, u32[]{:S(2)}) collective-permute-start(bf16[4,80,640]{2,1,0:T(8,128)(2,1)} %get-tuple-element.422), channel_id=1, source_target_pairs={{0,6},{2,4},{4,2},{6,0},{8,14},{10,12},{12,10},{14,8},{16,22},{18,... | collective-permute-start | bytes 1228808 | tf_op jit(solution)/shard_map/ppermute | solution.py:587
  267.7 14.5 %collective-permute-start.44 = (bf16[64,1280]{1,0:T(8,128)(2,1)S(1)}, bf16[64,1280]{1,0:T(8,128)(2,1)S(1)}, u32[]{:S(2)}, u32[]{:S(2)}) collective-permute-start(bf16[64,1280]{1,0:T(8,128)(2,1)S(1)} %copy-done.27), channel_id=1, source_target_pairs={{0,8},{2,10},{4,12},{6,14},{8,0},{10,2},{12,4},{14,6},{16,24},{18,... | collective-permute-start | bytes 491528 | tf_op jit(solution)/shard_map/ppermute | solution.py:587
  269.7 27.0 %collective-permute-start.45 = (bf16[64,1280]{1,0:T(8,128)(2,1)}, bf16[64,1280]{1,0:T(8,128)(2,1)S(1)}, u32[]{:S(2)}, u32[]{:S(2)}) collective-permute-start(bf16[64,1280]{1,0:T(8,128)(2,1)} %get-tuple-element.409), channel_id=1, source_target_pairs={{0,16},{2,18},{4,20},{6,22},{8,24},{10,26},{12,28},{14,30},{16,0},... | collective-permute-start | bytes 491528 | tf_op jit(solution)/shard_map/ppermute | solution.py:587
  282.2 14.5 %collective-permute-start.46 = (bf16[64,1280]{1,0:T(8,128)(2,1)}, bf16[64,1280]{1,0:T(8,128)(2,1)S(1)}, u32[]{:S(2)}, u32[]{:S(2)}) collective-permute-start(bf16[64,1280]{1,0:T(8,128)(2,1)} %copy-done.25), channel_id=1, source_target_pairs={{0,24},{2,26},{4,28},{6,30},{8,16},{10,18},{12,20},{14,22},{16,8},... | collective-permute-start | bytes 491528 | tf_op jit(solution)/shard_map/ppermute | solution.py:587
  299.0 13.7 %collective-permute-start.54 = (bf16[80,640]{1,0:T(8,128)(2,1)S(1)}, bf16[80,640]{1,0:T(8,128)(2,1)S(1)}, u32[]{:S(2)}, u32[]{:S(2)}) collective-permute-start(bf16[80,640]{1,0:T(8,128)(2,1)S(1)} %get-tuple-element.433), channel_id=1, source_target_pairs={{0,8},{2,10},{4,12},{6,14},{8,0},{10,2},{12,4},{14,6},{16,24},{18,... | collective-permute-start | bytes 307208 | tf_op jit(solution)/shard_map/ppermute | solution.py:587
  (64 other events, 414.3 us)

commit v3 on v2

--- a/solution.py
+++ b/solution.py
@@ -849,7 +849,11 @@
         moved=shard * local * 24,
     )(ids, *qkv_parts, w_query, w_key, w_value)
     lane = lax.broadcasted_iota(jnp.int32, small.shape, 1)
-    small = jnp.where(lane == 2, gain_two, small)
+    small = jnp.where(
+        lane == 0,
+        small / gain_attn.astype(F32)[:, None],
+        jnp.where(lane == 2, gain_two / gain_mlp.astype(F32)[:, None], small),
+    )
     small = small + swap(small)
     gx_other, small = tie(gx_other, small)
     grad_tokens = call(
@@ -867,8 +871,8 @@
         grad_out.T,
         grad_up,
         grad_down.T,
-        small[:, 0] / gain_attn.astype(F32),
-        small[:, 2] / gain_mlp.astype(F32),
+        small[:, 0],
+        small[:, 2],
         small[:size, 1],
     )
 

time: 319 us -> 319 us (level)
  no operation moved by 1% of the time
where the time goes in v3:
time: 319 us
  waiting for transfers between devices  129 us (40%)
  Pallas kernels  90.9 us (28%)
  starting transfers between devices  83.1 us (26%)
  local copies, waits for them, and re-layouts  13 us (4%)
    ppermute x46, waiting for transfers between devices, across(): return lax.ppermute(a, 'ctx', [(i, i ^ mask) for i in range(count)])  119 us
    ppermute x46, starting transfers between devices, across(): return lax.ppermute(a, 'ctx', [(i, i ^ mask) for i in range(count)])  64.2 us
    pallas_call x1, Pallas kernels, stream_per_group(): call(functools.partial(attend_back_kernel, heads, size, members, bq, bk),...  29.7 us
    pallas_call x1, Pallas kernels, stream_per_group(): call(functools.partial(attend_kernel, heads, size, members, bq, bk), (str...  15.5 us
    all_to_all x3, starting transfers between devices, exchange(): return lax.all_to_all(a, 'ctx', 0, 0, axis_index_groups=teams, tiled=True)  15.4 us
    ppermute x15, waiting for transfers between devices, swap(): return lax.ppermute(a, 'tp', [(0, 1), (1, 0)])  9.94 us
    unnamed x64, local copies, waits for them, and re-layouts  9.73 us
    pallas_call x1, Pallas kernels, stream_per_group(): call(functools.partial(project_kernel, members, 512), (struct((stream, pa...  7.25 us
  transfers between devices with their start and end apart: 64, of which 27 were waited for; matrix products, arithmetic and copies ran while one was open for 1% of the time, Pallas kernels for 23%

profile of v3, /device:TPU:0, one launch (start us, length us, event | category | flops | bytes accessed | tf_op | source)
XLA Modules:
  0.0 318.7 jit_solution(11382701343419415653)
XLA Ops:
  2.7 5.1 %collective-permute-start.2 = (bf16[64,1280]{1,0:T(8,128)(2,1)S(1)}, bf16[64,1280]{1,0:T(8,128)(2,1)S(1)}, u32[]{:S(2)}, u32[]{:S(2)}) collective-permute-start(bf16[64,1280]{1,0:T(8,128)(2,1)S(1)} %get-tuple-element.235), channel_id=1, source_target_pairs={{0,24},{2,26},{4,28},{6,30},{8,16},{10,18},{12,20},{14,22},{16,8},... | collective-permute-start | bytes 491528 | tf_op jit(solution)/shard_map/ppermute | solution.py:587
  10.5 2.5 collective-permute-done.2
  13.0 8.8 %collective-permute-done.1 = bf16[64,1280]{1,0:T(8,128)(2,1)S(1)} collective-permute-done((bf16[64,1280]{1,0:T(8,128)(2,1)S(1)}, bf16[64,1280]{1,0:T(8,128)(2,1)S(1)}, u32[]{:S(2)}, u32[]{:S(2)}) %collective-permute-start.1) | collective-permute-done | bytes 163872 | tf_op jit(solution)/shard_map/ppermute | solution.py:587
  21.8 3.8 %all-to-all-start = ((bf16[4,80,1920]{2,1,0:T(8,128)(2,1)}), bf16[4,80,1920]{2,1,0:T(8,128)(2,1)S(1)}, u32[]{:S(2)}, u32[]{:S(2)}) async-start(bf16[4,80,1920]{2,1,0:T(8,128)(2,1)} %shard_map.205), calls=%async_computation | async-start | bytes 2457600 | tf_op jit(solution)/shard_map/all_to_all | solution.py:603
  35.4 12.6 %collective-permute-done.3.refs_1_ = bf16[4,64,1280]{2,1,0:T(8,128)(2,1)S(1)} collective-permute-done((bf16[4,64,1280]{2,1,0:T(8,128)(2,1)S(1)}, bf16[4,64,1280]{2,1,0:T(8,128)(2,1)S(1)}, u32[]{:S(2)}, u32[]{:S(2)}) %collective-permute-start.3) | collective-permute-done | bytes 655392 | tf_op jit(solution)/shard_map/ppermute | solution.py:587
  47.9 13.3 %collective-permute-done.4.refs_2_ = bf16[4,64,1280]{2,1,0:T(8,128)(2,1)S(1)} collective-permute-done((bf16[4,64,1280]{2,1,0:T(8,128)(2,1)S(1)}, bf16[4,64,1280]{2,1,0:T(8,128)(2,1)S(1)}, u32[]{:S(2)}, u32[]{:S(2)}) %collective-permute-start.4) | collective-permute-done | bytes 655392 | tf_op jit(solution)/shard_map/ppermute | solution.py:587
  63.3 5.1 %all-to-all-start.1 = ((bf16[16,80,512]{2,1,0:T(8,128)(2,1)}), bf16[16,80,512]{2,1,0:T(8,128)(2,1)S(1)}, u32[]{:S(2)}, u32[]{:S(2)}) async-start(bf16[16,80,512]{2,1,0:T(8,128)(2,1)} %pad_maximum_fusion), calls=%async_computation.1 | async-start | bytes 2621440 | tf_op jit(solution)/shard_map/all_to_all | solution.py:603
  74.8 23.0 %collective-permute-done.13.refs_1_ = bf16[4,80,1920]{2,1,0:T(8,128)(2,1)S(1)} collective-permute-done((bf16[4,80,1920]{2,1,0:T(8,128)(2,1)S(1)}, bf16[4,80,1920]{2,1,0:T(8,128)(2,1)S(1)}, u32[]{:S(2)}, u32[]{:S(2)}) %collective-permute-start.13) | collective-permute-done | bytes 1228832 | tf_op jit(solution)/shard_map/ppermute | solution.py:587
  108.0 2.4 collective-permute-start.18
  111.5 7.2 %shard_map.208 = (bf16[2048,768]{1,0:T(8,128)(2,1)S(1)}, bf16[2048,1280]{1,0:T(8,128)(2,1)S(1)}) custom-call(s32[3]{0:T(128)S(1)} %pad_add_fusion.ids, bf16[4,64,1280]{2,1,0:T(8,128)(2,1)S(1)} %pad_maximum_fusion.2.refs_0_, bf16[4,64,1280]{2,1,0:T(8,128)(2,1)S(1)} %copy-done.16, bf16[4,64,1280]{2,1,0:T(8,128)(2,1)S(1)} %copy-done.18, ...), custom_call_target="tpu_custom_call" | custom-call | flops 4026531840 | bytes 10485760 | tf_op jit(solution)/shard_map/pallas_call | solution.py:658
  118.8 15.5 %shard_map.209 = (bf16[160,512]{1,0:T(8,128)(2,1)S(1)}, bf16[160,512]{1,0:T(8,128)(2,1)S(1)}, bf16[160,512]{1,0:T(8,128)(2,1)S(1)}, bf16[160,512]{1,0:T(8,128)(2,1)S(1)}, f32[2,136,2048]{2,1,0:T(8,128)S(1)}) custom-call(s32[3]{0:T(128)S(1)} %pad_add_fusion.ids, s32[4,8]{1,0:T(4,128)S(1)} %copy-done.28, bf16[2048,768]{1,0:T(8,128)(2,1)S(1)} %get-tuple-element.269.proj), custom_call_target="tpu_custom_call" | custom-call | flops 2147483648 | bytes 5242880 | tf_op jit(solution)/shard_map/pallas_call | solution.py:667
  141.5 2.6 collective-permute-done.22.refs_2_
  146.6 3.3 %collective-permute-done.20.refs_3_ = bf16[4,64,1280]{2,1,0:T(8,128)(2,1)S(1)} collective-permute-done((bf16[4,64,1280]{2,1,0:T(8,128)(2,1)S(1)}, bf16[4,64,1280]{2,1,0:T(8,128)(2,1)S(1)}, u32[]{:S(2)}, u32[]{:S(2)}) %collective-permute-start.20) | collective-permute-done | bytes 655392 | tf_op jit(solution)/shard_map/ppermute | solution.py:594
  150.0 6.0 %shard_map.212 = (f32[512,1280]{1,0:T(8,128)S(1)}, bf16[512,1280]{1,0:T(8,128)(2,1)S(1)}, bf16[512,640]{1,0:T(8,128)(2,1)S(1)}, bf16[512,640]{1,0:T(8,128)(2,1)S...) custom-call(s32[3]{0:T(128)S(1)} %pad_add_fusion.ids, ...), custom_call_target="tpu_custom_call" | custom-call | flops 3355443200 | bytes 9830400 | tf_op jit(solution)/shard_map/pallas_call | solution.py:697
  156.5 3.0 shard_map.213
  160.9 3.8 %shard_map.214 = (bf16[512,1280]{1,0:T(8,128)(2,1)S(1)}, f32[4,64,1280]{2,1,0:T(8,128)S(1)}, bf16[160,512]{1,0:T(8,128)(2,1)S(1)}, bf16[160,512]{1,0:T(8,128)(2,...) custom-call(s32[3]{0:T(128)S(1)} %pad_add_fusion.ids, ...), custom_call_target="tpu_custom_call" | custom-call | flops 838860800 | bytes 9830400 | tf_op jit(solution)/shard_map/pallas_call | solution.py:722
  169.0 2.9 shard_map.215
  172.0 2.9 collective-permute-done.29.refs_3_
  181.9 29.7 %shard_map.216 = (bf16[2048,768]{1,0:T(8,128)(2,1)S(1)}, bf16[4,4,64,1280]{3,2,1,0:T(8,128)(2,1)S(1)}, bf16[320,512]{1,0:T(8,128)(2,1)S(1)}, bf16[320,512]{1,0:T...) custom-call(s32[3]{0:T(128)S(1)} %pad_add_fusion.ids, s32[4,8]{1,0:T(4,128)S(1)} %copy-done.28, ...), custom_call_target="tpu_custom_call" | custom-call | flops 5368709120 | bytes 10485760 | tf_op jit(solution)/shard_map/pallas_call | solution.py:753
  213.9 3.4 %collective-permute-done.36.other = bf16[4,4,64,1280]{3,2,1,0:T(8,128)(2,1)S(1)} collective-permute-done((bf16[4,4,64,1280]{3,2,1,0:T(8,128)(2,1)S(1)}, bf16[4,4,64,1280]{3,2,1,0:T(8,128)(2,1)S(1)}, u32[]{:S(2)}, u32[]{:S(2)}) %collective-permute-start.36) | collective-permute-done | bytes 2621472 | tf_op jit(solution)/shard_map/ppermute | solution.py:594
  217.3 2.8 shard_map.217
  220.1 2.6 collective-permute-done.37.refs_1_
  232.7 17.5 %collective-permute-done.42.refs_2_ = bf16[320,512]{1,0:T(8,128)(2,1)S(1)} collective-permute-done((bf16[320,512]{1,0:T(8,128)(2,1)S(1)}, bf16[320,512]{1,0:T(8,128)(2,1)S(1)}, u32[]{:S(2)}, u32[]{:S(2)}) %collective-permute-start.42) | collective-permute-done | bytes 327712 | tf_op jit(solution)/shard_map/ppermute | solution.py:587
  250.2 3.5 %collective-permute-done.40.refs_5_ = bf16[4,64,1280]{2,1,0:T(8,128)(2,1)S(1)} collective-permute-done((bf16[4,64,1280]{2,1,0:T(8,128)(2,1)S(1)}, bf16[4,64,1280]{2,1,0:T(8,128)(2,1)S(1)}, u32[]{:S(2)}, u32[]{:S(2)}) %collective-permute-start.40) | collective-permute-done | bytes 655392 | tf_op jit(solution)/shard_map/ppermute | solution.py:587
  257.6 6.5 %all-to-all-start.2 = ((bf16[4,80,1280]{2,1,0:T(8,128)(2,1)}), bf16[4,80,1280]{2,1,0:T(8,128)(2,1)S(1)}, u32[]{:S(2)}, u32[]{:S(2)}) async-start(bf16[4,80,1280]{2,1,0:T(8,128)(2,1)} %shard_map.218), calls=%async_computation.2 | async-start | bytes 1638400 | tf_op jit(solution)/shard_map/all_to_all | solution.py:603
  269.7 2.4 collective-permute-start.45
  272.1 10.1 %collective-permute-done.44.refs_1_ = bf16[64,1280]{1,0:T(8,128)(2,1)S(1)} collective-permute-done((bf16[64,1280]{1,0:T(8,128)(2,1)S(1)}, bf16[64,1280]{1,0:T(8,128)(2,1)S(1)}, u32[]{:S(2)}, u32[]{:S(2)}) %collective-permute-start.44) | collective-permute-done | bytes 163872 | tf_op jit(solution)/shard_map/ppermute | solution.py:587
  282.2 3.9 %collective-permute-start.46 = (bf16[64,1280]{1,0:T(8,128)(2,1)}, bf16[64,1280]{1,0:T(8,128)(2,1)S(1)}, u32[]{:S(2)}, u32[]{:S(2)}) collective-permute-start(bf16[64,1280]{1,0:T(8,128)(2,1)} %copy-done.25), channel_id=1, source_target_pairs={{0,24},{2,26},{4,28},{6,30},{8,16},{10,18},{12,20},{14,22},{16,8},... | collective-permute-start | bytes 491528 | tf_op jit(solution)/shard_map/ppermute | solution.py:587
  286.9 9.8 %collective-permute-done.45.refs_2_ = bf16[64,1280]{1,0:T(8,128)(2,1)S(1)} collective-permute-done((bf16[64,1280]{1,0:T(8,128)(2,1)}, bf16[64,1280]{1,0:T(8,128)(2,1)S(1)}, u32[]{:S(2)}, u32[]{:S(2)}) %collective-permute-start.45) | collective-permute-done | bytes 163872 | tf_op jit(solution)/shard_map/ppermute | solution.py:587
  301.2 3.1 collective-permute-start.57
  304.4 2.4 collective-permute-start.59
  309.2 4.0 %collective-permute-done.58.refs_2_ = bf16[80,640]{1,0:T(8,128)(2,1)S(1)} collective-permute-done((bf16[80,640]{1,0:T(8,128)(2,1)S(1)}, bf16[80,640]{1,0:T(8,128)(2,1)S(1)}, u32[]{:S(2)}, u32[]{:S(2)}) %collective-permute-start.58) | collective-permute-done | bytes 102432 | tf_op jit(solution)/shard_map/ppermute | solution.py:587
  (204 shorter events, 92.3 us)
Async XLA Ops:
  7.8 13.9 %collective-permute-start.1 = (bf16[64,1280]{1,0:T(8,128)(2,1)S(1)}, bf16[64,1280]{1,0:T(8,128)(2,1)S(1)}, u32[]{:S(2)}, u32[]{:S(2)}) collective-permute-start(bf16[64,1280]{1,0:T(8,128)(2,1)S(1)} %get-tuple-element.234), channel_id=1, source_target_pairs={{0,16},{2,18},{4,20},{6,22},{8,24},{10,26},{12,28},{14,30},{16,0},... | collective-permute-start | bytes 491528 | tf_op jit(solution)/shard_map/ppermute | solution.py:587
  7.8 13.9 %collective-permute-start = (bf16[64,1280]{1,0:T(8,128)(2,1)S(1)}, bf16[64,1280]{1,0:T(8,128)(2,1)S(1)}, u32[]{:S(2)}, u32[]{:S(2)}) collective-permute-start(bf16[64,1280]{1,0:T(8,128)(2,1)S(1)} %get-tuple-element.233), channel_id=1, source_target_pairs={{0,8},{2,10},{4,12},{6,14},{8,0},{10,2},{12,4},{14,6},{16,24},{18,... | collective-permute-start | bytes 491528 | tf_op jit(solution)/shard_map/ppermute | solution.py:587
  21.8 40.3 %all-to-all-start = ((bf16[4,80,1920]{2,1,0:T(8,128)(2,1)}), bf16[4,80,1920]{2,1,0:T(8,128)(2,1)S(1)}, u32[]{:S(2)}, u32[]{:S(2)}) async-start(bf16[4,80,1920]{2,1,0:T(8,128)(2,1)} %shard_map.205), calls=%async_computation | async-start | bytes 2457600 | tf_op jit(solution)/shard_map/all_to_all | solution.py:603
  29.1 18.9 %collective-permute-start.3 = (bf16[4,64,1280]{2,1,0:T(8,128)(2,1)S(1)}, bf16[4,64,1280]{2,1,0:T(8,128)(2,1)S(1)}, u32[]{:S(2)}, u32[]{:S(2)}) collective-permute-start(bf16[4,64,1280]{2,1,0:T(8,128)(2,1)S(1)} %pad_maximum_fusion.2.refs_0_), channel_id=1, source_target_pairs={{0,2},{2,0},{4,6},{6,4},{8,10},{10,8},{12,14},{14,12},{16,18},{18,... | collective-permute-start | bytes 1966088 | tf_op jit(solution)/shard_map/ppermute | solution.py:587
  30.5 30.7 %collective-permute-start.4 = (bf16[4,64,1280]{2,1,0:T(8,128)(2,1)S(1)}, bf16[4,64,1280]{2,1,0:T(8,128)(2,1)S(1)}, u32[]{:S(2)}, u32[]{:S(2)}) collective-permute-start(bf16[4,64,1280]{2,1,0:T(8,128)(2,1)S(1)} %pad_maximum_fusion.2.refs_0_), channel_id=1, source_target_pairs={{0,4},{2,6},{4,0},{6,2},{8,12},{10,14},{12,8},{14,10},{16,20},{18,... | collective-permute-start | bytes 1966088 | tf_op jit(solution)/shard_map/ppermute | solution.py:587
  34.9 27.2 %collective-permute-start.8 = (bf16[4,64,1280]{2,1,0:T(8,128)(2,1)S(1)}, bf16[4,64,1280]{2,1,0:T(8,128)(2,1)}, u32[]{:S(2)}, u32[]{:S(2)}) collective-permute-start(bf16[4,64,1280]{2,1,0:T(8,128)(2,1)S(1)} %pad_maximum_fusion.2.refs_0_), channel_id=1, source_target_pairs={{0,6},{2,4},{4,2},{6,0},{8,14},{10,12},{12,10},{14,8},{16,22},{18,... | collective-permute-start | bytes 1966088 | tf_op jit(solution)/shard_map/ppermute | solution.py:587
  63.3 35.5 %all-to-all-start.1 = ((bf16[16,80,512]{2,1,0:T(8,128)(2,1)}), bf16[16,80,512]{2,1,0:T(8,128)(2,1)S(1)}, u32[]{:S(2)}, u32[]{:S(2)}) async-start(bf16[16,80,512]{2,1,0:T(8,128)(2,1)} %pad_maximum_fusion), calls=%async_computation.1 | async-start | bytes 2621440 | tf_op jit(solution)/shard_map/all_to_all | solution.py:603
  68.4 29.4 %collective-permute-start.13 = (bf16[4,80,1920]{2,1,0:T(8,128)(2,1)S(1)}, bf16[4,80,1920]{2,1,0:T(8,128)(2,1)S(1)}, u32[]{:S(2)}, u32[]{:S(2)}) collective-permute-start(bf16[4,80,1920]{2,1,0:T(8,128)(2,1)S(1)} %all-to-all-done.refs_0_), channel_id=1, source_target_pairs={{0,2},{2,0},{4,6},{6,4},{8,10},{10,8},{12,14},{14,12},{16,18},{18,... | collective-permute-start | bytes 3686408 | tf_op jit(solution)/shard_map/ppermute | solution.py:587
  68.4 30.5 %collective-permute-start.14 = (bf16[4,80,1920]{2,1,0:T(8,128)(2,1)S(1)}, bf16[4,80,1920]{2,1,0:T(8,128)(2,1)}, u32[]{:S(2)}, u32[]{:S(2)}) collective-permute-start(bf16[4,80,1920]{2,1,0:T(8,128)(2,1)S(1)} %all-to-all-done.refs_0_), channel_id=1, source_target_pairs={{0,4},{2,6},{4,0},{6,2},{8,12},{10,14},{12,8},{14,10},{16,20},{18,... | collective-permute-start | bytes 3686408 | tf_op jit(solution)/shard_map/ppermute | solution.py:587
  100.1 34.2 %collective-permute-start.16 = (bf16[2,80,1920]{2,1,0:T(8,128)(2,1)S(1)}, bf16[2,80,1920]{2,1,0:T(8,128)(2,1)S(1)}, u32[]{:S(2)}, u32[]{:S(2)}) collective-permute-start(bf16[2,80,1920]{2,1,0:T(8,128)(2,1)S(1)} %slice.16), channel_id=1, source_target_pairs={{0,4},{2,6},{4,0},{6,2},{8,12},{10,14},{12,8},{14,10},{16,20},{18,... | collective-permute-start | bytes 1843208 | tf_op jit(solution)/shard_map/ppermute | solution.py:587
  102.4 31.9 %collective-permute-start.15 = (bf16[2,80,1920]{2,1,0:T(8,128)(2,1)S(1)}, bf16[2,80,1920]{2,1,0:T(8,128)(2,1)S(1)}, u32[]{:S(2)}, u32[]{:S(2)}) collective-permute-start(bf16[2,80,1920]{2,1,0:T(8,128)(2,1)S(1)} %slice.15), channel_id=1, source_target_pairs={{0,2},{2,0},{4,6},{6,4},{8,10},{10,8},{12,14},{14,12},{16,18},{18,... | collective-permute-start | bytes 1843208 | tf_op jit(solution)/shard_map/ppermute | solution.py:587
  105.9 28.6 %collective-permute-start.17 = (bf16[64,1280]{1,0:T(8,128)(2,1)S(1)}, bf16[64,1280]{1,0:T(8,128)(2,1)S(1)}, u32[]{:S(2)}, u32[]{:S(2)}) collective-permute-start(bf16[64,1280]{1,0:T(8,128)(2,1)S(1)} %get-tuple-element.280), channel_id=1, source_target_pairs={{0,8},{2,10},{4,12},{6,14},{8,0},{10,2},{12,4},{14,6},{16,24},{18,... | collective-permute-start | bytes 491528 | tf_op jit(solution)/shard_map/ppermute | solution.py:587
  108.0 26.5 %collective-permute-start.18 = (bf16[64,1280]{1,0:T(8,128)(2,1)S(1)}, bf16[64,1280]{1,0:T(8,128)(2,1)S(1)}, u32[]{:S(2)}, u32[]{:S(2)}) collective-permute-start(bf16[64,1280]{1,0:T(8,128)(2,1)S(1)} %get-tuple-element.281), channel_id=1, source_target_pairs={{0,16},{2,18},{4,20},{6,22},{8,24},{10,26},{12,28},{14,30},{16,0},... | collective-permute-start | bytes 491528 | tf_op jit(solution)/shard_map/ppermute | solution.py:587
  110.3 24.2 %collective-permute-start.19 = (bf16[64,1280]{1,0:T(8,128)(2,1)S(1)}, bf16[64,1280]{1,0:T(8,128)(2,1)S(1)}, u32[]{:S(2)}, u32[]{:S(2)}) collective-permute-start(bf16[64,1280]{1,0:T(8,128)(2,1)S(1)} %get-tuple-element.282), channel_id=1, source_target_pairs={{0,24},{2,26},{4,28},{6,30},{8,16},{10,18},{12,20},{14,22},{16,8},... | collective-permute-start | bytes 491528 | tf_op jit(solution)/shard_map/ppermute | solution.py:587
  174.9 36.7 %collective-permute-start.31 = (bf16[4,80,1280]{2,1,0:T(8,128)(2,1)S(1)}, bf16[4,80,1280]{2,1,0:T(8,128)(2,1)S(1)}, u32[]{:S(2)}, u32[]{:S(2)}) collective-permute-start(bf16[4,80,1280]{2,1,0:T(8,128)(2,1)S(1)} %get-tuple-element.341), channel_id=1, source_target_pairs={{0,2},{2,0},{4,6},{6,4},{8,10},{10,8},{12,14},{14,12},{16,18},{18,... | collective-permute-start | bytes 2457608 | tf_op jit(solution)/shard_map/ppermute | solution.py:587
  176.2 35.4 %collective-permute-start.32 = (bf16[4,80,1280]{2,1,0:T(8,128)(2,1)S(1)}, bf16[4,80,1280]{2,1,0:T(8,128)(2,1)S(1)}, u32[]{:S(2)}, u32[]{:S(2)}) collective-permute-start(bf16[4,80,1280]{2,1,0:T(8,128)(2,1)S(1)} %get-tuple-element.342), channel_id=1, source_target_pairs={{0,4},{2,6},{4,0},{6,2},{8,12},{10,14},{12,8},{14,10},{16,20},{18,... | collective-permute-start | bytes 2457608 | tf_op jit(solution)/shard_map/ppermute | solution.py:587
  177.3 35.1 %collective-permute-start.33 = (bf16[4,80,1280]{2,1,0:T(8,128)(2,1)S(1)}, bf16[4,80,1280]{2,1,0:T(8,128)(2,1)S(1)}, u32[]{:S(2)}, u32[]{:S(2)}) collective-permute-start(bf16[4,80,1280]{2,1,0:T(8,128)(2,1)S(1)} %get-tuple-element.343), channel_id=1, source_target_pairs={{0,6},{2,4},{4,2},{6,0},{8,14},{10,12},{12,10},{14,8},{16,22},{18,... | collective-permute-start | bytes 2457608 | tf_op jit(solution)/shard_map/ppermute | solution.py:587
  178.4 33.2 %collective-permute-start.34 = (bf16[64,1280]{1,0:T(8,128)(2,1)S(1)}, bf16[64,1280]{1,0:T(8,128)(2,1)S(1)}, u32[]{:S(2)}, u32[]{:S(2)}) collective-permute-start(bf16[64,1280]{1,0:T(8,128)(2,1)S(1)} %get-tuple-element.346), channel_id=1, source_target_pairs={{0,16},{2,18},{4,20},{6,22},{8,24},{10,26},{12,28},{14,30},{16,0},... | collective-permute-start | bytes 491528 | tf_op jit(solution)/shard_map/ppermute | solution.py:587
  180.1 31.5 %collective-permute-start.35 = (bf16[64,1280]{1,0:T(8,128)(2,1)S(1)}, bf16[64,1280]{1,0:T(8,128)(2,1)S(1)}, u32[]{:S(2)}, u32[]{:S(2)}) collective-permute-start(bf16[64,1280]{1,0:T(8,128)(2,1)S(1)} %get-tuple-element.347), channel_id=1, source_target_pairs={{0,24},{2,26},{4,28},{6,30},{8,16},{10,18},{12,20},{14,22},{16,8},... | collective-permute-start | bytes 491528 | tf_op jit(solution)/shard_map/ppermute | solution.py:587
  212.5 10.3 %collective-permute-start.38 = (bf16[4,64,1280]{2,1,0:T(8,128)(2,1)S(1)}, bf16[4,64,1280]{2,1,0:T(8,128)(2,1)S(1)}, u32[]{:S(2)}, u32[]{:S(2)}) collective-permute-start(bf16[4,64,1280]{2,1,0:T(8,128)(2,1)S(1)} %pad_maximum_fusion.4.own), channel_id=1, source_target_pairs={{0,1},{1,0},{2,3},{3,2},{4,5},{5,4},{6,7},{7,6},{8,9},{9,8},{10,11... | collective-permute-start | bytes 1966088 | tf_op jit(solution)/shard_map/ppermute | solution.py:594
  222.8 27.5 %collective-permute-start.39 = (bf16[4,64,1280]{2,1,0:T(8,128)(2,1)S(1)}, bf16[4,64,1280]{2,1,0:T(8,128)(2,1)S(1)}, u32[]{:S(2)}, u32[]{:S(2)}) collective-permute-start(bf16[4,64,1280]{2,1,0:T(8,128)(2,1)S(1)} %get-tuple-element.371), channel_id=1, source_target_pairs={{0,2},{2,0},{4,6},{6,4},{8,10},{10,8},{12,14},{14,12},{16,18},{18,... | collective-permute-start | bytes 1966088 | tf_op jit(solution)/shard_map/ppermute | solution.py:587
  224.1 29.6 %collective-permute-start.40 = (bf16[4,64,1280]{2,1,0:T(8,128)(2,1)S(1)}, bf16[4,64,1280]{2,1,0:T(8,128)(2,1)S(1)}, u32[]{:S(2)}, u32[]{:S(2)}) collective-permute-start(bf16[4,64,1280]{2,1,0:T(8,128)(2,1)S(1)} %get-tuple-element.372), channel_id=1, source_target_pairs={{0,4},{2,6},{4,0},{6,2},{8,12},{10,14},{12,8},{14,10},{16,20},{18,... | collective-permute-start | bytes 1966088 | tf_op jit(solution)/shard_map/ppermute | solution.py:587
  225.1 28.6 %collective-permute-start.41 = (bf16[4,64,1280]{2,1,0:T(8,128)(2,1)S(1)}, bf16[4,64,1280]{2,1,0:T(8,128)(2,1)S(1)}, u32[]{:S(2)}, u32[]{:S(2)}) collective-permute-start(bf16[4,64,1280]{2,1,0:T(8,128)(2,1)S(1)} %get-tuple-element.373), channel_id=1, source_target_pairs={{0,6},{2,4},{4,2},{6,0},{8,14},{10,12},{12,10},{14,8},{16,22},{18,... | collective-permute-start | bytes 1966088 | tf_op jit(solution)/shard_map/ppermute | solution.py:587
  226.2 24.0 %collective-permute-start.42 = (bf16[320,512]{1,0:T(8,128)(2,1)S(1)}, bf16[320,512]{1,0:T(8,128)(2,1)S(1)}, u32[]{:S(2)}, u32[]{:S(2)}) collective-permute-start(bf16[320,512]{1,0:T(8,128)(2,1)S(1)} %get-tuple-element.384), channel_id=1, source_target_pairs={{0,16},{2,18},{4,20},{6,22},{8,24},{10,26},{12,28},{14,30},{16,0},... | collective-permute-start | bytes 983048 | tf_op jit(solution)/shard_map/ppermute | solution.py:587
  228.6 21.7 %collective-permute-start.43 = (bf16[320,512]{1,0:T(8,128)(2,1)S(1)}, bf16[320,512]{1,0:T(8,128)(2,1)S(1)}, u32[]{:S(2)}, u32[]{:S(2)}) collective-permute-start(bf16[320,512]{1,0:T(8,128)(2,1)S(1)} %get-tuple-element.385), channel_id=1, source_target_pairs={{0,24},{2,26},{4,28},{6,30},{8,16},{10,18},{12,20},{14,22},{16,8},... | collective-permute-start | bytes 983048 | tf_op jit(solution)/shard_map/ppermute | solution.py:587
  257.6 55.6 %all-to-all-start.2 = ((bf16[4,80,1280]{2,1,0:T(8,128)(2,1)}), bf16[4,80,1280]{2,1,0:T(8,128)(2,1)S(1)}, u32[]{:S(2)}, u32[]{:S(2)}) async-start(bf16[4,80,1280]{2,1,0:T(8,128)(2,1)} %shard_map.218), calls=%async_computation.2 | async-start | bytes 1638400 | tf_op jit(solution)/shard_map/all_to_all | solution.py:603
  264.2 32.5 %collective-permute-start.47 = (bf16[4,80,640]{2,1,0:T(8,128)(2,1)}, bf16[4,80,640]{2,1,0:T(8,128)(2,1)S(1)}, u32[]{:S(2)}, u32[]{:S(2)}) collective-permute-start(bf16[4,80,640]{2,1,0:T(8,128)(2,1)} %get-tuple-element.420), channel_id=1, source_target_pairs={{0,2},{2,0},{4,6},{6,4},{8,10},{10,8},{12,14},{14,12},{16,18},{18,... | collective-permute-start | bytes 1228808 | tf_op jit(solution)/shard_map/ppermute | solution.py:587
  265.5 31.2 %collective-permute-start.48 = (bf16[4,80,640]{2,1,0:T(8,128)(2,1)}, bf16[4,80,640]{2,1,0:T(8,128)(2,1)S(1)}, u32[]{:S(2)}, u32[]{:S(2)}) collective-permute-start(bf16[4,80,640]{2,1,0:T(8,128)(2,1)} %get-tuple-element.421), channel_id=1, source_target_pairs={{0,4},{2,6},{4,0},{6,2},{8,12},{10,14},{12,8},{14,10},{16,20},{18,... | collective-permute-start | bytes 1228808 | tf_op jit(solution)/shard_map/ppermute | solution.py:587
  266.5 30.2 %collective-permute-start.49 = (bf16[4,80,640]{2,1,0:T(8,128)(2,1)}, bf16[4,80,640]{2,1,0:T(8,128)(2,1)S(1)}, u32[]{:S(2)}, u32[]{:S(2)}) collective-permute-start(bf16[4,80,640]{2,1,0:T(8,128)(2,1)} %get-tuple-element.422), channel_id=1, source_target_pairs={{0,6},{2,4},{4,2},{6,0},{8,14},{10,12},{12,10},{14,8},{16,22},{18,... | collective-permute-start | bytes 1228808 | tf_op jit(solution)/shard_map/ppermute | solution.py:587
  267.7 14.5 %collective-permute-start.44 = (bf16[64,1280]{1,0:T(8,128)(2,1)S(1)}, bf16[64,1280]{1,0:T(8,128)(2,1)S(1)}, u32[]{:S(2)}, u32[]{:S(2)}) collective-permute-start(bf16[64,1280]{1,0:T(8,128)(2,1)S(1)} %copy-done.27), channel_id=1, source_target_pairs={{0,8},{2,10},{4,12},{6,14},{8,0},{10,2},{12,4},{14,6},{16,24},{18,... | collective-permute-start | bytes 491528 | tf_op jit(solution)/shard_map/ppermute | solution.py:587
  269.7 27.0 %collective-permute-start.45 = (bf16[64,1280]{1,0:T(8,128)(2,1)}, bf16[64,1280]{1,0:T(8,128)(2,1)S(1)}, u32[]{:S(2)}, u32[]{:S(2)}) collective-permute-start(bf16[64,1280]{1,0:T(8,128)(2,1)} %get-tuple-element.409), channel_id=1, source_target_pairs={{0,16},{2,18},{4,20},{6,22},{8,24},{10,26},{12,28},{14,30},{16,0},... | collective-permute-start | bytes 491528 | tf_op jit(solution)/shard_map/ppermute | solution.py:587
  282.2 14.5 %collective-permute-start.46 = (bf16[64,1280]{1,0:T(8,128)(2,1)}, bf16[64,1280]{1,0:T(8,128)(2,1)S(1)}, u32[]{:S(2)}, u32[]{:S(2)}) collective-permute-start(bf16[64,1280]{1,0:T(8,128)(2,1)} %copy-done.25), channel_id=1, source_target_pairs={{0,24},{2,26},{4,28},{6,30},{8,16},{10,18},{12,20},{14,22},{16,8},... | collective-permute-start | bytes 491528 | tf_op jit(solution)/shard_map/ppermute | solution.py:587
  (64 other events, 421.5 us)
